TPU v7x, 32 devices: a whole 2x2x4 slice. The times are simulated.
32 devices in a mesh: section: 2 (over y), hid: 4 (over x, core), wid: 4 (over z).
Axes of the slice: x: 2, y: 2, z: 4, core: 2. Of those that a mesh axis runs over, the one named last changes fastest.
Arguments:
- w_first: bfloat16 [2, 5120, 20480], P('section', 'wid', 'hid'), may hold values from -0.078125 to 0.078125
- w_second: bfloat16 [2, 20480, 5120], P('section', 'hid', 'wid'), may hold values from -0.0390625 to 0.0390625
- saved_inputs: bfloat16 [2, 2, 256, 5120], P('section', None, None, 'wid'), may hold values from -0.75 to 0.75
- saved_hidden: bfloat16 [2, 2, 256, 20480], P('section', None, None, 'hid'), may hold values from -0.375 to 0.375
- cotangent: bfloat16 [2, 256, 5120], P(None, None, 'wid'), may hold values from -6 to 6
Outputs:
- grad_first: float32 [2, 5120, 20480], P('section', 'wid', 'hid')
- grad_second: float32 [2, 20480, 5120], P('section', 'hid', 'wid')
- input_grads: bfloat16 [2, 2, 256, 5120], P('section', None, 'hid', 'wid')
All inputs are finite; a program needn't handle non-finite values.
Results may differ from a plain program's by a relative error of at most 0.0055.
Values may be sent and summed in bfloat16 or wider, within the bound.
No kernel may reach another device: no remote copies, remote signals or barrier semaphores. Data moves between devices by JAX's collectives and lax.ppermute only.
A program may use at most 192 MiB of HBM per device.

v0:
```python
import jax
import jax.numpy as jnp
from jax import lax
from jax.sharding import PartitionSpec as P


def passed_along(array, axis, by):
    count = lax.axis_size(axis)
    pairs = [(i, i + by) for i in range(count) if 0 <= i + by < count]
    return lax.ppermute(array, axis, pairs)


def per_device(w_first, w_second, saved_inputs, saved_hidden, cotangent):
    section_index = lax.axis_index("section")
    weight_first = w_first[0]
    weight_second = w_second[0]
    inputs_all = saved_inputs[0]
    hidden_all = saved_hidden[0]
    micro_count = cotangent.shape[0]
    row_count = cotangent.shape[1]
    width_local = cotangent.shape[2]
    share_rows_count = row_count // lax.axis_size("hid")
    received = jnp.zeros((row_count, width_local), jnp.bfloat16)
    first_sum = jnp.zeros(weight_first.shape, jnp.float32)
    second_sum = jnp.zeros(weight_second.shape, jnp.float32)
    results = [
        jnp.zeros((share_rows_count, width_local), jnp.bfloat16) for entry in range(micro_count)
    ]
    for period in range(micro_count + 1):
        micro_index = jnp.int32(period - 1) + section_index
        active = jnp.logical_and(micro_index >= 0, micro_index < micro_count)
        chosen = jnp.clip(micro_index, 0, micro_count - 1)
        given_rows = lax.dynamic_index_in_dim(cotangent, chosen, 0, keepdims=False)
        incoming = jnp.where(section_index == 1, given_rows, received)
        incoming = jnp.where(active, incoming, jnp.zeros_like(incoming))
        inputs_now = lax.dynamic_index_in_dim(inputs_all, chosen, 0, keepdims=False)
        pre_act = lax.dynamic_index_in_dim(hidden_all, chosen, 0, keepdims=False)
        activated = jnp.maximum(pre_act, 0)
        partial_sum = lax.dot_general(
            incoming, weight_second, (((1,), (1,)), ((), ())), preferred_element_type=jnp.float32
        )
        block_sum = lax.psum_scatter(partial_sum, "wid", scatter_dimension=0, tiled=True)
        block_rows = block_sum.shape[0]
        block_pre = lax.dynamic_slice_in_dim(
            pre_act, lax.axis_index("wid") * block_rows, block_rows, 0
        )
        block_grad = jnp.where(block_pre > 0, block_sum, jnp.float32(0.0)).astype(jnp.bfloat16)
        hidden_grad = lax.all_gather(block_grad, "wid", axis=0, tiled=True)
        second_sum = second_sum + lax.dot_general(
            activated, incoming, (((0,), (0,)), ((), ())), preferred_element_type=jnp.float32
        )
        first_sum = first_sum + lax.dot_general(
            inputs_now, hidden_grad, (((0,), (0,)), ((), ())), preferred_element_type=jnp.float32
        )
        row_share = lax.psum_scatter(
            lax.dot_general(
                hidden_grad,
                weight_first,
                (((1,), (1,)), ((), ())),
                preferred_element_type=jnp.float32,
            ),
            "hid",
            scatter_dimension=0,
            tiled=True,
        ).astype(jnp.bfloat16)
        for entry in range(micro_count):
            results[entry] = jnp.where(
                jnp.logical_and(active, chosen == entry), row_share, results[entry]
            )
        if period < micro_count:
            whole_grad = lax.all_gather(row_share, "hid", axis=0, tiled=True)
            received = passed_along(whole_grad, "section", -1)
    input_grads = jnp.stack(results)[None]
    return (first_sum[None], second_sum[None], input_grads)


def solution(mesh):
    placed = (
        P("section", "wid", "hid"),
        P("section", "hid", "wid"),
        P("section", None, None, "wid"),
        P("section", None, None, "hid"),
        P(None, None, "wid"),
    )
    return jax.shard_map(
        per_device,
        mesh=mesh,
        in_specs=placed,
        out_specs=(
            P("section", "wid", "hid"),
            P("section", "hid", "wid"),
            P("section", None, "hid", "wid"),
        ),
        check_vma=False,
    )
```

profile of v0, /device:TPU:0, one launch (start us, length us, event | category | flops | bytes accessed | tf_op | source)
XLA Modules:
  0.0 703.3 jit_solution(6821142226279977669)
XLA Ops:
  7.2 0.0 reduce-scatter.7.cloned.1.call-start
  7.2 11.0 %fusion.10 = f32[256,5120]{1,0:T(8,128)} fusion(bf16[1,5120,1280]{2,1,0:T(8,128)(2,1)} %param.6, bf16[2,256,1280]{2,1,0:T(8,128)(2,1)} %param.9, s32[]{:T(128)S(6)} %min.16, pred[]{:T(512)S(6)} %eq.23, pred[]{:T(512)S(6)} %and.29), kind=kOutput, calls=%fused_computation.12 | convolution fusion | flops 3356098560 | bytes 19005446 | tf_op jit(solution)/shard_map/dot_general | solution.py:39
  18.2 0.0 reduce-scatter.7.cloned.1.call-update
  18.2 0.0 all-gather.4.cloned.1.call-start
  18.3 96.6 %reduce-scatter.7.cloned.1.call-done = f32[64,5120]{1,0:T(8,128)} async-done(((f32[256,5120]{1,0:T(8,128)}), f32[64,5120]{1,0:T(8,128)}) %reduce-scatter.7.cloned.1.call-update) | async-done | bytes 1310736 | tf_op jit(solution)/shard_map/reduce_scatter | solution.py:42
  114.9 2.6 select_convert_fusion.2
  117.5 0.0 all-gather.4.cloned.1.call-update
  117.5 0.0 reduce-scatter.9.cloned.1.call-start
  117.5 55.4 %all-gather.4.cloned.1.call-done = bf16[256,5120]{1,0:T(8,128)(2,1)} async-done(((bf16[64,5120]{1,0:T(8,128)(2,1)}), bf16[256,5120]{1,0:T(8,128)(2,1)}) %all-gather.4.cloned.1.call-update) | async-done | bytes 2621456 | tf_op jit(solution)/shard_map/all_gather | solution.py:48
  172.9 10.2 %fusion.4 = f32[256,1280]{1,0:T(8,128)} fusion(bf16[256,5120]{1,0:T(8,128)(2,1)} %all-gather.4.cloned.1.call-done, bf16[1,1280,5120]{2,1,0:T(8,128)(2,1)} %param.5), kind=kOutput, calls=%fused_computation.6 | convolution fusion | flops 3355443200 | bytes 17039360 | tf_op jit(solution)/shard_map/dot_general | solution.py:56
  183.1 0.0 reduce-scatter.9.cloned.1.call-update
  183.1 0.0 reduce-scatter.11.cloned.1.call-start
  183.1 25.3 %reduce-scatter.9.cloned.1.call-done = f32[64,1280]{1,0:T(8,128)} async-done(((f32[256,1280]{1,0:T(8,128)}), f32[64,1280]{1,0:T(8,128)}) %reduce-scatter.9.cloned.1.call-update) | async-done | bytes 327696 | tf_op jit(solution)/shard_map/reduce_scatter | solution.py:55
  208.5 1.0 convert_element_type.19
  209.5 7.3 %all_gather.16 = bf16[256,1280]{1,0:T(8,128)(2,1)S(1)} all-gather(bf16[64,1280]{1,0:T(8,128)(2,1)S(1)} %convert_element_type.19), channel_id=1, replica_groups=mesh['section'=2,'hid'=4,'wid'=4] {'hid'}, dimensions={0}, use_global_device_ids=true | all-gather | bytes 819200 | tf_op jit(solution)/shard_map/all_gather | solution.py:71
  216.7 1.3 collective-permute-start
  218.0 17.7 %collective-permute-done = bf16[256,1280]{1,0:T(8,128)(2,1)} collective-permute-done((bf16[256,1280]{1,0:T(8,128)(2,1)S(1)}, bf16[256,1280]{1,0:T(8,128)(2,1)}, u32[]{:S(2)}, u32[]{:S(2)}) %collective-permute-start) | collective-permute-done | bytes 655392 | tf_op jit(solution)/shard_map/ppermute | solution.py:10
  235.7 10.9 %fusion.8 = f32[256,5120]{1,0:T(8,128)} fusion(bf16[1,5120,1280]{2,1,0:T(8,128)(2,1)} %param.6, bf16[256,1280]{1,0:T(8,128)(2,1)} %collective-permute-done, bf16[2,256,1280]{2,1,0:T(8,128)(2,1)S(1)} %copy-done.1, s32[]{:T(128)S(6)} %min.18, pred[]{:T(512)S(6)} %eq.23, pred[]{:T(512)S(6)} %and.30), kind=kOutput, calls=%fused_computation.10 | convolution fusion | flops 3356098560 | bytes 19660806 | tf_op jit(solution)/shard_map/dot_general | solution.py:39
  246.6 0.0 all-gather.6.cloned.1.call-start
  246.7 93.5 %reduce-scatter.11.cloned.1.call-done = f32[64,5120]{1,0:T(8,128)} async-done(((f32[256,5120]{1,0:T(8,128)}), f32[64,5120]{1,0:T(8,128)}) %reduce-scatter.11.cloned.1.call-update) | async-done | bytes 1310736 | tf_op jit(solution)/shard_map/reduce_scatter | solution.py:42
  340.2 2.6 select_convert_fusion.1
  342.8 0.2 reduce-scatter.13.cloned.1.call-start
  343.1 55.2 %all-gather.6.cloned.1.call-done = bf16[256,5120]{1,0:T(8,128)(2,1)} async-done(((bf16[64,5120]{1,0:T(8,128)(2,1)}), bf16[256,5120]{1,0:T(8,128)(2,1)}) %all-gather.6.cloned.1.call-update) | async-done | bytes 2621456 | tf_op jit(solution)/shard_map/all_gather | solution.py:48
  398.2 10.2 %fusion.2 = f32[256,1280]{1,0:T(8,128)} fusion(bf16[256,5120]{1,0:T(8,128)(2,1)} %all-gather.6.cloned.1.call-done, bf16[1,1280,5120]{2,1,0:T(8,128)(2,1)} %param.5), kind=kOutput, calls=%fused_computation.4 | convolution fusion | flops 3355443200 | bytes 17039360 | tf_op jit(solution)/shard_map/dot_general | solution.py:56
  408.4 0.0 reduce-scatter.15.cloned.1.call-start
  408.5 25.3 %reduce-scatter.13.cloned.1.call-done = f32[64,1280]{1,0:T(8,128)} async-done(((f32[256,1280]{1,0:T(8,128)}), f32[64,1280]{1,0:T(8,128)}) %reduce-scatter.13.cloned.1.call-update) | async-done | bytes 327696 | tf_op jit(solution)/shard_map/reduce_scatter | solution.py:55
  433.8 1.0 convert_element_type.21
  434.8 7.8 %all_gather.18 = bf16[256,1280]{1,0:T(8,128)(2,1)} all-gather(bf16[64,1280]{1,0:T(8,128)(2,1)S(1)} %convert_element_type.21), channel_id=1, replica_groups=mesh['section'=2,'hid'=4,'wid'=4] {'hid'}, dimensions={0}, use_global_device_ids=true | all-gather | bytes 819200 | tf_op jit(solution)/shard_map/all_gather | solution.py:71
  442.5 1.3 collective-permute-start.1
  443.8 17.8 %collective-permute-done.1 = bf16[256,1280]{1,0:T(8,128)(2,1)S(1)} collective-permute-done((bf16[256,1280]{1,0:T(8,128)(2,1)}, bf16[256,1280]{1,0:T(8,128)(2,1)S(1)}, u32[]{:S(2)}, u32[]{:S(2)}) %collective-permute-start.1) | collective-permute-done | bytes 655392 | tf_op jit(solution)/shard_map/ppermute | solution.py:10
  461.6 14.8 %fusion.6 = f32[256,5120]{1,0:T(8,128)} fusion(bf16[1,5120,1280]{2,1,0:T(8,128)(2,1)} %param.6, bf16[256,1280]{1,0:T(8,128)(2,1)S(1)} %collective-permute-done.1, bf16[2,256,1280]{2,1,0:T(8,128)(2,1)S(1)} %copy-done.1, s32[]{:T(128)S(6)} %min.20, pred[]{:T(512)S(6)} %and.31, pred[]{:T(512)S(6)} %eq.23), kind=kOutput, calls=%fused_computation.8 | convolution fusion | flops 3356098560 | bytes 19660806 | tf_op jit(solution)/shard_map/dot_general | solution.py:39
  476.5 0.0 reduce-scatter.15.cloned.1.call-update
  476.5 0.0 all-gather.8.cloned.1.call-start
  476.6 13.3 %fusion.15 = f32[5120,1280]{1,0:T(8,128)} fusion(bf16[1,2,256,5120]{3,2,1,0:T(8,128)(2,1)} %param.8, s32[]{:T(128)S(6)} %min.16, bf16[2,256,1280]{2,1,0:T(8,128)(2,1)S(1)} %copy-done.1, pred[]{:T(512)S(6)} %eq.23, pred[]{:T(512)S(6)} %and.29), kind=kOutput, calls=%fused_computation.17 | convolution fusion | flops 3357409280 | bytes 29493248 | tf_op jit(solution)/shard_map/dot_general | solution.py:49
  489.9 80.2 %reduce-scatter.15.cloned.1.call-done = f32[64,5120]{1,0:T(8,128)} async-done(((f32[256,5120]{1,0:T(8,128)}), f32[64,5120]{1,0:T(8,128)}) %reduce-scatter.15.cloned.1.call-update) | async-done | bytes 1310736 | tf_op jit(solution)/shard_map/reduce_scatter | solution.py:42
  570.1 2.6 select_convert_fusion
  572.7 0.0 all-gather.8.cloned.1.call-update
  572.7 0.3 reduce-scatter.17.cloned.1.call-start
  573.0 12.9 %fusion.33 = f32[1280,5120]{1,0:T(8,128)} fusion(bf16[256,5120]{1,0:T(8,128)(2,1)} %all-gather.4.cloned.1.call-done, bf16[1,2,256,1280]{3,2,1,0:T(8,128)(2,1)S(1)} %copy-done, s32[]{:T(128)S(6)} %min.16), kind=kOutput, calls=%fused_computation.40 | convolution fusion | flops 3355443200 | bytes 29491204 | tf_op jit(solution)/shard_map/dot_general | solution.py:52
  585.9 14.4 %fusion.13 = f32[5120,1280]{1,0:T(8,128)} fusion(bf16[1,2,256,5120]{3,2,1,0:T(8,128)(2,1)} %param.8, s32[]{:T(128)S(6)} %min.18, bf16[256,1280]{1,0:T(8,128)(2,1)} %collective-permute-done, bf16[2,256,1280]{2,1,0:T(8,128)(2,1)S(1)} %copy-done.1, pred[]{:T(512)S(6)} %eq.23, pred[]{:T(512)S(6)} %and.30), kind=kOutput, calls=%fused_computation.15 | convolution fusion | flops 3357409280 | bytes 30148608 | tf_op jit(solution)/shard_map/dot_general | solution.py:49
  600.4 10.6 %fusion.29 = f32[1280,5120]{1,0:T(8,128)} fusion(bf16[256,5120]{1,0:T(8,128)(2,1)S(1)} %copy-done.2, bf16[1,2,256,1280]{3,2,1,0:T(8,128)(2,1)S(1)} %copy-done, s32[]{:T(128)S(6)} %min.18), kind=kOutput, calls=%fused_computation.36 | convolution fusion | flops 3355443200 | bytes 29491204 | tf_op jit(solution)/shard_map/dot_general | solution.py:52
  611.0 17.1 %all-gather.8.cloned.1.call-done = bf16[256,5120]{1,0:T(8,128)(2,1)} async-done(((bf16[64,5120]{1,0:T(8,128)(2,1)}), bf16[256,5120]{1,0:T(8,128)(2,1)}) %all-gather.8.cloned.1.call-update) | async-done | bytes 2621456 | tf_op jit(solution)/shard_map/all_gather | solution.py:48
  628.1 10.2 %fusion = f32[256,1280]{1,0:T(8,128)} fusion(bf16[256,5120]{1,0:T(8,128)(2,1)} %all-gather.8.cloned.1.call-done, bf16[1,1280,5120]{2,1,0:T(8,128)(2,1)} %param.5), kind=kOutput, calls=%fused_computation.2 | convolution fusion | flops 3355443200 | bytes 17039360 | tf_op jit(solution)/shard_map/dot_general | solution.py:56
  638.3 0.0 reduce-scatter.17.cloned.1.call-update
  638.3 28.8 %add_bitcast_fusion = f32[1,5120,1280]{2,1,0:T(8,128)} fusion(f32[5120,1280]{1,0:T(8,128)} %fusion.15, f32[5120,1280]{1,0:T(8,128)} %fusion.13, bf16[1,2,256,5120]{3,2,1,0:T(8,128)(2,1)} %param.8, s32[]{:T(128)S(6)} %min.20, bf16[256,1280]{1,0:T(8,128)(2,1)S(1)} %collective-permute-done.1, bf16[2,256,1280]{2,1,0:T(8,128)(2,1)S(1)} %copy-done.1, pred[]{:T(512)S(6)} %and.31, ...), kind=kOutput, calls=%fused_computation | convolution fusion | flops 3370516480 | bytes 82577408 | tf_op jit(solution)/shard_map/dot_general | solution.py:49
  667.2 27.8 %add_bitcast_fusion.1 = f32[1,1280,5120]{2,1,0:T(8,128)} fusion(f32[1280,5120]{1,0:T(8,128)} %fusion.33, f32[1280,5120]{1,0:T(8,128)} %fusion.29, bf16[256,5120]{1,0:T(8,128)(2,1)} %all-gather.8.cloned.1.call-done, bf16[1,2,256,1280]{3,2,1,0:T(8,128)(2,1)S(1)} %copy-done, s32[]{:T(128)S(6)} %min.20), kind=kOutput, calls=%fused_computation.1 | convolution fusion | flops 3368550400 | bytes 81920000 | tf_op jit(solution)/shard_map/dot_general | solution.py:52
  694.9 1.0 select_bitcast_fusion.1
  696.0 0.8 maximum_bitcast_fusion
  (14 shorter events, 0.1 us)
Async XLA Ops:
  7.2 565.8 %copy-start = (bf16[1,2,256,1280]{3,2,1,0:T(8,128)(2,1)S(1)}, bf16[1,2,256,1280]{3,2,1,0:T(8,128)(2,1)}, u32[]{:S(2)}) copy-start(bf16[1,2,256,1280]{3,2,1,0:T(8,128)(2,1)} %param.7) | copy-start | bytes 3932164
  7.2 107.7 %reduce-scatter.7.cloned.1.call-start = ((), (), s32[]{:S(2)}) async-start(), calls=%async_computation.6 | async-start | bytes 6553600 | tf_op jit(solution)/shard_map/reduce_scatter | solution.py:42
  18.2 154.7 %all-gather.4.cloned.1.call-start = ((), (), s32[]{:S(2)}) async-start(), calls=%async_computation.7 | async-start | bytes 3276800 | tf_op jit(solution)/shard_map/all_gather | solution.py:48
  117.5 91.0 %reduce-scatter.9.cloned.1.call-start = ((), (), s32[]{:S(2)}) async-start(), calls=%async_computation.8 | async-start | bytes 1638400 | tf_op jit(solution)/shard_map/reduce_scatter | solution.py:55
  183.1 52.7 %copy-start.1 = (bf16[2,256,1280]{2,1,0:T(8,128)(2,1)S(1)}, bf16[2,256,1280]{2,1,0:T(8,128)(2,1)}, u32[]{:S(2)}) copy-start(bf16[2,256,1280]{2,1,0:T(8,128)(2,1)} %param.9) | copy-start | bytes 3932164
  183.1 157.1 %reduce-scatter.11.cloned.1.call-start = ((), (), s32[]{:S(2)}) async-start(), calls=%async_computation.9 | async-start | bytes 6553600 | tf_op jit(solution)/shard_map/reduce_scatter | solution.py:42
  216.7 19.0 %collective-permute-start = (bf16[256,1280]{1,0:T(8,128)(2,1)S(1)}, bf16[256,1280]{1,0:T(8,128)(2,1)}, u32[]{:S(2)}, u32[]{:S(2)}) collective-permute-start(bf16[256,1280]{1,0:T(8,128)(2,1)S(1)} %all_gather.16), channel_id=1, source_target_pairs={{16,0},{17,1},{18,2},{19,3},{20,4},{21,5},{22,6},{23,7},{24,8},{25... | collective-permute-start | bytes 1966088 | tf_op jit(solution)/shard_map/ppermute | solution.py:10
  246.6 151.6 %all-gather.6.cloned.1.call-start = ((), (), s32[]{:S(2)}) async-start(), calls=%async_computation.10 | async-start | bytes 3276800 | tf_op jit(solution)/shard_map/all_gather | solution.py:48
  342.8 90.9 %reduce-scatter.13.cloned.1.call-start = ((), (), s32[]{:S(2)}) async-start(), calls=%async_computation.11 | async-start | bytes 1638400 | tf_op jit(solution)/shard_map/reduce_scatter | solution.py:55
  408.4 161.7 %reduce-scatter.15.cloned.1.call-start = ((), (), s32[]{:S(2)}) async-start(), calls=%async_computation.12 | async-start | bytes 6553600 | tf_op jit(solution)/shard_map/reduce_scatter | solution.py:42
  442.5 19.1 %collective-permute-start.1 = (bf16[256,1280]{1,0:T(8,128)(2,1)}, bf16[256,1280]{1,0:T(8,128)(2,1)S(1)}, u32[]{:S(2)}, u32[]{:S(2)}) collective-permute-start(bf16[256,1280]{1,0:T(8,128)(2,1)} %all_gather.18), channel_id=1, source_target_pairs={{16,0},{17,1},{18,2},{19,3},{20,4},{21,5},{22,6},{23,7},{24,8},{25... | collective-permute-start | bytes 1966088 | tf_op jit(solution)/shard_map/ppermute | solution.py:10
  476.5 151.6 %all-gather.8.cloned.1.call-start = ((), (), s32[]{:S(2)}) async-start(), calls=%async_computation.13 | async-start | bytes 3276800 | tf_op jit(solution)/shard_map/all_gather | solution.py:48
  572.7 122.2 %reduce-scatter.17.cloned.1.call-start = ((), (), s32[]{:S(2)}) async-start(), calls=%async_computation.14 | async-start | bytes 1638400 | tf_op jit(solution)/shard_map/reduce_scatter | solution.py:55
  585.9 14.4 %copy-start.2 = (bf16[256,5120]{1,0:T(8,128)(2,1)S(1)}, bf16[256,5120]{1,0:T(8,128)(2,1)}, u32[]{:S(2)}) copy-start(bf16[256,5120]{1,0:T(8,128)(2,1)} %all-gather.6.cloned.1.call-done) | copy-start | bytes 7864324
  667.2 27.8 %copy-start.3 = (f32[64,1280]{1,0:T(8,128)S(1)}, f32[64,1280]{1,0:T(8,128)}, u32[]{:S(2)}) copy-start(f32[64,1280]{1,0:T(8,128)} %reduce-scatter.9.cloned.1.call-done) | copy-start | bytes 983044
  667.2 27.8 %copy-start.4 = (f32[64,1280]{1,0:T(8,128)S(1)}, f32[64,1280]{1,0:T(8,128)}, u32[]{:S(2)}) copy-start(f32[64,1280]{1,0:T(8,128)} %reduce-scatter.13.cloned.1.call-done) | copy-start | bytes 983044
Sparse Core Ops, SparseCore 0:
  18.3 96.4 reduce-scatter.6
  117.6 55.2 all-gather.3
  183.2 25.2 reduce-scatter.8
  246.8 93.4 reduce-scatter.10
  343.0 55.2 all-gather.5
  408.6 25.1 reduce-scatter.12
  476.6 93.4 reduce-scatter.14
  572.8 55.2 all-gather.7
  638.4 25.1 reduce-scatter.16
where the time goes:
time: 704 us; the launch traced here: 703 us
  waiting for transfers between devices  484 us (69%)
  matrix products  175 us (25%)
  blocking collectives  15.1 us (2%)
  between operations  14 us (2%)
  other arithmetic  11.6 us (2%)
    reduce_scatter x3, waiting for transfers between devices, per_device(): lax.psum_scatter(partial_sum, 'wid', scatter_dimension=0, tiled=True)  270 us
    all_gather x3, waiting for transfers between devices, per_device(): hidden_grad = lax.all_gather(block_grad, 'wid', axis=0, tiled=True)  128 us
    dot_general x3, matrix products, per_device(): lax.dot_general(activated, incoming, (((0,), (0,)), ((), ())), preferred_...  56.6 us
    dot_general x3, matrix products, per_device(): lax.dot_general(inputs_now, hidden_grad, (((0,), (0,)), ((), ())), prefer...  51.3 us
    reduce_scatter x3, waiting for transfers between devices, per_device(): lax.psum_scatter(lax.dot_general(hidden_grad, weight_first, (((1,), (1,))...  50.6 us
    dot_general x3, matrix products, per_device(): lax.dot_general(incoming, weight_second, (((1,), (1,)), ((), ())), prefer...  36.7 us
    ppermute x2, waiting for transfers between devices, passed_along(): return lax.ppermute(array, axis, pairs)  35.5 us
    dot_general x3, matrix products, per_device(): lax.dot_general(hidden_grad, weight_first, (((1,), (1,)), ((), ())), pref...  30.5 us
  transfers between devices with their start and end apart: 11, of which 10 were waited for; matrix products, arithmetic and copies ran while one was open for 15% of the time, Pallas kernels for 0%

commit v1 on v0

v1 whole, which is shorter than its diff:
```python
import functools

import jax
import jax.numpy as jnp
from jax import lax
from jax.experimental import pallas as pl
from jax.experimental.pallas import tpu as pltpu
from jax.sharding import PartitionSpec as P

SUB_CHUNKS = 2
LAG = 2


def exchange(blocks, axis):
    count = lax.axis_size(axis)
    arrived = []
    for shift in range(1, count):
        pairs = [(i, (i + shift) % count) for i in range(count)]
        arrived.append(lax.ppermute(blocks[shift - 1], axis, pairs))
    return arrived


def hand_down(share):
    sections, hids = lax.axis_size("section"), lax.axis_size("hid")
    arrived = []
    for shift in range(hids):
        pairs = [
            (s * hids + h, (s - 1) * hids + (h + shift) % hids)
            for s in range(1, sections)
            for h in range(hids)
        ]
        arrived.append(lax.ppermute(share, ("section", "hid"), pairs))
    return arrived


def estimate(flops, moved):
    return pl.CostEstimate(flops=flops, bytes_accessed=moved, transcendentals=0)


def dot(left, right, left_dim, right_dim):
    return lax.dot_general(
        left, right, (((left_dim,), (right_dim,)), ((), ())), preferred_element_type=jnp.float32
    )


def piece_of(size, wanted):
    fits = [p for p in range(128, wanted + 1, 128) if size % p == 0]
    return fits[-1] if fits else size


def project_kernel(count, hids, place_ref, given_ref, *refs):
    received_refs, refs = refs[:hids], refs[hids:]
    weight_ref, refs = refs[0], refs[1:]
    sent_refs, (own_ref, incoming_ref, turned_ref) = refs[: count - 1], refs[count - 1 :]
    step = pl.program_id(0)
    rows, width = incoming_ref.shape
    sub = rows // hids

    @pl.when((step == 0) & (pl.program_id(1) == 0))
    def _():
        @pl.when(place_ref[0] == 1)
        def _():
            incoming_ref[...] = given_ref[...].reshape(rows, width)

        @pl.when(place_ref[0] != 1)
        def _():
            for k in range(hids):
                start = pl.multiple_of(place_ref[3 + k] * sub, sub)
                incoming_ref[pl.ds(start, sub), :] = received_refs[k][...]

        turned_ref[...] = incoming_ref[...].T

    block = dot(weight_ref[...], turned_ref[...], 1, 0)
    for k in range(count - 1):

        @pl.when(step == k)
        def _(k=k):
            sent_refs[k][...] = block.astype(sent_refs[k].dtype)

    @pl.when(step == count - 1)
    def _():
        own_ref[...] = block


def project(place, given_parts, received, weight, count):
    hidden, width = weight.shape
    hids, _, sub = given_parts.shape[1:4]
    rows = hids * sub
    columns = hidden // count
    piece = piece_of(columns, 1280)
    pieces = columns // piece

    def block_at(own_step):
        def index(k, c, s):
            return (jnp.where(k == own_step, c, jnp.where(k < own_step, 0, pieces - 1)), 0)

        return pl.BlockSpec((piece, rows), index)

    grid_spec = pltpu.PrefetchScalarGridSpec(
        num_scalar_prefetch=1,
        grid=(count, pieces),
        in_specs=[
            pl.BlockSpec((1, hids, 1, sub, width), lambda k, c, s: (s[1], 0, s[2], 0, 0)),
            *[pl.BlockSpec((sub, width), lambda k, c, s: (0, 0)) for _ in range(hids)],
            pl.BlockSpec((piece, width), lambda k, c, s: (s[3 + hids + k] * pieces + c, 0)),
        ],
        out_specs=[
            *[block_at(k) for k in range(count)],
            pl.BlockSpec((rows, width), lambda k, c, s: (0, 0)),
        ],
        scratch_shapes=[pltpu.VMEM((width, rows), jnp.bfloat16)],
    )
    out = pl.pallas_call(
        functools.partial(project_kernel, count, hids),
        grid_spec=grid_spec,
        out_shape=[
            *[jax.ShapeDtypeStruct((columns, rows), jnp.bfloat16) for _ in range(count - 1)],
            jax.ShapeDtypeStruct((columns, rows), jnp.float32),
            jax.ShapeDtypeStruct((rows, width), jnp.bfloat16),
        ],
        cost_estimate=estimate(2 * rows * width * hidden, 2 * width * hidden),
        name="project",
    )(place, given_parts, *received, weight)
    return out[: count - 1], out[count - 1], out[count]


def join_kernel(place_ref, own_ref, *refs):
    arrived_refs, (hidden_ref, out_ref) = refs[:-2], refs[-2:]
    total = own_ref[...]
    for ref in arrived_refs:
        total += ref[...].astype(jnp.float32)
    out_ref[...] = jnp.where(hidden_ref[...] > 0, total, jnp.float32(0.0)).astype(out_ref.dtype)


def join(place, own, arrived, hidden_t):
    columns, rows = own.shape
    piece = piece_of(columns, 640)
    pieces = columns // piece
    here = pl.BlockSpec((piece, rows), lambda n, s: (n, 0))
    grid_spec = pltpu.PrefetchScalarGridSpec(
        num_scalar_prefetch=1,
        grid=(pieces,),
        in_specs=[here]
        + [here for _ in arrived]
        + [pl.BlockSpec((piece, rows), lambda n, s: (s[0] * pieces + n, s[1]))],
        out_specs=here,
    )
    return pl.pallas_call(
        join_kernel,
        grid_spec=grid_spec,
        out_shape=jax.ShapeDtypeStruct(own.shape, jnp.bfloat16),
        cost_estimate=estimate(5 * own.size, 14 * own.size),
        name="join",
    )(place, own, *arrived, hidden_t)


def total_kernel(own_ref, *refs):
    total = own_ref[...]
    for ref in refs[:-1]:
        total += ref[...]
    refs[-1][...] = total.astype(refs[-1].dtype)


def rounded_total(own, arrived):
    return pl.pallas_call(
        total_kernel,
        out_shape=jax.ShapeDtypeStruct(own.shape, jnp.bfloat16),
        cost_estimate=estimate(4 * own.size, 18 * own.size),
        name="total",
    )(own, *arrived)


def back_kernel(hids, place_ref, grads_ref, weight_ref, *refs):
    out_refs, piece_ref = refs[:hids], refs[hids]
    sub = out_refs[0].shape[0]
    piece_ref[...] = dot(weight_ref[...], grads_ref[...], 1, 0).T
    for k in range(hids):
        start = pl.multiple_of(place_ref[k] * sub, sub)
        out_refs[k][...] = piece_ref[pl.ds(start, sub), :]


def back(place, grads, weight, hids):
    hidden, rows = grads.shape
    width = weight.shape[0]
    sub = rows // hids
    piece = piece_of(width, 256)
    grid_spec = pltpu.PrefetchScalarGridSpec(
        num_scalar_prefetch=1,
        grid=(width // piece,),
        in_specs=[
            pl.BlockSpec((hidden, rows), lambda n, s: (0, 0)),
            pl.BlockSpec((piece, hidden), lambda n, s: (n, 0)),
        ],
        out_specs=[pl.BlockSpec((sub, piece), lambda n, s: (0, n)) for _ in range(hids)],
        scratch_shapes=[pltpu.VMEM((rows, piece), jnp.float32)],
    )
    return pl.pallas_call(
        functools.partial(back_kernel, hids),
        grid_spec=grid_spec,
        out_shape=[jax.ShapeDtypeStruct((sub, width), jnp.float32) for _ in range(hids)],
        cost_estimate=estimate(2 * rows * width * hidden, 2 * width * hidden),
        name="back",
    )(place, grads, weight)


def first_kernel(inputs_ref, grads_ref, out_ref):
    grads = jnp.concatenate([grads_ref[c] for c in range(grads_ref.shape[0])], axis=1)
    out_ref[...] = dot(inputs_ref[...], grads, 1, 1)


def first_gradient(inputs_t, slots, chunks):
    width, rows = inputs_t.shape
    _, hidden, chunk_rows = slots.shape
    piece = piece_of(hidden, 640)
    return pl.pallas_call(
        first_kernel,
        grid=(hidden // piece,),
        in_specs=[
            pl.BlockSpec((width, rows), lambda n: (0, 0)),
            pl.BlockSpec((chunks, piece, chunk_rows), lambda n: (0, n, 0)),
        ],
        out_specs=pl.BlockSpec((width, piece), lambda n: (0, n)),
        out_shape=jax.ShapeDtypeStruct((width, hidden), jnp.float32),
        cost_estimate=estimate(2 * rows * width * hidden, 4 * width * hidden),
        name="first_gradient",
    )(inputs_t, slots)


def second_kernel(hidden_ref, incoming_ref, out_ref):
    chunks, rows, width = incoming_ref.shape
    active = jnp.maximum(hidden_ref[...], 0)
    out_ref[...] = dot(active, incoming_ref[...].reshape(chunks * rows, width), 1, 0)


def second_gradient(hidden_t, slots, chunks):
    hidden, rows = hidden_t.shape
    _, chunk_rows, width = slots.shape
    piece = piece_of(hidden, 640)
    return pl.pallas_call(
        second_kernel,
        grid=(hidden // piece,),
        in_specs=[
            pl.BlockSpec((piece, rows), lambda n: (n, 0)),
            pl.BlockSpec((chunks, chunk_rows, width), lambda n: (0, 0, 0)),
        ],
        out_specs=pl.BlockSpec((piece, width), lambda n: (n, 0)),
        out_shape=jax.ShapeDtypeStruct((hidden, width), jnp.float32),
        cost_estimate=estimate(2 * rows * width * hidden, 4 * width * hidden),
        name="second_gradient",
    )(hidden_t, slots)


def rows_last(parts):
    return parts.transpose(4, 0, 2, 1, 3).reshape(parts.shape[-1], -1)


def per_device(w_first, w_second, saved_inputs, saved_hidden, cotangent):
    sections = lax.axis_size("section")
    hids = lax.axis_size("hid")
    wids = lax.axis_size("wid")
    section = lax.axis_index("section")
    wid = lax.axis_index("wid")
    hid = lax.axis_index("hid")
    behind = LAG * (sections - 1 - section)
    is_last = (section == sections - 1).astype(jnp.int32)
    weight_first = w_first[0]
    weight_second = w_second[0]
    micro, rows, width = cotangent.shape
    hidden = saved_hidden.shape[-1]
    sub = rows // hids // SUB_CHUNKS
    chunk_rows = hids * sub
    chunks = micro * SUB_CHUNKS
    periods = chunks + LAG * (sections - 1)
    parts = (micro, hids, SUB_CHUNKS, sub)
    cot_parts = cotangent.reshape(*parts, width)
    hidden_t = rows_last(saved_hidden.reshape(*parts, hidden))
    inputs_t = rows_last(saved_inputs.reshape(*parts, width))
    wid_order = lax.rem(wid + 1 + jnp.arange(wids, dtype=jnp.int32), wids)
    hid_order = lax.rem(hid + 1 + jnp.arange(hids, dtype=jnp.int32), hids)
    hid_senders = lax.rem(hid + hids - jnp.arange(hids, dtype=jnp.int32), hids)

    incoming_slots = jnp.zeros((periods, chunk_rows, width), jnp.bfloat16)
    grad_slots = jnp.zeros((periods, hidden, chunk_rows), jnp.bfloat16)
    result_slots = jnp.zeros((periods, sub, width), jnp.bfloat16)
    nothing = [jnp.zeros((sub, width), jnp.bfloat16)] * hids
    received = {}
    for period in range(periods):
        slot = jnp.maximum(period - behind, 0)
        chosen = jnp.minimum(slot, chunks - 1)
        m, j = chosen // SUB_CHUNKS, lax.rem(chosen, SUB_CHUNKS)
        taken = is_last if period in received else jnp.int32(1)
        place = jnp.concatenate([jnp.stack([taken, m, j]), hid_senders, wid_order])
        sent, own, incoming = project(
            place, cot_parts, received.get(period, nothing), weight_second, wids
        )
        arrived = exchange(sent, "wid")
        block_grad = join(jnp.stack([wid, chosen]), own, arrived, hidden_t)
        hidden_grad = lax.all_gather(block_grad, "wid", axis=0, tiled=True)
        incoming_slots = lax.dynamic_update_slice_in_dim(incoming_slots, incoming[None], slot, 0)
        grad_slots = lax.dynamic_update_slice_in_dim(grad_slots, hidden_grad[None], slot, 0)
        shares = back(hid_order, hidden_grad, weight_first, hids)
        arrived = exchange(shares[:-1], "hid")
        row_share = rounded_total(shares[-1], arrived)
        result_slots = lax.dynamic_update_slice_in_dim(result_slots, row_share[None], slot, 0)
        if period + LAG < periods:
            received[period + LAG] = hand_down(row_share)

    grad_second = second_gradient(hidden_t, incoming_slots, chunks)
    grad_first = first_gradient(inputs_t, grad_slots, chunks)
    input_grads = result_slots[:chunks].reshape(micro, SUB_CHUNKS * sub, width)
    return (grad_first[None], grad_second[None], input_grads[None])


def solution(mesh):
    placed = (
        P("section", "wid", "hid"),
        P("section", "hid", "wid"),
        P("section", None, None, "wid"),
        P("section", None, None, "hid"),
        P(None, None, "wid"),
    )

    def step(*arrays):
        return jax.shard_map(
            per_device,
            mesh=mesh,
            in_specs=placed,
            out_specs=(
                P("section", "wid", "hid"),
                P("section", "hid", "wid"),
                P("section", None, "hid", "wid"),
            ),
            check_vma=False,
        )(*arrays)

    return step
```

time: 704 us -> 472 us (0.67)
  waiting for transfers between devices: 484 us -> 148 us
  matrix products: 175 us -> 0 us
  Pallas kernels: 0 us -> 113 us
  local copies, waits for them, and re-layouts: 0.02 us -> 98.6 us
  starting transfers between devices: 3.33 us -> 91.4 us
  blocking collectives: 15.1 us -> 0 us
  other arithmetic: 11.6 us -> 4.33 us
    reduce_scatter x6 -> x0, waiting for transfers between devices: 321 us -> none  [the longest x3 270 us: per_device(): lax.psum_scatter(partial_sum, 'wid', scatter_dimension=0, tiled=True)]
    dot_general x12 -> x0, matrix products: 175 us -> none  [the longest x3 56.6 us: per_device(): lax.dot_general(activated, incoming, (((0,), (0,)), ((), ())), preferred_...]
    pallas_call x0 -> x18, Pallas kernels: none -> 113 us  [the longest x6 58.9 us: back(): pl.pallas_call(functools.partial(back_kernel, hids), grid_spec=grid_spec,...]
    all_gather x3 -> x6, waiting for transfers between devices: 128 us -> 25.1 us  [per_device(): hidden_grad = lax.all_gather(block_grad, 'wid', axis=0, tiled=True)]
    ppermute x2 -> x52, starting transfers between devices: 2.56 us -> 91.2 us  [the longest x36 70.4 us: exchange(): arrived.append(lax.ppermute(blocks[shift - 1], axis, pairs))]
    ppermute x2 -> x52, waiting for transfers between devices: 35.5 us -> 122 us  [the longest x36 96.8 us: exchange(): arrived.append(lax.ppermute(blocks[shift - 1], axis, pairs))]
    pallas_call x0 -> x8, local copies, waits for them, and re-layouts: none -> 56.6 us  [the longest x6 55.3 us: project(): pl.pallas_call(functools.partial(project_kernel, count, hids), grid_spec=...]
    all_gather x2 -> x0, blocking collectives: 15.1 us -> none  [per_device(): whole_grad = lax.all_gather(row_share, 'hid', axis=0, tiled=True)]
  transfers between devices with their start and end apart: 11 -> 58, of which waited for: 10 -> 31; matrix products, arithmetic and copies ran while one was open for 15% -> 18% of each run, Pallas kernels for 0% -> 23%
where the time goes in v1:
time: 472 us; the launch traced here: 470 us
  waiting for transfers between devices  148 us (31%)
  Pallas kernels  113 us (24%)
  local copies, waits for them, and re-layouts  98.6 us (21%)
  starting transfers between devices  91.4 us (19%)
  between operations  14.6 us (3%)
    ppermute x36, waiting for transfers between devices, exchange(): arrived.append(lax.ppermute(blocks[shift - 1], axis, pairs))  96.8 us
    ppermute x36, starting transfers between devices, exchange(): arrived.append(lax.ppermute(blocks[shift - 1], axis, pairs))  70.4 us
    pallas_call x6, Pallas kernels, back(): pl.pallas_call(functools.partial(back_kernel, hids), grid_spec=grid_spec,...  58.9 us
    pallas_call x6, local copies, waits for them, and re-layouts, project(): pl.pallas_call(functools.partial(project_kernel, count, hids), grid_spec=...  55.3 us
    ppermute x16, waiting for transfers between devices, hand_down(): arrived.append(lax.ppermute(share, ('section', 'hid'), pairs))  25.5 us
    all_gather x6, waiting for transfers between devices, per_device(): hidden_grad = lax.all_gather(block_grad, 'wid', axis=0, tiled=True)  25.1 us
    ppermute x16, starting transfers between devices, hand_down(): arrived.append(lax.ppermute(share, ('section', 'hid'), pairs))  20.8 us
    pallas_call x6, Pallas kernels, join(): pl.pallas_call(join_kernel, grid_spec=grid_spec, out_shape=jax.ShapeDtype...  18.3 us
  transfers between devices with their start and end apart: 58, of which 31 were waited for; matrix products, arithmetic and copies ran while one was open for 18% of the time, Pallas kernels for 23%

profile of v1, /device:TPU:0, one launch (start us, length us, event | category | flops | bytes accessed | tf_op | source)
XLA Modules:
  0.0 469.8 jit_solution(5185871555368696098)
XLA Ops:
  8.5 9.2 %project.11 = (bf16[6,128,1280]{2,1,0:T(8,128)(2,1)S(1)}, f32[1280,128]{1,0:T(8,128)}, bf16[1280,128]{1,0:T(8,128)(2,1)}, bf16[1280,128]{1,0:T(8,128)(2,1)}, bf16[1280,128]{1,0:T(8,128)(2,1)}) fusion(bf16[6,128,1280]{2,1,0:T(8,128)(2,1)S(1)} %broadcast_in_dim.81, s32[]{:T(128)S(6)} %max.18, s32[11]{0:T(128)S(1)} %concatenate.18, ...), kind=kCustom, calls=%fused_computation.11 | custom fusion | bytes 16466436 | tf_op jit(solution)/shard_map/project/pallas_call | solution.py:113
  17.7 3.1 collective-permute-start
  20.7 2.6 collective-permute-start.1
  24.7 5.3 %copy.19 = bf16[5120,2,2,4,32]{0,4,3,2,1:T(8,128)(2,1)} copy(bf16[5120,2,2,4,32]{0,4,2,3,1:T(8,128)(2,1)} %bitcast.91) | data formatting | bytes 10485760 | tf_op jit(solution)/shard_map/transpose | solution.py:254
  30.0 7.9 %copy.20.refs_3_.hidden_ref = bf16[5120,512]{1,0:T(8,128)(2,1)} copy(bf16[5120,512]{0,1:T(8,128)(2,1)} %bitcast.90) | data formatting | bytes 10485760 | tf_op jit(solution)/shard_map/reshape | solution.py:254
  38.5 6.5 %collective-permute-done.1.refs_1_ = bf16[1280,128]{1,0:T(8,128)(2,1)} collective-permute-done((bf16[1280,128]{1,0:T(8,128)(2,1)}, bf16[1280,128]{1,0:T(8,128)(2,1)}, u32[]{:S(2)}, u32[]{:S(2)}) %collective-permute-start.1) | collective-permute-done | bytes 327712 | tf_op jit(solution)/shard_map/ppermute | solution.py:19
  45.0 3.0 join.6
  48.1 9.2 %project.10 = (bf16[6,128,1280]{2,1,0:T(8,128)(2,1)S(1)}, f32[1280,128]{1,0:T(8,128)}, bf16[1280,128]{1,0:T(8,128)(2,1)}, bf16[1280,128]{1,0:T(8,128)(2,1)}, bf16[1280,128]{1,0:T(8,128)(2,1)}) fusion(bf16[6,128,1280]{2,1,0:T(8,128)(2,1)S(1)} %get-tuple-element.132, s32[]{:T(128)S(6)} %max.19, s32[11]{0:T(128)S(1)} %concatenate.19, ...), kind=kCustom, calls=%fused_computation.10 | custom fusion | bytes 16466436 | tf_op jit(solution)/shard_map/project/pallas_call | solution.py:113
  57.3 7.5 %collective-permute-start.3 = (bf16[1280,128]{1,0:T(8,128)(2,1)}, bf16[1280,128]{1,0:T(8,128)(2,1)}, u32[]{:S(2)}, u32[]{:S(2)}) collective-permute-start(bf16[1280,128]{1,0:T(8,128)(2,1)} %get-tuple-element.145), channel_id=1, source_target_pairs={{0,1},{1,2},{2,3},{3,0},{4,5},{5,6},{6,7},{7,4},{8,9},{9,10},{10,1... | collective-permute-start | bytes 983048 | tf_op jit(solution)/shard_map/ppermute | solution.py:19
  67.8 13.8 %collective-permute-done.3.refs_0_ = bf16[1280,128]{1,0:T(8,128)(2,1)} collective-permute-done((bf16[1280,128]{1,0:T(8,128)(2,1)}, bf16[1280,128]{1,0:T(8,128)(2,1)}, u32[]{:S(2)}, u32[]{:S(2)}) %collective-permute-start.3) | collective-permute-done | bytes 327712 | tf_op jit(solution)/shard_map/ppermute | solution.py:19
  81.6 22.9 %collective-permute-done.4.refs_1_ = bf16[1280,128]{1,0:T(8,128)(2,1)} collective-permute-done((bf16[1280,128]{1,0:T(8,128)(2,1)}, bf16[1280,128]{1,0:T(8,128)(2,1)}, u32[]{:S(2)}, u32[]{:S(2)}) %collective-permute-start.4) | collective-permute-done | bytes 327712 | tf_op jit(solution)/shard_map/ppermute | solution.py:19
  104.5 3.0 join.7
  108.1 3.0 all-gather.7.cloned.1.call-done.grads_ref
  111.1 9.8 %back.6 = (f32[32,1280]{1,0:T(8,128)}, f32[32,1280]{1,0:T(8,128)}, f32[32,1280]{1,0:T(8,128)}, f32[32,1280]{1,0:T(8,128)}) custom-call(s32[4]{0:T(128)} %compare_select_fusion.place_ref, bf16[5120,128]{1,0:T(8,128)(2,1)} %all-gather.7.cloned.1.call-done.grads_ref, bf16[1280,5120]{1,0:T(8,128)(2,1)} %bitcast.76), custom_call_target="tpu_custom_call" | custom-call | flops 1677721600 | bytes 13107200 | tf_op jit(solution)/shard_map/back/pallas_call | solution.py:197
  123.9 3.1 collective-permute-done.6.refs_0_
  138.0 4.5 collective-permute-done.11
  143.0 2.6 collective-permute-done.9
  145.7 9.2 %project.9 = (bf16[6,128,1280]{2,1,0:T(8,128)(2,1)S(1)}, f32[1280,128]{1,0:T(8,128)}, bf16[1280,128]{1,0:T(8,128)(2,1)}, bf16[1280,128]{1,0:T(8,128)(2,1)}, bf16[1280,128]{1,0:T(8,128)(2,1)}) fusion(bf16[6,128,1280]{2,1,0:T(8,128)(2,1)S(1)} %get-tuple-element.142, s32[]{:T(128)S(6)} %max.20, s32[11]{0:T(128)S(1)} %concatenate.20, ...), kind=kCustom, calls=%fused_computation.9 | custom fusion | bytes 16712196 | tf_op jit(solution)/shard_map/project/pallas_call | solution.py:113
  154.9 8.0 %collective-permute-start.13 = (bf16[1280,128]{1,0:T(8,128)(2,1)}, bf16[1280,128]{1,0:T(8,128)(2,1)}, u32[]{:S(2)}, u32[]{:S(2)}) collective-permute-start(bf16[1280,128]{1,0:T(8,128)(2,1)} %get-tuple-element.125), channel_id=1, source_target_pairs={{0,1},{1,2},{2,3},{3,0},{4,5},{5,6},{6,7},{7,4},{8,9},{9,10},{10,1... | collective-permute-start | bytes 983048 | tf_op jit(solution)/shard_map/ppermute | solution.py:19
  165.9 6.5 %collective-permute-done.13.refs_0_ = bf16[1280,128]{1,0:T(8,128)(2,1)} collective-permute-done((bf16[1280,128]{1,0:T(8,128)(2,1)}, bf16[1280,128]{1,0:T(8,128)(2,1)}, u32[]{:S(2)}, u32[]{:S(2)}) %collective-permute-start.13) | collective-permute-done | bytes 327712 | tf_op jit(solution)/shard_map/ppermute | solution.py:19
  172.3 12.7 %collective-permute-done.14.refs_1_ = bf16[1280,128]{1,0:T(8,128)(2,1)} collective-permute-done((bf16[1280,128]{1,0:T(8,128)(2,1)}, bf16[1280,128]{1,0:T(8,128)(2,1)}, u32[]{:S(2)}, u32[]{:S(2)}) %collective-permute-start.14) | collective-permute-done | bytes 327712 | tf_op jit(solution)/shard_map/ppermute | solution.py:19
  185.0 3.0 join.8
  188.1 9.8 %back.7 = (f32[32,1280]{1,0:T(8,128)}, f32[32,1280]{1,0:T(8,128)}, f32[32,1280]{1,0:T(8,128)}, f32[32,1280]{1,0:T(8,128)}) custom-call(s32[4]{0:T(128)} %compare_select_fusion.place_ref, bf16[5120,128]{1,0:T(8,128)(2,1)} %all-gather.9.cloned.1.call-done.grads_ref, bf16[1280,5120]{1,0:T(8,128)(2,1)} %bitcast.77), custom_call_target="tpu_custom_call" | custom-call | flops 1677721600 | bytes 13107200 | tf_op jit(solution)/shard_map/back/pallas_call | solution.py:197
  201.1 2.9 collective-permute-done.16.refs_0_
  215.2 4.2 collective-permute-done.21
  219.9 2.7 collective-permute-done.19
  222.6 9.2 %project.8 = (bf16[6,128,1280]{2,1,0:T(8,128)(2,1)S(1)}, f32[1280,128]{1,0:T(8,128)}, bf16[1280,128]{1,0:T(8,128)(2,1)}, bf16[1280,128]{1,0:T(8,128)(2,1)}, bf16[1280,128]{1,0:T(8,128)(2,1)}) fusion(bf16[6,128,1280]{2,1,0:T(8,128)(2,1)S(1)} %get-tuple-element.122, s32[]{:T(128)S(6)} %max.21, s32[11]{0:T(128)S(1)} %concatenate.21, ...), kind=kCustom, calls=%fused_computation.8 | custom fusion | bytes 16712196 | tf_op jit(solution)/shard_map/project/pallas_call | solution.py:113
  231.8 7.6 %collective-permute-start.23 = (bf16[1280,128]{1,0:T(8,128)(2,1)}, bf16[1280,128]{1,0:T(8,128)(2,1)}, u32[]{:S(2)}, u32[]{:S(2)}) collective-permute-start(bf16[1280,128]{1,0:T(8,128)(2,1)} %get-tuple-element.165), channel_id=1, source_target_pairs={{0,1},{1,2},{2,3},{3,0},{4,5},{5,6},{6,7},{7,4},{8,9},{9,10},{10,1... | collective-permute-start | bytes 983048 | tf_op jit(solution)/shard_map/ppermute | solution.py:19
  242.4 9.8 %back.8 = (f32[32,1280]{1,0:T(8,128)}, f32[32,1280]{1,0:T(8,128)}, f32[32,1280]{1,0:T(8,128)}, f32[32,1280]{1,0:T(8,128)}) custom-call(s32[4]{0:T(128)} %compare_select_fusion.place_ref, bf16[5120,128]{1,0:T(8,128)(2,1)} %all-gather.11.cloned.1.call-done.grads_ref, bf16[1280,5120]{1,0:T(8,128)(2,1)} %bitcast.78), custom_call_target="tpu_custom_call" | custom-call | flops 1677721600 | bytes 13107200 | tf_op jit(solution)/shard_map/back/pallas_call | solution.py:197
  262.4 3.0 join.9
  273.3 4.2 broadcast_in_dim.72
  281.3 9.2 %project.7 = (bf16[6,128,1280]{2,1,0:T(8,128)(2,1)S(1)}, f32[1280,128]{1,0:T(8,128)}, bf16[1280,128]{1,0:T(8,128)(2,1)}, bf16[1280,128]{1,0:T(8,128)(2,1)}, bf16[1280,128]{1,0:T(8,128)(2,1)}) fusion(bf16[6,128,1280]{2,1,0:T(8,128)(2,1)S(1)} %get-tuple-element.162, s32[]{:T(128)S(6)} %max.22, s32[11]{0:T(128)S(1)} %concatenate.22, ...), kind=kCustom, calls=%fused_computation.7 | custom fusion | bytes 16712196 | tf_op jit(solution)/shard_map/project/pallas_call | solution.py:113
  290.5 7.5 %collective-permute-start.33 = (bf16[1280,128]{1,0:T(8,128)(2,1)}, bf16[1280,128]{1,0:T(8,128)(2,1)}, u32[]{:S(2)}, u32[]{:S(2)}) collective-permute-start(bf16[1280,128]{1,0:T(8,128)(2,1)} %get-tuple-element.115), channel_id=1, source_target_pairs={{0,1},{1,2},{2,3},{3,0},{4,5},{5,6},{6,7},{7,4},{8,9},{9,10},{10,1... | collective-permute-start | bytes 983048 | tf_op jit(solution)/shard_map/ppermute | solution.py:19
  304.0 14.4 %all-gather.13.cloned.1.call-done.grads_ref = bf16[5120,128]{1,0:T(8,128)(2,1)} async-done(((bf16[1280,128]{1,0:T(8,128)(2,1)}), bf16[5120,128]{1,0:T(8,128)(2,1)}) %all-gather.13.cloned.1.call-update) | async-done | bytes 1310736 | tf_op jit(solution)/shard_map/all_gather | solution.py:298
  318.4 9.8 %back.9 = (f32[32,1280]{1,0:T(8,128)}, f32[32,1280]{1,0:T(8,128)}, f32[32,1280]{1,0:T(8,128)}, f32[32,1280]{1,0:T(8,128)}) custom-call(s32[4]{0:T(128)} %compare_select_fusion.place_ref, bf16[5120,128]{1,0:T(8,128)(2,1)} %all-gather.13.cloned.1.call-done.grads_ref, bf16[1280,5120]{1,0:T(8,128)(2,1)} %bitcast.79), custom_call_target="tpu_custom_call" | custom-call | flops 1677721600 | bytes 13107200 | tf_op jit(solution)/shard_map/back/pallas_call | solution.py:197
  331.3 3.1 join.10
  345.4 4.0 collective-permute-done.41
  349.9 2.5 collective-permute-done.39
  353.1 9.2 %project.6 = (bf16[6,128,1280]{2,1,0:T(8,128)(2,1)S(1)}, f32[1280,128]{1,0:T(8,128)}, bf16[1280,128]{1,0:T(8,128)(2,1)}, bf16[1280,128]{1,0:T(8,128)(2,1)}, bf16[1280,128]{1,0:T(8,128)(2,1)}) fusion(bf16[6,128,1280]{2,1,0:T(8,128)(2,1)S(1)} %get-tuple-element.112, s32[]{:T(128)S(6)} %max.23, s32[11]{0:T(128)S(1)} %concatenate.23, ...), kind=kCustom, calls=%fused_computation.6 | custom fusion | bytes 16712196 | tf_op jit(solution)/shard_map/project/pallas_call | solution.py:113
  362.4 3.7 collective-permute-start.45
  368.6 6.4 %collective-permute-done.43.refs_0_ = bf16[1280,128]{1,0:T(8,128)(2,1)S(1)} collective-permute-done((bf16[1280,128]{1,0:T(8,128)(2,1)}, bf16[1280,128]{1,0:T(8,128)(2,1)S(1)}, u32[]{:S(2)}, u32[]{:S(2)}) %collective-permute-start.43) | collective-permute-done | bytes 327712 | tf_op jit(solution)/shard_map/ppermute | solution.py:19
  375.0 13.0 %collective-permute-done.44.refs_1_ = bf16[1280,128]{1,0:T(8,128)(2,1)S(1)} collective-permute-done((bf16[1280,128]{1,0:T(8,128)(2,1)}, bf16[1280,128]{1,0:T(8,128)(2,1)S(1)}, u32[]{:S(2)}, u32[]{:S(2)}) %collective-permute-start.44) | collective-permute-done | bytes 327712 | tf_op jit(solution)/shard_map/ppermute | solution.py:19
  389.5 3.1 join.11
  395.1 14.0 %second_gradient.1 = f32[5120,1280]{1,0:T(8,128)} custom-call(bf16[5120,512]{1,0:T(8,128)(2,1)} %copy.20.refs_3_.hidden_ref, bf16[6,128,1280]{2,1,0:T(8,128)(2,1)} %copy-done.1), custom_call_target="tpu_custom_call" | custom-call | flops 6710886400 | bytes 26214400 | tf_op jit(solution)/shard_map/second_gradient/pallas_call | solution.py:239
  409.2 9.8 %back.10 = (f32[32,1280]{1,0:T(8,128)}, f32[32,1280]{1,0:T(8,128)}, f32[32,1280]{1,0:T(8,128)}, f32[32,1280]{1,0:T(8,128)}) custom-call(s32[4]{0:T(128)} %compare_select_fusion.place_ref, bf16[5120,128]{1,0:T(8,128)(2,1)} %all-gather.15.cloned.1.call-done.grads_ref, bf16[1280,5120]{1,0:T(8,128)(2,1)} %bitcast.80), custom_call_target="tpu_custom_call" | custom-call | flops 1677721600 | bytes 13107200 | tf_op jit(solution)/shard_map/back/pallas_call | solution.py:197
  422.1 7.7 %all-gather.17.cloned.1.call-done.grads_ref = bf16[5120,128]{1,0:T(8,128)(2,1)} async-done(((bf16[1280,128]{1,0:T(8,128)(2,1)}), bf16[5120,128]{1,0:T(8,128)(2,1)}) %all-gather.17.cloned.1.call-update) | async-done | bytes 1310736 | tf_op jit(solution)/shard_map/all_gather | solution.py:298
  429.8 9.8 %back.11 = (f32[32,1280]{1,0:T(8,128)}, f32[32,1280]{1,0:T(8,128)}, f32[32,1280]{1,0:T(8,128)}, f32[32,1280]{1,0:T(8,128)}) custom-call(s32[4]{0:T(128)} %compare_select_fusion.place_ref, bf16[5120,128]{1,0:T(8,128)(2,1)} %all-gather.17.cloned.1.call-done.grads_ref, bf16[1280,5120]{1,0:T(8,128)(2,1)} %bitcast.81), custom_call_target="tpu_custom_call" | custom-call | flops 1677721600 | bytes 13107200 | tf_op jit(solution)/shard_map/back/pallas_call | solution.py:197
  445.0 14.8 %first_gradient.1 = f32[1280,5120]{1,0:T(8,128)} custom-call(bf16[1280,512]{1,0:T(8,128)(2,1)} %copy.26.inputs_ref, bf16[6,5120,128]{2,1,0:T(8,128)(2,1)} %bitcast_dynamic-update-slice_fusion.grads_ref), custom_call_target="tpu_custom_call" | custom-call | flops 6710886400 | bytes 26214400 | tf_op jit(solution)/shard_map/first_gradient/pallas_call | solution.py:215
  (177 shorter events, 103.2 us)
Async XLA Ops:
  7.2 104.0 %all-gather.7.cloned.1.call-start = ((), (), s32[]{:S(2)}) async-start(), calls=%async_computation | async-start | bytes 1638400 | tf_op jit(solution)/shard_map/all_gather | solution.py:298
  17.7 20.8 %collective-permute-start = (bf16[1280,128]{1,0:T(8,128)(2,1)}, bf16[1280,128]{1,0:T(8,128)(2,1)}, u32[]{:S(2)}, u32[]{:S(2)}) collective-permute-start(bf16[1280,128]{1,0:T(8,128)(2,1)} %get-tuple-element.135), channel_id=1, source_target_pairs={{0,1},{1,2},{2,3},{3,0},{4,5},{5,6},{6,7},{7,4},{8,9},{9,10},{10,1... | collective-permute-start | bytes 983048 | tf_op jit(solution)/shard_map/ppermute | solution.py:19
  20.7 24.2 %collective-permute-start.1 = (bf16[1280,128]{1,0:T(8,128)(2,1)}, bf16[1280,128]{1,0:T(8,128)(2,1)}, u32[]{:S(2)}, u32[]{:S(2)}) collective-permute-start(bf16[1280,128]{1,0:T(8,128)(2,1)} %get-tuple-element.137), channel_id=1, source_target_pairs={{0,2},{1,3},{2,0},{3,1},{4,6},{5,7},{6,4},{7,5},{8,10},{9,11},{10,... | collective-permute-start | bytes 983048 | tf_op jit(solution)/shard_map/ppermute | solution.py:19
  23.3 21.6 %collective-permute-start.2 = (bf16[1280,128]{1,0:T(8,128)(2,1)}, bf16[1280,128]{1,0:T(8,128)(2,1)}, u32[]{:S(2)}, u32[]{:S(2)}) collective-permute-start(bf16[1280,128]{1,0:T(8,128)(2,1)} %get-tuple-element.139), channel_id=1, source_target_pairs={{0,3},{1,0},{2,1},{3,2},{4,7},{5,4},{6,5},{7,6},{8,11},{9,8},{10,9... | collective-permute-start | bytes 983048 | tf_op jit(solution)/shard_map/ppermute | solution.py:19
  48.0 140.1 %all-gather.9.cloned.1.call-start = ((), (), s32[]{:S(2)}) async-start(), calls=%async_computation.1 | async-start | bytes 1638400 | tf_op jit(solution)/shard_map/all_gather | solution.py:298
  57.3 24.3 %collective-permute-start.3 = (bf16[1280,128]{1,0:T(8,128)(2,1)}, bf16[1280,128]{1,0:T(8,128)(2,1)}, u32[]{:S(2)}, u32[]{:S(2)}) collective-permute-start(bf16[1280,128]{1,0:T(8,128)(2,1)} %get-tuple-element.145), channel_id=1, source_target_pairs={{0,1},{1,2},{2,3},{3,0},{4,5},{5,6},{6,7},{7,4},{8,9},{9,10},{10,1... | collective-permute-start | bytes 983048 | tf_op jit(solution)/shard_map/ppermute | solution.py:19
  64.8 39.7 %collective-permute-start.4 = (bf16[1280,128]{1,0:T(8,128)(2,1)}, bf16[1280,128]{1,0:T(8,128)(2,1)}, u32[]{:S(2)}, u32[]{:S(2)}) collective-permute-start(bf16[1280,128]{1,0:T(8,128)(2,1)} %get-tuple-element.147), channel_id=1, source_target_pairs={{0,2},{1,3},{2,0},{3,1},{4,6},{5,7},{6,4},{7,5},{8,10},{9,11},{10,... | collective-permute-start | bytes 983048 | tf_op jit(solution)/shard_map/ppermute | solution.py:19
  66.4 38.1 %collective-permute-start.5 = (bf16[1280,128]{1,0:T(8,128)(2,1)}, bf16[1280,128]{1,0:T(8,128)(2,1)}, u32[]{:S(2)}, u32[]{:S(2)}) collective-permute-start(bf16[1280,128]{1,0:T(8,128)(2,1)} %get-tuple-element.149), channel_id=1, source_target_pairs={{0,3},{1,0},{2,1},{3,2},{4,7},{5,4},{6,5},{7,6},{8,11},{9,8},{10,9... | collective-permute-start | bytes 983048 | tf_op jit(solution)/shard_map/ppermute | solution.py:19
  107.6 134.8 %all-gather.11.cloned.1.call-start = ((), (), s32[]{:S(2)}) async-start(), calls=%async_computation.2 | async-start | bytes 1638400 | tf_op jit(solution)/shard_map/all_gather | solution.py:298
  133.4 9.1 %collective-permute-start.11 = (bf16[32,1280]{1,0:T(8,128)(2,1)}, bf16[32,1280]{1,0:T(8,128)(2,1)S(1)}, u32[]{:S(2)}, u32[]{:S(2)}) collective-permute-start(bf16[32,1280]{1,0:T(8,128)(2,1)} %total.6), channel_id=1, source_target_pairs={{16,8},{20,12},{24,0},{28,4},{17,9},{21,13},{25,1},{29,5},{18,10},... | collective-permute-start | bytes 245768 | tf_op jit(solution)/shard_map/ppermute | solution.py:32
  134.7 8.3 %collective-permute-start.10 = (bf16[32,1280]{1,0:T(8,128)(2,1)}, bf16[32,1280]{1,0:T(8,128)(2,1)S(1)}, u32[]{:S(2)}, u32[]{:S(2)}) collective-permute-start(bf16[32,1280]{1,0:T(8,128)(2,1)} %total.6), channel_id=1, source_target_pairs={{16,4},{20,8},{24,12},{28,0},{17,5},{21,9},{25,13},{29,1},{18,6},{... | collective-permute-start | bytes 245768 | tf_op jit(solution)/shard_map/ppermute | solution.py:32
  136.0 9.7 %collective-permute-start.9 = (bf16[32,1280]{1,0:T(8,128)(2,1)}, bf16[32,1280]{1,0:T(8,128)(2,1)}, u32[]{:S(2)}, u32[]{:S(2)}) collective-permute-start(bf16[32,1280]{1,0:T(8,128)(2,1)} %total.6), channel_id=1, source_target_pairs={{16,0},{20,4},{24,8},{28,12},{17,1},{21,5},{25,9},{29,13},{18,2},{... | collective-permute-start | bytes 245768 | tf_op jit(solution)/shard_map/ppermute | solution.py:32
  154.9 17.5 %collective-permute-start.13 = (bf16[1280,128]{1,0:T(8,128)(2,1)}, bf16[1280,128]{1,0:T(8,128)(2,1)}, u32[]{:S(2)}, u32[]{:S(2)}) collective-permute-start(bf16[1280,128]{1,0:T(8,128)(2,1)} %get-tuple-element.125), channel_id=1, source_target_pairs={{0,1},{1,2},{2,3},{3,0},{4,5},{5,6},{6,7},{7,4},{8,9},{9,10},{10,1... | collective-permute-start | bytes 983048 | tf_op jit(solution)/shard_map/ppermute | solution.py:19
  162.9 22.1 %collective-permute-start.14 = (bf16[1280,128]{1,0:T(8,128)(2,1)}, bf16[1280,128]{1,0:T(8,128)(2,1)}, u32[]{:S(2)}, u32[]{:S(2)}) collective-permute-start(bf16[1280,128]{1,0:T(8,128)(2,1)} %get-tuple-element.127), channel_id=1, source_target_pairs={{0,2},{1,3},{2,0},{3,1},{4,6},{5,7},{6,4},{7,5},{8,10},{9,11},{10,... | collective-permute-start | bytes 983048 | tf_op jit(solution)/shard_map/ppermute | solution.py:19
  163.9 21.1 %collective-permute-start.15 = (bf16[1280,128]{1,0:T(8,128)(2,1)}, bf16[1280,128]{1,0:T(8,128)(2,1)}, u32[]{:S(2)}, u32[]{:S(2)}) collective-permute-start(bf16[1280,128]{1,0:T(8,128)(2,1)} %get-tuple-element.129), channel_id=1, source_target_pairs={{0,3},{1,0},{2,1},{3,2},{4,7},{5,4},{6,5},{7,6},{8,11},{9,8},{10,9... | collective-permute-start | bytes 983048 | tf_op jit(solution)/shard_map/ppermute | solution.py:19
  188.0 130.3 %all-gather.13.cloned.1.call-start = ((), (), s32[]{:S(2)}) async-start(), calls=%async_computation.3 | async-start | bytes 1638400 | tf_op jit(solution)/shard_map/all_gather | solution.py:298
  199.7 7.8 %collective-permute-start.18 = (f32[32,1280]{1,0:T(8,128)}, f32[32,1280]{1,0:T(8,128)}, u32[]{:S(2)}, u32[]{:S(2)}) collective-permute-start(f32[32,1280]{1,0:T(8,128)} %get-tuple-element.76), channel_id=1, source_target_pairs={{0,12},{4,0},{8,4},{12,8},{1,13},{5,1},{9,5},{13,9},{2,14},{6,2},{... | collective-permute-start | bytes 491528 | tf_op jit(solution)/shard_map/ppermute | solution.py:19
  210.6 8.9 %collective-permute-start.21 = (bf16[32,1280]{1,0:T(8,128)(2,1)}, bf16[32,1280]{1,0:T(8,128)(2,1)S(1)}, u32[]{:S(2)}, u32[]{:S(2)}) collective-permute-start(bf16[32,1280]{1,0:T(8,128)(2,1)} %total.7), channel_id=1, source_target_pairs={{16,8},{20,12},{24,0},{28,4},{17,9},{21,13},{25,1},{29,5},{18,10},... | collective-permute-start | bytes 245768 | tf_op jit(solution)/shard_map/ppermute | solution.py:32
  211.9 8.1 %collective-permute-start.20 = (bf16[32,1280]{1,0:T(8,128)(2,1)}, bf16[32,1280]{1,0:T(8,128)(2,1)S(1)}, u32[]{:S(2)}, u32[]{:S(2)}) collective-permute-start(bf16[32,1280]{1,0:T(8,128)(2,1)} %total.7), channel_id=1, source_target_pairs={{16,4},{20,8},{24,12},{28,0},{17,5},{21,9},{25,13},{29,1},{18,6},{... | collective-permute-start | bytes 245768 | tf_op jit(solution)/shard_map/ppermute | solution.py:32
  213.2 9.4 %collective-permute-start.19 = (bf16[32,1280]{1,0:T(8,128)(2,1)}, bf16[32,1280]{1,0:T(8,128)(2,1)}, u32[]{:S(2)}, u32[]{:S(2)}) collective-permute-start(bf16[32,1280]{1,0:T(8,128)(2,1)} %total.7), channel_id=1, source_target_pairs={{16,0},{20,4},{24,8},{28,12},{17,1},{21,5},{25,9},{29,13},{18,2},{... | collective-permute-start | bytes 245768 | tf_op jit(solution)/shard_map/ppermute | solution.py:32
  231.8 22.1 %collective-permute-start.23 = (bf16[1280,128]{1,0:T(8,128)(2,1)}, bf16[1280,128]{1,0:T(8,128)(2,1)}, u32[]{:S(2)}, u32[]{:S(2)}) collective-permute-start(bf16[1280,128]{1,0:T(8,128)(2,1)} %get-tuple-element.165), channel_id=1, source_target_pairs={{0,1},{1,2},{2,3},{3,0},{4,5},{5,6},{6,7},{7,4},{8,9},{9,10},{10,1... | collective-permute-start | bytes 983048 | tf_op jit(solution)/shard_map/ppermute | solution.py:19
  240.0 22.4 %collective-permute-start.24 = (bf16[1280,128]{1,0:T(8,128)(2,1)}, bf16[1280,128]{1,0:T(8,128)(2,1)}, u32[]{:S(2)}, u32[]{:S(2)}) collective-permute-start(bf16[1280,128]{1,0:T(8,128)(2,1)} %get-tuple-element.167), channel_id=1, source_target_pairs={{0,2},{1,3},{2,0},{3,1},{4,6},{5,7},{6,4},{7,5},{8,10},{9,11},{10,... | collective-permute-start | bytes 983048 | tf_op jit(solution)/shard_map/ppermute | solution.py:19
  241.9 20.5 %collective-permute-start.25 = (bf16[1280,128]{1,0:T(8,128)(2,1)}, bf16[1280,128]{1,0:T(8,128)(2,1)}, u32[]{:S(2)}, u32[]{:S(2)}) collective-permute-start(bf16[1280,128]{1,0:T(8,128)(2,1)} %get-tuple-element.169), channel_id=1, source_target_pairs={{0,3},{1,0},{2,1},{3,2},{4,7},{5,4},{6,5},{7,6},{8,11},{9,8},{10,9... | collective-permute-start | bytes 983048 | tf_op jit(solution)/shard_map/ppermute | solution.py:19
  252.2 13.3 %collective-permute-start.26 = (f32[32,1280]{1,0:T(8,128)}, f32[32,1280]{1,0:T(8,128)S(1)}, u32[]{:S(2)}, u32[]{:S(2)}) collective-permute-start(f32[32,1280]{1,0:T(8,128)} %get-tuple-element.82), channel_id=1, source_target_pairs={{0,4},{4,8},{8,12},{12,0},{1,5},{5,9},{9,13},{13,1},{2,6},{6,10},{... | collective-permute-start | bytes 491528 | tf_op jit(solution)/shard_map/ppermute | solution.py:19
  252.2 13.3 %collective-permute-start.27 = (f32[32,1280]{1,0:T(8,128)}, f32[32,1280]{1,0:T(8,128)}, u32[]{:S(2)}, u32[]{:S(2)}) collective-permute-start(f32[32,1280]{1,0:T(8,128)} %get-tuple-element.83), channel_id=1, source_target_pairs={{0,8},{4,12},{8,0},{12,4},{1,9},{5,13},{9,1},{13,5},{2,10},{6,14},... | collective-permute-start | bytes 491528 | tf_op jit(solution)/shard_map/ppermute | solution.py:19
  253.9 11.6 %collective-permute-start.28 = (f32[32,1280]{1,0:T(8,128)}, f32[32,1280]{1,0:T(8,128)}, u32[]{:S(2)}, u32[]{:S(2)}) collective-permute-start(f32[32,1280]{1,0:T(8,128)} %get-tuple-element.84), channel_id=1, source_target_pairs={{0,12},{4,0},{8,4},{12,8},{1,13},{5,1},{9,5},{13,9},{2,14},{6,2},{... | collective-permute-start | bytes 491528 | tf_op jit(solution)/shard_map/ppermute | solution.py:19
  265.4 143.8 %all-gather.15.cloned.1.call-start = ((), (), s32[]{:S(2)}) async-start(), calls=%async_computation.4 | async-start | bytes 1638400 | tf_op jit(solution)/shard_map/all_gather | solution.py:298
  267.9 10.7 %collective-permute-start.32 = (bf16[32,1280]{1,0:T(8,128)(2,1)}, bf16[32,1280]{1,0:T(8,128)(2,1)S(1)}, u32[]{:S(2)}, u32[]{:S(2)}) collective-permute-start(bf16[32,1280]{1,0:T(8,128)(2,1)} %total.8), channel_id=1, source_target_pairs={{16,12},{20,0},{24,4},{28,8},{17,13},{21,1},{25,5},{29,9},{18,14},... | collective-permute-start | bytes 245768 | tf_op jit(solution)/shard_map/ppermute | solution.py:32
  269.4 9.2 %collective-permute-start.31 = (bf16[32,1280]{1,0:T(8,128)(2,1)}, bf16[32,1280]{1,0:T(8,128)(2,1)S(1)}, u32[]{:S(2)}, u32[]{:S(2)}) collective-permute-start(bf16[32,1280]{1,0:T(8,128)(2,1)} %total.8), channel_id=1, source_target_pairs={{16,8},{20,12},{24,0},{28,4},{17,9},{21,13},{25,1},{29,5},{18,10},... | collective-permute-start | bytes 245768 | tf_op jit(solution)/shard_map/ppermute | solution.py:32
  270.7 7.9 %collective-permute-start.30 = (bf16[32,1280]{1,0:T(8,128)(2,1)}, bf16[32,1280]{1,0:T(8,128)(2,1)S(1)}, u32[]{:S(2)}, u32[]{:S(2)}) collective-permute-start(bf16[32,1280]{1,0:T(8,128)(2,1)} %total.8), channel_id=1, source_target_pairs={{16,4},{20,8},{24,12},{28,0},{17,5},{21,9},{25,13},{29,1},{18,6},{... | collective-permute-start | bytes 245768 | tf_op jit(solution)/shard_map/ppermute | solution.py:32
  272.0 8.6 %collective-permute-start.29 = (bf16[32,1280]{1,0:T(8,128)(2,1)}, bf16[32,1280]{1,0:T(8,128)(2,1)S(1)}, u32[]{:S(2)}, u32[]{:S(2)}) collective-permute-start(bf16[32,1280]{1,0:T(8,128)(2,1)} %total.8), channel_id=1, source_target_pairs={{16,0},{20,4},{24,8},{28,12},{17,1},{21,5},{25,9},{29,13},{18,2},{... | collective-permute-start | bytes 245768 | tf_op jit(solution)/shard_map/ppermute | solution.py:32
  290.5 39.4 %collective-permute-start.33 = (bf16[1280,128]{1,0:T(8,128)(2,1)}, bf16[1280,128]{1,0:T(8,128)(2,1)}, u32[]{:S(2)}, u32[]{:S(2)}) collective-permute-start(bf16[1280,128]{1,0:T(8,128)(2,1)} %get-tuple-element.115), channel_id=1, source_target_pairs={{0,1},{1,2},{2,3},{3,0},{4,5},{5,6},{6,7},{7,4},{8,9},{9,10},{10,1... | collective-permute-start | bytes 983048 | tf_op jit(solution)/shard_map/ppermute | solution.py:19
  298.0 33.3 %collective-permute-start.34 = (bf16[1280,128]{1,0:T(8,128)(2,1)}, bf16[1280,128]{1,0:T(8,128)(2,1)}, u32[]{:S(2)}, u32[]{:S(2)}) collective-permute-start(bf16[1280,128]{1,0:T(8,128)(2,1)} %get-tuple-element.117), channel_id=1, source_target_pairs={{0,2},{1,3},{2,0},{3,1},{4,6},{5,7},{6,4},{7,5},{8,10},{9,11},{10,... | collective-permute-start | bytes 983048 | tf_op jit(solution)/shard_map/ppermute | solution.py:19
  299.2 32.1 %collective-permute-start.35 = (bf16[1280,128]{1,0:T(8,128)(2,1)}, bf16[1280,128]{1,0:T(8,128)(2,1)}, u32[]{:S(2)}, u32[]{:S(2)}) collective-permute-start(bf16[1280,128]{1,0:T(8,128)(2,1)} %get-tuple-element.119), channel_id=1, source_target_pairs={{0,3},{1,0},{2,1},{3,2},{4,7},{5,4},{6,5},{7,6},{8,11},{9,8},{10,9... | collective-permute-start | bytes 983048 | tf_op jit(solution)/shard_map/ppermute | solution.py:19
  329.9 7.8 %collective-permute-start.38 = (f32[32,1280]{1,0:T(8,128)}, f32[32,1280]{1,0:T(8,128)}, u32[]{:S(2)}, u32[]{:S(2)}) collective-permute-start(f32[32,1280]{1,0:T(8,128)} %get-tuple-element.92), channel_id=1, source_target_pairs={{0,12},{4,0},{8,4},{12,8},{1,13},{5,1},{9,5},{13,9},{2,14},{6,2},{... | collective-permute-start | bytes 491528 | tf_op jit(solution)/shard_map/ppermute | solution.py:19
  334.5 95.3 %all-gather.17.cloned.1.call-start = ((), (), s32[]{:S(2)}) async-start(), calls=%async_computation.5 | async-start | bytes 1638400 | tf_op jit(solution)/shard_map/all_gather | solution.py:298
  340.8 8.7 %collective-permute-start.41 = (bf16[32,1280]{1,0:T(8,128)(2,1)}, bf16[32,1280]{1,0:T(8,128)(2,1)S(1)}, u32[]{:S(2)}, u32[]{:S(2)}) collective-permute-start(bf16[32,1280]{1,0:T(8,128)(2,1)} %total.9), channel_id=1, source_target_pairs={{16,8},{20,12},{24,0},{28,4},{17,9},{21,13},{25,1},{29,5},{18,10},... | collective-permute-start | bytes 245768 | tf_op jit(solution)/shard_map/ppermute | solution.py:32
  342.1 7.9 %collective-permute-start.40 = (bf16[32,1280]{1,0:T(8,128)(2,1)}, bf16[32,1280]{1,0:T(8,128)(2,1)S(1)}, u32[]{:S(2)}, u32[]{:S(2)}) collective-permute-start(bf16[32,1280]{1,0:T(8,128)(2,1)} %total.9), channel_id=1, source_target_pairs={{16,4},{20,8},{24,12},{28,0},{17,5},{21,9},{25,13},{29,1},{18,6},{... | collective-permute-start | bytes 245768 | tf_op jit(solution)/shard_map/ppermute | solution.py:32
  343.4 9.1 %collective-permute-start.39 = (bf16[32,1280]{1,0:T(8,128)(2,1)}, bf16[32,1280]{1,0:T(8,128)(2,1)S(1)}, u32[]{:S(2)}, u32[]{:S(2)}) collective-permute-start(bf16[32,1280]{1,0:T(8,128)(2,1)} %total.9), channel_id=1, source_target_pairs={{16,0},{20,4},{24,8},{28,12},{17,1},{21,5},{25,9},{29,13},{18,2},{... | collective-permute-start | bytes 245768 | tf_op jit(solution)/shard_map/ppermute | solution.py:32
  362.4 12.7 %collective-permute-start.43 = (bf16[1280,128]{1,0:T(8,128)(2,1)}, bf16[1280,128]{1,0:T(8,128)(2,1)S(1)}, u32[]{:S(2)}, u32[]{:S(2)}) collective-permute-start(bf16[1280,128]{1,0:T(8,128)(2,1)} %get-tuple-element.155), channel_id=1, source_target_pairs={{0,1},{1,2},{2,3},{3,0},{4,5},{5,6},{6,7},{7,4},{8,9},{9,10},{10,1... | collective-permute-start | bytes 983048 | tf_op jit(solution)/shard_map/ppermute | solution.py:19
  362.4 25.7 %collective-permute-start.44 = (bf16[1280,128]{1,0:T(8,128)(2,1)}, bf16[1280,128]{1,0:T(8,128)(2,1)S(1)}, u32[]{:S(2)}, u32[]{:S(2)}) collective-permute-start(bf16[1280,128]{1,0:T(8,128)(2,1)} %get-tuple-element.157), channel_id=1, source_target_pairs={{0,2},{1,3},{2,0},{3,1},{4,6},{5,7},{6,4},{7,5},{8,10},{9,11},{10,... | collective-permute-start | bytes 983048 | tf_op jit(solution)/shard_map/ppermute | solution.py:19
  362.4 25.6 %collective-permute-start.45 = (bf16[1280,128]{1,0:T(8,128)(2,1)}, bf16[1280,128]{1,0:T(8,128)(2,1)S(1)}, u32[]{:S(2)}, u32[]{:S(2)}) collective-permute-start(bf16[1280,128]{1,0:T(8,128)(2,1)} %get-tuple-element.159), channel_id=1, source_target_pairs={{0,3},{1,0},{2,1},{3,2},{4,7},{5,4},{6,5},{7,6},{8,11},{9,8},{10,9... | collective-permute-start | bytes 983048 | tf_op jit(solution)/shard_map/ppermute | solution.py:19
  419.0 24.6 %collective-permute-start.46 = (f32[32,1280]{1,0:T(8,128)}, f32[32,1280]{1,0:T(8,128)S(1)}, u32[]{:S(2)}, u32[]{:S(2)}) collective-permute-start(f32[32,1280]{1,0:T(8,128)} %get-tuple-element.104), channel_id=1, source_target_pairs={{0,4},{4,8},{8,12},{12,0},{1,5},{5,9},{9,13},{13,1},{2,6},{6,10},{... | collective-permute-start | bytes 491528 | tf_op jit(solution)/shard_map/ppermute | solution.py:19
  419.0 40.8 %collective-permute-start.47 = (f32[32,1280]{1,0:T(8,128)}, f32[32,1280]{1,0:T(8,128)S(1)}, u32[]{:S(2)}, u32[]{:S(2)}) collective-permute-start(f32[32,1280]{1,0:T(8,128)} %get-tuple-element.105), channel_id=1, source_target_pairs={{0,8},{4,12},{8,0},{12,4},{1,9},{5,13},{9,1},{13,5},{2,10},{6,14},... | collective-permute-start | bytes 491528 | tf_op jit(solution)/shard_map/ppermute | solution.py:19
  420.7 39.2 %collective-permute-start.48 = (f32[32,1280]{1,0:T(8,128)}, f32[32,1280]{1,0:T(8,128)S(1)}, u32[]{:S(2)}, u32[]{:S(2)}) collective-permute-start(f32[32,1280]{1,0:T(8,128)} %get-tuple-element.106), channel_id=1, source_target_pairs={{0,12},{4,0},{8,4},{12,8},{1,13},{5,1},{9,5},{13,9},{2,14},{6,2},{... | collective-permute-start | bytes 491528 | tf_op jit(solution)/shard_map/ppermute | solution.py:19
  439.6 20.9 %collective-permute-start.49 = (f32[32,1280]{1,0:T(8,128)}, f32[32,1280]{1,0:T(8,128)S(1)}, u32[]{:S(2)}, u32[]{:S(2)}) collective-permute-start(f32[32,1280]{1,0:T(8,128)} %get-tuple-element.108), channel_id=1, source_target_pairs={{0,4},{4,8},{8,12},{12,0},{1,5},{5,9},{9,13},{13,1},{2,6},{6,10},{... | collective-permute-start | bytes 491528 | tf_op jit(solution)/shard_map/ppermute | solution.py:19
  439.7 20.9 %collective-permute-start.50 = (f32[32,1280]{1,0:T(8,128)}, f32[32,1280]{1,0:T(8,128)S(1)}, u32[]{:S(2)}, u32[]{:S(2)}) collective-permute-start(f32[32,1280]{1,0:T(8,128)} %get-tuple-element.109), channel_id=1, source_target_pairs={{0,8},{4,12},{8,0},{12,4},{1,9},{5,13},{9,1},{13,5},{2,10},{6,14},... | collective-permute-start | bytes 491528 | tf_op jit(solution)/shard_map/ppermute | solution.py:19
  443.6 16.9 %collective-permute-start.51 = (f32[32,1280]{1,0:T(8,128)S(1)}, f32[32,1280]{1,0:T(8,128)S(1)}, u32[]{:S(2)}, u32[]{:S(2)}) collective-permute-start(f32[32,1280]{1,0:T(8,128)S(1)} %copy-done.21), channel_id=1, source_target_pairs={{0,12},{4,0},{8,4},{12,8},{1,13},{5,1},{9,5},{13,9},{2,14},{6,2},{... | collective-permute-start | bytes 491528 | tf_op jit(solution)/shard_map/ppermute | solution.py:19
  (32 other events, 216.4 us)
Sparse Core Ops, SparseCore 0:
  48.1 62.9 all-gather.6
  112.7 36.6 all-gather.8
  188.2 37.9 all-gather.10
  265.5 52.8 all-gather.12
  334.6 31.0 all-gather.14
  392.8 36.9 all-gather.16

commit v2 on v1

v2 whole, which is shorter than its diff:
```python
import functools

import jax
import jax.numpy as jnp
from jax import lax
from jax.experimental import pallas as pl
from jax.experimental.pallas import tpu as pltpu
from jax.sharding import PartitionSpec as P

SUB_CHUNKS = 2
LAG = 2
PROJECT_PIECE = 640
REST_PIECE = 1280
BACK_PIECE = 640
HID_SENT_AS = jnp.float32


def exchange(blocks, axis):
    count = lax.axis_size(axis)
    arrived = []
    for shift in range(1, count):
        pairs = [(i, (i + shift) % count) for i in range(count)]
        arrived.append(lax.ppermute(blocks[shift - 1], axis, pairs))
    return arrived


def swap(block, axis, bit):
    pairs = [(i, i ^ bit) for i in range(lax.axis_size(axis))]
    return lax.ppermute(block, axis, pairs)


def bits_of(count):
    assert count & (count - 1) == 0, count
    return [1 << k for k in range(count.bit_length() - 1)]


def mask_order(count):
    odd = sorted(range(1, count, 2), reverse=True)
    return odd + sorted(range(0, count, 2), reverse=True)


def reduce_blocks(blocks, axis):
    count = lax.axis_size(axis)
    held = dict(blocks)
    mine = []
    for bit in bits_of(count):
        arrived = {}
        for m in mask_order(count):
            if m in held and m & bit:
                arrived[m ^ bit] = swap(held.pop(m), axis, bit)
        mine.append(arrived.pop(0))
        for m, block in arrived.items():
            if isinstance(held[m], list):
                held[m] = held[m] + [block]
            else:
                held[m] = [held[m], block]
        for m in list(held):
            if m and m & (2 * bit) and isinstance(held[m], list):
                held[m] = rounded_total(held[m][0], held[m][1:])
    return held[0], mine


def gather_blocks(block, axis):
    held = {0: block}
    for bit in reversed(bits_of(lax.axis_size(axis))):
        held.update({m ^ bit: swap(b, axis, bit) for m, b in held.items()})
    return held


def hand_down(share):
    sections, hids = lax.axis_size("section"), lax.axis_size("hid")
    arrived = []
    for shift in range(hids):
        pairs = [
            (s * hids + h, (s - 1) * hids + (h + shift) % hids)
            for s in range(1, sections)
            for h in range(hids)
        ]
        arrived.append(lax.ppermute(share, ("section", "hid"), pairs))
    return arrived


def estimate(flops, moved):
    return pl.CostEstimate(flops=flops, bytes_accessed=moved, transcendentals=0)


def dot(left, right, left_dim, right_dim):
    return lax.dot_general(
        left, right, (((left_dim,), (right_dim,)), ((), ())), preferred_element_type=jnp.float32
    )


def piece_of(size, wanted):
    fits = [p for p in range(128, wanted + 1, 128) if size % p == 0]
    return fits[-1] if fits else size


class Places:
    def __init__(self, wids, hids):
        self.section, self.wid, self.ordered = 0, 1, 2
        self.by_mask = self.ordered + wids
        self.senders = self.by_mask + wids
        self.row_blocks = self.senders + hids
        self.periods = self.row_blocks + hids

    def period(self, number):
        return self.periods + 4 * number


def project_kernel(hids, given_at, senders_at, table_ref, given_ref, *refs):
    received_refs, weight_ref, (block_ref, turned_ref, incoming_ref) = (
        refs[:hids],
        refs[hids],
        refs[hids + 1 :],
    )
    rows, width = incoming_ref.shape
    sub = rows // hids

    @pl.when(pl.program_id(0) == 0)
    def _():
        @pl.when(table_ref[given_at] == 1)
        def _():
            incoming_ref[...] = given_ref[...].reshape(rows, width)

        @pl.when(table_ref[given_at] != 1)
        def _():
            for k in range(hids):
                start = pl.multiple_of(table_ref[senders_at + k] * sub, sub)
                incoming_ref[pl.ds(start, sub), :] = received_refs[k][...]

        turned_ref[...] = incoming_ref[...].T

    block_ref[...] = dot(weight_ref[...], turned_ref[...], 1, 0).astype(block_ref.dtype)


def project(table, places, period, given_parts, received, weight, count):
    hidden, width = weight.shape
    hids, _, sub = given_parts.shape[1:4]
    rows = hids * sub
    columns = hidden // count
    piece = piece_of(columns, PROJECT_PIECE)
    pieces = columns // piece
    at = places.period(period)
    grid_spec = pltpu.PrefetchScalarGridSpec(
        num_scalar_prefetch=1,
        grid=(pieces,),
        in_specs=[
            pl.BlockSpec((1, hids, 1, sub, width), lambda c, s: (s[at + 1], 0, s[at + 2], 0, 0)),
            *[pl.BlockSpec((sub, width), lambda c, s: (0, 0)) for _ in range(hids)],
            pl.BlockSpec((piece, width), lambda c, s: (s[places.ordered] * pieces + c, 0)),
        ],
        out_specs=[
            pl.BlockSpec((piece, rows), lambda c, s: (c, 0)),
            pl.BlockSpec((width, rows), lambda c, s: (0, 0)),
            pl.BlockSpec((rows, width), lambda c, s: (0, 0)),
        ],
    )
    return pl.pallas_call(
        functools.partial(project_kernel, hids, at, places.senders),
        grid_spec=grid_spec,
        out_shape=[
            jax.ShapeDtypeStruct((columns, rows), jnp.bfloat16),
            jax.ShapeDtypeStruct((width, rows), jnp.bfloat16),
            jax.ShapeDtypeStruct((rows, width), jnp.bfloat16),
        ],
        cost_estimate=estimate(2 * rows * width * columns, 2 * width * columns),
        name="project",
    )(table, given_parts, *received, weight)


def rest_kernel(table_ref, turned_ref, weight_ref, *out_refs):
    step = pl.program_id(0)
    block = dot(weight_ref[...], turned_ref[...], 1, 0)
    for k, ref in enumerate(out_refs):

        @pl.when(step == k)
        def _(ref=ref):
            ref[...] = block.astype(ref.dtype)


def rest(table, places, turned, weight, count):
    hidden, width = weight.shape
    rows = turned.shape[1]
    columns = hidden // count
    piece = piece_of(columns, REST_PIECE)
    pieces = columns // piece
    masks = mask_order(count)[1:]

    def block_at(own_step):
        def index(k, c, s):
            return (jnp.where(k == own_step, c, jnp.where(k < own_step, 0, pieces - 1)), 0)

        return pl.BlockSpec((piece, rows), index)

    grid_spec = pltpu.PrefetchScalarGridSpec(
        num_scalar_prefetch=1,
        grid=(count - 1, pieces),
        in_specs=[
            pl.BlockSpec((width, rows), lambda k, c, s: (0, 0)),
            pl.BlockSpec((piece, width), lambda k, c, s: (s[places.ordered + 1 + k] * pieces + c, 0)),
        ],
        out_specs=[block_at(k) for k in range(count - 1)],
    )
    out = pl.pallas_call(
        rest_kernel,
        grid_spec=grid_spec,
        out_shape=[
            jax.ShapeDtypeStruct((columns, rows), jnp.bfloat16 if m % 2 else jnp.float32)
            for m in masks
        ],
        cost_estimate=estimate(2 * rows * width * (hidden - columns), 2 * width * (hidden - columns)),
        name="rest",
    )(table, turned, weight)
    return dict(zip(masks, out))


def join_kernel(table_ref, own_ref, *refs):
    arrived_refs, (hidden_ref, out_ref) = refs[:-2], refs[-2:]
    total = own_ref[...]
    for ref in arrived_refs:
        total += ref[...].astype(jnp.float32)
    out_ref[...] = jnp.where(hidden_ref[...] > 0, total, jnp.float32(0.0)).astype(out_ref.dtype)


def join(table, places, period, own, arrived, hidden_t):
    columns, rows = own.shape
    piece = piece_of(columns, 640)
    pieces = columns // piece
    chunk_at = places.period(period) + 3
    here = pl.BlockSpec((piece, rows), lambda n, s: (n, 0))
    grid_spec = pltpu.PrefetchScalarGridSpec(
        num_scalar_prefetch=1,
        grid=(pieces,),
        in_specs=[here]
        + [here for _ in arrived]
        + [pl.BlockSpec((piece, rows), lambda n, s: (s[places.wid] * pieces + n, s[chunk_at]))],
        out_specs=here,
    )
    return pl.pallas_call(
        join_kernel,
        grid_spec=grid_spec,
        out_shape=jax.ShapeDtypeStruct(own.shape, jnp.bfloat16),
        cost_estimate=estimate(5 * own.size, 14 * own.size),
        name="join",
    )(table, own, *arrived, hidden_t)


def rounded_total(own, arrived):
    total = own
    for block in arrived:
        total = total + block.astype(jnp.float32)
    return total.astype(jnp.bfloat16)


def back_kernel(count, hids, places, table_ref, *refs):
    block_refs, weight_ref, refs = refs[:count], refs[count], refs[count + 1 :]
    out_refs, (grads_ref, piece_ref) = refs[:hids], refs[hids:]
    sub = out_refs[0].shape[0]
    columns = block_refs[0].shape[0]

    @pl.when(pl.program_id(0) == 0)
    def _():
        for m in range(count):
            start = pl.multiple_of(table_ref[places.by_mask + m] * columns, columns)
            grads_ref[pl.ds(start, columns), :] = block_refs[m][...]

    piece_ref[...] = dot(weight_ref[...], grads_ref[...], 1, 0).T
    for k in range(hids):
        start = pl.multiple_of(table_ref[places.row_blocks + k] * sub, sub)
        out_refs[k][...] = piece_ref[pl.ds(start, sub), :].astype(out_refs[k].dtype)


def back(table, places, blocks, weight, hids):
    columns, rows = blocks[0].shape
    count = len(blocks)
    width, hidden = weight.shape
    sub = rows // hids
    piece = piece_of(width, BACK_PIECE)
    grid_spec = pltpu.PrefetchScalarGridSpec(
        num_scalar_prefetch=1,
        grid=(width // piece,),
        in_specs=[
            *[pl.BlockSpec((columns, rows), lambda n, s: (0, 0)) for _ in range(count)],
            pl.BlockSpec((piece, hidden), lambda n, s: (n, 0)),
        ],
        out_specs=[
            *[pl.BlockSpec((sub, piece), lambda n, s: (0, n)) for _ in range(hids)],
            pl.BlockSpec((hidden, rows), lambda n, s: (0, 0)),
        ],
        scratch_shapes=[pltpu.VMEM((rows, piece), jnp.float32)],
    )
    out = pl.pallas_call(
        functools.partial(back_kernel, count, hids, places),
        grid_spec=grid_spec,
        out_shape=[
            *[jax.ShapeDtypeStruct((sub, width), HID_SENT_AS) for _ in range(hids - 1)],
            jax.ShapeDtypeStruct((sub, width), jnp.float32),
            jax.ShapeDtypeStruct((hidden, rows), jnp.bfloat16),
        ],
        cost_estimate=estimate(2 * rows * width * hidden, 2 * width * hidden),
        name="back",
    )(table, *[blocks[m] for m in range(count)], weight)
    return out[:hids], out[hids]


def pick(place_ref, candidates, write):
    for c, by_section in enumerate(candidates):
        for s, ref in enumerate(by_section):

            @pl.when(place_ref[0] == s)
            def _(c=c, ref=ref):
                write(c, ref)


def grouped(refs, sections):
    return [refs[i : i + sections] for i in range(0, len(refs), sections)]


def first_kernel(sections, place_ref, inputs_ref, *refs):
    candidates, (out_ref, grads_ref) = grouped(refs[:-2], sections), refs[-2:]

    def write(c, ref):
        rows = ref.shape[1]
        grads_ref[:, c * rows : (c + 1) * rows] = ref[...]

    pick(place_ref, candidates, write)
    out_ref[...] = dot(inputs_ref[...], grads_ref[...], 1, 1)


def first_gradient(place, inputs_t, candidates):
    width, rows = inputs_t.shape
    sections = len(candidates[0])
    hidden, chunk_rows = candidates[0][0].shape
    piece = piece_of(hidden, 640)

    def only_on(section):
        return pl.BlockSpec((piece, chunk_rows), lambda n, s: (jnp.where(s[0] == section, n, 0), 0))

    grid_spec = pltpu.PrefetchScalarGridSpec(
        num_scalar_prefetch=1,
        grid=(hidden // piece,),
        in_specs=[pl.BlockSpec((width, rows), lambda n, s: (0, 0))]
        + [only_on(s) for _ in candidates for s in range(sections)],
        out_specs=pl.BlockSpec((width, piece), lambda n, s: (0, n)),
        scratch_shapes=[pltpu.VMEM((piece, rows), jnp.bfloat16)],
    )
    return pl.pallas_call(
        functools.partial(first_kernel, sections),
        grid_spec=grid_spec,
        out_shape=jax.ShapeDtypeStruct((width, hidden), jnp.float32),
        cost_estimate=estimate(2 * rows * width * hidden, 4 * width * hidden),
        name="first_gradient",
    )(place, inputs_t, *[a for by_section in candidates for a in by_section])


def second_kernel(sections, place_ref, hidden_ref, *refs):
    candidates, (out_ref, incoming_ref) = grouped(refs[:-2], sections), refs[-2:]

    def write(c, ref):
        rows = ref.shape[0]
        incoming_ref[c * rows : (c + 1) * rows, :] = ref[...]

    @pl.when(pl.program_id(0) == 0)
    def _():
        pick(place_ref, candidates, write)

    active = jnp.maximum(hidden_ref[...], 0)
    out_ref[...] = dot(active, incoming_ref[...], 1, 0)


def second_gradient(place, hidden_t, candidates):
    hidden, rows = hidden_t.shape
    sections = len(candidates[0])
    chunk_rows, width = candidates[0][0].shape
    piece = piece_of(hidden, 640)
    whole = pl.BlockSpec((chunk_rows, width), lambda n, s: (0, 0))
    grid_spec = pltpu.PrefetchScalarGridSpec(
        num_scalar_prefetch=1,
        grid=(hidden // piece,),
        in_specs=[pl.BlockSpec((piece, rows), lambda n, s: (n, 0))]
        + [whole for _ in candidates for _ in range(sections)],
        out_specs=pl.BlockSpec((piece, width), lambda n, s: (n, 0)),
        scratch_shapes=[pltpu.VMEM((rows, width), jnp.bfloat16)],
    )
    return pl.pallas_call(
        functools.partial(second_kernel, sections),
        grid_spec=grid_spec,
        out_shape=jax.ShapeDtypeStruct((hidden, width), jnp.float32),
        cost_estimate=estimate(2 * rows * width * hidden, 4 * width * hidden),
        name="second_gradient",
    )(place, hidden_t, *[a for by_section in candidates for a in by_section])


def rows_last(parts):
    return parts.transpose(4, 0, 2, 1, 3).reshape(parts.shape[-1], -1)


def per_device(w_first, w_second, saved_inputs, saved_hidden, cotangent):
    sections = lax.axis_size("section")
    hids = lax.axis_size("hid")
    wids = lax.axis_size("wid")
    section = lax.axis_index("section")
    wid = lax.axis_index("wid")
    hid = lax.axis_index("hid")
    behind = LAG * (sections - 1 - section)
    is_last = (section == sections - 1).astype(jnp.int32)
    weight_first = w_first[0]
    weight_second = w_second[0]
    micro, rows, width = cotangent.shape
    hidden = saved_hidden.shape[-1]
    sub = rows // hids // SUB_CHUNKS
    chunks = micro * SUB_CHUNKS
    periods = chunks + LAG * (sections - 1)
    parts = (micro, hids, SUB_CHUNKS, sub)
    cot_parts = cotangent.reshape(*parts, width)
    hidden_t = rows_last(saved_hidden.reshape(*parts, hidden))
    inputs_t = rows_last(saved_inputs.reshape(*parts, width))
    places = Places(wids, hids)
    steps = jnp.arange(hids, dtype=jnp.int32)
    number = jnp.arange(periods, dtype=jnp.int32)
    chosen = jnp.clip(number - behind, 0, chunks - 1)
    given_now = jnp.where(number < LAG, 1, is_last)
    table = jnp.concatenate(
        [
            jnp.stack([section, wid]),
            wid ^ jnp.array(mask_order(wids), jnp.int32),
            wid ^ jnp.arange(wids, dtype=jnp.int32),
            lax.rem(hid + hids - steps, hids),
            lax.rem(hid + 1 + steps, hids),
            jnp.stack(
                [given_now, lax.div(chosen, SUB_CHUNKS), lax.rem(chosen, SUB_CHUNKS), chosen], axis=1
            ).reshape(-1),
        ]
    )

    nothing = [jnp.zeros((sub, width), jnp.bfloat16)] * hids
    received = {}
    incoming, grads, results = [], [], []
    for period in range(periods):
        first, turned, given = project(
            table, places, period, cot_parts, received.get(period, nothing), weight_second, wids
        )
        blocks = rest(table, places, turned, weight_second, wids)
        blocks[mask_order(wids)[0]] = first
        incoming.append(given)
        own, arrived = reduce_blocks(blocks, "wid")
        block_grad = join(table, places, period, own, arrived, hidden_t)
        gathered = gather_blocks(block_grad, "wid")
        shares, hidden_grad = back(table, places, gathered, weight_first, hids)
        grads.append(hidden_grad)
        arrived = exchange(shares[:-1], "hid")
        row_share = rounded_total(shares[-1], arrived)
        results.append(lax.optimization_barrier(row_share))
        if period + LAG < periods:
            received[period + LAG] = hand_down(row_share)

    def by_chunk(values):
        return [
            [values[c + LAG * (sections - 1 - s)] for s in range(sections)] for c in range(chunks)
        ]

    grad_second = second_gradient(table, hidden_t, by_chunk(incoming))
    grad_first = first_gradient(table, inputs_t, by_chunk(grads))
    input_grads = jnp.stack(
        [lax.select_n(section, *by_section) if sections > 1 else by_section[0]
         for by_section in by_chunk(results)]
    ).reshape(micro, SUB_CHUNKS * sub, width)
    return (grad_first[None], grad_second[None], input_grads[None])


def solution(mesh):
    placed = (
        P("section", "wid", "hid"),
        P("section", "hid", "wid"),
        P("section", None, None, "wid"),
        P("section", None, None, "hid"),
        P(None, None, "wid"),
    )

    def step(*arrays):
        return jax.shard_map(
            per_device,
            mesh=mesh,
            in_specs=placed,
            out_specs=(
                P("section", "wid", "hid"),
                P("section", "hid", "wid"),
                P("section", None, "hid", "wid"),
            ),
            check_vma=False,
        )(*arrays)

    return step
```

time: 472 us -> 436 us (0.924); the launches traced: 470 us -> 428 us
  local copies, waits for them, and re-layouts: 98.6 us -> 31.3 us
  Pallas kernels: 113 us -> 177 us
  starting transfers between devices: 91.4 us -> 71.6 us
  between operations: 14.6 us -> 1.36 us
  waiting for transfers between devices: 148 us -> 140 us
    ppermute x0 -> x36, waiting for transfers between devices: none -> 114 us  [swap(): return lax.ppermute(block, axis, pairs)]
    ppermute x36 -> x18, waiting for transfers between devices: 96.8 us -> 10.9 us  [exchange(): arrived.append(lax.ppermute(blocks[shift - 1], axis, pairs))]
    pallas_call x12 -> x20, Pallas kernels: 95 us -> 160 us  [the longest x6 52.9 us: back(): pl.pallas_call(functools.partial(back_kernel, count, hids, places), grid_...]
    pallas_call x8 -> x0, local copies, waits for them, and re-layouts: 56.6 us -> none  [the longest x6 55.3 us: project(): pl.pallas_call(functools.partial(project_kernel, count, hids), grid_spec=...]
    ppermute x36 -> x18, starting transfers between devices: 70.4 us -> 16.3 us  [exchange(): arrived.append(lax.ppermute(blocks[shift - 1], axis, pairs))]
    ppermute x0 -> x36, starting transfers between devices: none -> 34.2 us  [swap(): return lax.ppermute(block, axis, pairs)]
    all_gather x6 -> x0, waiting for transfers between devices: 25.1 us -> none  [per_device(): hidden_grad = lax.all_gather(block_grad, 'wid', axis=0, tiled=True)]
    dynamic_update_slice x10 -> x0, local copies, waits for them, and re-layouts: 12.1 us -> none  [the longest x6 9.6 us: per_device(): lax.dynamic_update_slice_in_dim(grad_slots, hidden_grad[None], slot, 0)]
  transfers between devices with their start and end apart: 58 -> 70, of which waited for: 31 -> 27; matrix products, arithmetic and copies ran while one was open for 18% -> 5% of each run, Pallas kernels for 23% -> 40%
where the time goes in v2:
time: 436 us; the launch traced here: 428 us
  Pallas kernels  177 us (41%)
  waiting for transfers between devices  140 us (32%)
  starting transfers between devices  71.6 us (16%)
  local copies, waits for them, and re-layouts  31.3 us (7%)
  other arithmetic  6.2 us (1%)
    ppermute x36, waiting for transfers between devices, swap(): return lax.ppermute(block, axis, pairs)  114 us
    pallas_call x6, Pallas kernels, back(): pl.pallas_call(functools.partial(back_kernel, count, hids, places), grid_...  52.9 us
    pallas_call x6, Pallas kernels, rest(): pl.pallas_call(rest_kernel, grid_spec=grid_spec, out_shape=[jax.ShapeDtyp...  47.4 us
    ppermute x36, starting transfers between devices, swap(): return lax.ppermute(block, axis, pairs)  34.2 us
    pallas_call x6, Pallas kernels, project(): pl.pallas_call(functools.partial(project_kernel, hids, at, places.senders...  26.7 us
    ppermute x16, starting transfers between devices, hand_down(): arrived.append(lax.ppermute(share, ('section', 'hid'), pairs))  21.1 us
    pallas_call x6, Pallas kernels, join(): pl.pallas_call(join_kernel, grid_spec=grid_spec, out_shape=jax.ShapeDtype...  17.7 us
    pallas_call x1, Pallas kernels, first_gradient(): pl.pallas_call(functools.partial(first_kernel, sections), grid_spec=grid_...  17.3 us
  transfers between devices with their start and end apart: 70, of which 27 were waited for; matrix products, arithmetic and copies ran while one was open for 5% of the time, Pallas kernels for 40%

profile of v2, /device:TPU:0, one launch (start us, length us, event | category | flops | bytes accessed | tf_op | source)
XLA Modules:
  0.0 427.8 jit_solution(326921898910676624)
XLA Ops:
  2.8 4.7 %project.8 = (bf16[1280,128]{1,0:T(8,128)(2,1)}, bf16[1280,128]{1,0:T(8,128)(2,1)}, bf16[128,1280]{1,0:T(8,128)(2,1)}) custom-call(s32[42]{0:T(128)} %concatenate.3.table_ref.place_ref, bf16[2,4,2,32,1280]{4,3,2,1,0:T(8,128)(2,1)} %bitcast.42, bf16[32,1280]{1,0:T(8,128)(2,1)} %broadcast_in_dim.19.refs_0_.refs_1_.refs_2_.refs_3_, ...), custom_call_target="tpu_custom_call" | custom-call | flops 419430400 | bytes 3276800 | tf_op jit(solution)/shard_map/project/pallas_call | solution.py:158
  7.5 3.0 collective-permute-start.20
  10.5 7.9 %rest.8 = (bf16[1280,128]{1,0:T(8,128)(2,1)}, f32[1280,128]{1,0:T(8,128)}, f32[1280,128]{1,0:T(8,128)}) custom-call(s32[42]{0:T(128)} %concatenate.3.table_ref.place_ref, bf16[1280,128]{1,0:T(8,128)(2,1)} %get-tuple-element.85.turned_ref, bf16[5120,1280]{1,0:T(8,128)(2,1)} %bitcast.25), custom_call_target="tpu_custom_call" | custom-call | flops 1258291200 | bytes 9830400 | tf_op jit(solution)/shard_map/rest/pallas_call | solution.py:204
  19.6 3.0 collective-permute-start.21
  22.6 4.7 %project.6 = (bf16[1280,128]{1,0:T(8,128)(2,1)}, bf16[1280,128]{1,0:T(8,128)(2,1)}, bf16[128,1280]{1,0:T(8,128)(2,1)}) custom-call(s32[42]{0:T(128)} %concatenate.3.table_ref.place_ref, bf16[2,4,2,32,1280]{4,3,2,1,0:T(8,128)(2,1)} %bitcast.43, bf16[32,1280]{1,0:T(8,128)(2,1)} %broadcast_in_dim.19.refs_0_.refs_1_.refs_2_.refs_3_, ...), custom_call_target="tpu_custom_call" | custom-call | flops 419430400 | bytes 3276800 | tf_op jit(solution)/shard_map/project/pallas_call | solution.py:158
  29.0 7.9 %rest.6 = (bf16[1280,128]{1,0:T(8,128)(2,1)}, f32[1280,128]{1,0:T(8,128)}, f32[1280,128]{1,0:T(8,128)}) custom-call(s32[42]{0:T(128)} %concatenate.3.table_ref.place_ref, bf16[1280,128]{1,0:T(8,128)(2,1)} %get-tuple-element.69.turned_ref, bf16[5120,1280]{1,0:T(8,128)(2,1)} %bitcast.27), custom_call_target="tpu_custom_call" | custom-call | flops 1258291200 | bytes 9830400 | tf_op jit(solution)/shard_map/rest/pallas_call | solution.py:204
  37.3 5.3 %copy.20 = bf16[5120,2,2,4,32]{0,4,3,2,1:T(8,128)(2,1)} copy(bf16[5120,2,2,4,32]{0,4,2,3,1:T(8,128)(2,1)} %bitcast.51) | data formatting | bytes 10485760 | tf_op jit(solution)/shard_map/transpose | solution.py:395
  42.6 7.9 %copy.21.refs_2_.hidden_ref = bf16[5120,512]{1,0:T(8,128)(2,1)} copy(bf16[5120,512]{0,1:T(8,128)(2,1)} %bitcast.50) | data formatting | bytes 10485760 | tf_op jit(solution)/shard_map/reshape | solution.py:395
  51.4 3.0 join.8.refs_0_
  54.5 3.0 collective-permute-start.2
  59.1 19.7 %collective-permute-done.23.refs_2_ = bf16[1280,128]{1,0:T(8,128)(2,1)S(1)} collective-permute-done((bf16[1280,128]{1,0:T(8,128)(2,1)}, bf16[1280,128]{1,0:T(8,128)(2,1)S(1)}, u32[]{:S(2)}, u32[]{:S(2)}) %collective-permute-start.23) | collective-permute-done | bytes 327712 | tf_op jit(solution)/shard_map/ppermute | solution.py:29
  78.8 5.9 %collective-permute-done.2.refs_1_ = bf16[1280,128]{1,0:T(8,128)(2,1)S(1)} collective-permute-done((bf16[1280,128]{1,0:T(8,128)(2,1)S(1)}, bf16[1280,128]{1,0:T(8,128)(2,1)S(1)}, u32[]{:S(2)}, u32[]{:S(2)}) %collective-permute-start.2) | collective-permute-done | bytes 327712 | tf_op jit(solution)/shard_map/ppermute | solution.py:29
  85.4 2.9 join.6.refs_0_
  88.3 3.4 collective-permute-done.24.refs_3_
  92.4 8.9 %back.8 = (f32[32,1280]{1,0:T(8,128)}, f32[32,1280]{1,0:T(8,128)}, f32[32,1280]{1,0:T(8,128)}, f32[32,1280]{1,0:T(8,128)}, bf16[5120,128]{1,0:T(8,128)(2,1)}) custom-call(s32[42]{0:T(128)} %concatenate.3.table_ref.place_ref, bf16[1280,128]{1,0:T(8,128)(2,1)} %join.8.refs_0_, bf16[1280,128]{1,0:T(8,128)(2,1)} %copy-done.35, bf16[1280,128]{1,0:T(8,128)(2,1)} %copy-done.28, ...), custom_call_target="tpu_custom_call" | custom-call | flops 1677721600 | bytes 13107200 | tf_op jit(solution)/shard_map/back/pallas_call | solution.py:292
  114.9 5.2 %collective-permute-done.5.refs_3_ = bf16[1280,128]{1,0:T(8,128)(2,1)S(1)} collective-permute-done((bf16[1280,128]{1,0:T(8,128)(2,1)S(1)}, bf16[1280,128]{1,0:T(8,128)(2,1)S(1)}, u32[]{:S(2)}, u32[]{:S(2)}) %collective-permute-start.5) | collective-permute-done | bytes 327712 | tf_op jit(solution)/shard_map/ppermute | solution.py:29
  120.8 8.8 %back.6 = (f32[32,1280]{1,0:T(8,128)}, f32[32,1280]{1,0:T(8,128)}, f32[32,1280]{1,0:T(8,128)}, f32[32,1280]{1,0:T(8,128)}, bf16[5120,128]{1,0:T(8,128)(2,1)}) custom-call(s32[42]{0:T(128)} %concatenate.3.table_ref.place_ref, bf16[1280,128]{1,0:T(8,128)(2,1)} %join.6.refs_0_, bf16[1280,128]{1,0:T(8,128)(2,1)} %copy-done.30, bf16[1280,128]{1,0:T(8,128)(2,1)} %copy-done.24, ...), custom_call_target="tpu_custom_call" | custom-call | flops 1677721600 | bytes 13107200 | tf_op jit(solution)/shard_map/back/pallas_call | solution.py:292
  135.0 6.7 %collective-permute-done.29.refs_1_ = bf16[32,1280]{1,0:T(8,128)(2,1)S(1)} collective-permute-done((bf16[32,1280]{1,0:T(8,128)(2,1)S(1)}, bf16[32,1280]{1,0:T(8,128)(2,1)S(1)}, u32[]{:S(2)}, u32[]{:S(2)}) %collective-permute-start.29) | collective-permute-done | bytes 81952 | tf_op jit(solution)/shard_map/ppermute | solution.py:79
  143.0 4.3 %project.9 = (bf16[1280,128]{1,0:T(8,128)(2,1)}, bf16[1280,128]{1,0:T(8,128)(2,1)}, bf16[128,1280]{1,0:T(8,128)(2,1)}) custom-call(s32[42]{0:T(128)} %concatenate.3.table_ref.place_ref, bf16[2,4,2,32,1280]{4,3,2,1,0:T(8,128)(2,1)} %bitcast.44, bf16[32,1280]{1,0:T(8,128)(2,1)} %copy-done.58, bf16[32,1280]{1,0:T(8,128)(2,1)} %copy-done.56, ...), custom_call_target="tpu_custom_call" | custom-call | flops 419430400 | bytes 3276800 | tf_op jit(solution)/shard_map/project/pallas_call | solution.py:158
  153.0 7.9 %rest.9 = (bf16[1280,128]{1,0:T(8,128)(2,1)}, f32[1280,128]{1,0:T(8,128)}, f32[1280,128]{1,0:T(8,128)}) custom-call(s32[42]{0:T(128)} %concatenate.3.table_ref.place_ref, bf16[1280,128]{1,0:T(8,128)(2,1)} %get-tuple-element.94.turned_ref, bf16[5120,1280]{1,0:T(8,128)(2,1)} %bitcast.29), custom_call_target="tpu_custom_call" | custom-call | flops 1258291200 | bytes 9830400 | tf_op jit(solution)/shard_map/rest/pallas_call | solution.py:204
  165.2 4.3 %project.7 = (bf16[1280,128]{1,0:T(8,128)(2,1)}, bf16[1280,128]{1,0:T(8,128)(2,1)}, bf16[128,1280]{1,0:T(8,128)(2,1)}) custom-call(s32[42]{0:T(128)} %concatenate.3.table_ref.place_ref, bf16[2,4,2,32,1280]{4,3,2,1,0:T(8,128)(2,1)} %bitcast.45, bf16[32,1280]{1,0:T(8,128)(2,1)} %copy-done.51, bf16[32,1280]{1,0:T(8,128)(2,1)} %copy-done.50, ...), custom_call_target="tpu_custom_call" | custom-call | flops 419430400 | bytes 3276800 | tf_op jit(solution)/shard_map/project/pallas_call | solution.py:158
  171.3 7.8 %rest.7 = (bf16[1280,128]{1,0:T(8,128)(2,1)}, f32[1280,128]{1,0:T(8,128)}, f32[1280,128]{1,0:T(8,128)}) custom-call(s32[42]{0:T(128)} %concatenate.3.table_ref.place_ref, bf16[1280,128]{1,0:T(8,128)(2,1)} %get-tuple-element.78.turned_ref, bf16[5120,1280]{1,0:T(8,128)(2,1)} %bitcast.31), custom_call_target="tpu_custom_call" | custom-call | flops 1258291200 | bytes 9830400 | tf_op jit(solution)/shard_map/rest/pallas_call | solution.py:204
  180.3 3.0 join.9.refs_0_
  183.3 2.9 collective-permute-start.36
  188.1 20.5 %collective-permute-done.36.refs_2_ = bf16[1280,128]{1,0:T(8,128)(2,1)S(1)} collective-permute-done((bf16[1280,128]{1,0:T(8,128)(2,1)}, bf16[1280,128]{1,0:T(8,128)(2,1)S(1)}, u32[]{:S(2)}, u32[]{:S(2)}) %collective-permute-start.36) | collective-permute-done | bytes 327712 | tf_op jit(solution)/shard_map/ppermute | solution.py:29
  208.6 3.5 collective-permute-done.15.refs_1_
  212.8 2.9 join.7.refs_0_
  215.7 4.4 %collective-permute-done.37.refs_3_ = bf16[1280,128]{1,0:T(8,128)(2,1)S(1)} collective-permute-done((bf16[1280,128]{1,0:T(8,128)(2,1)S(1)}, bf16[1280,128]{1,0:T(8,128)(2,1)S(1)}, u32[]{:S(2)}, u32[]{:S(2)}) %collective-permute-start.37) | collective-permute-done | bytes 327712 | tf_op jit(solution)/shard_map/ppermute | solution.py:29
  220.9 8.8 %back.9 = (f32[32,1280]{1,0:T(8,128)}, f32[32,1280]{1,0:T(8,128)}, f32[32,1280]{1,0:T(8,128)}, f32[32,1280]{1,0:T(8,128)}, bf16[5120,128]{1,0:T(8,128)(2,1)}) custom-call(s32[42]{0:T(128)} %concatenate.3.table_ref.place_ref, bf16[1280,128]{1,0:T(8,128)(2,1)} %join.9.refs_0_, bf16[1280,128]{1,0:T(8,128)(2,1)} %copy-done.36, bf16[1280,128]{1,0:T(8,128)(2,1)} %copy-done.29, ...), custom_call_target="tpu_custom_call" | custom-call | flops 1677721600 | bytes 13107200 | tf_op jit(solution)/shard_map/back/pallas_call | solution.py:292
  232.5 2.5 collective-permute-start.16
  243.6 5.5 %collective-permute-done.18.refs_3_ = bf16[1280,128]{1,0:T(8,128)(2,1)S(1)} collective-permute-done((bf16[1280,128]{1,0:T(8,128)(2,1)S(1)}, bf16[1280,128]{1,0:T(8,128)(2,1)S(1)}, u32[]{:S(2)}, u32[]{:S(2)}) %collective-permute-start.18) | collective-permute-done | bytes 327712 | tf_op jit(solution)/shard_map/ppermute | solution.py:29
  249.8 8.8 %back.7 = (f32[32,1280]{1,0:T(8,128)}, f32[32,1280]{1,0:T(8,128)}, f32[32,1280]{1,0:T(8,128)}, f32[32,1280]{1,0:T(8,128)}, bf16[5120,128]{1,0:T(8,128)(2,1)}) custom-call(s32[42]{0:T(128)} %concatenate.3.table_ref.place_ref, bf16[1280,128]{1,0:T(8,128)(2,1)} %join.7.refs_0_, bf16[1280,128]{1,0:T(8,128)(2,1)} %copy-done.31, bf16[1280,128]{1,0:T(8,128)(2,1)} %copy-done.25, ...), custom_call_target="tpu_custom_call" | custom-call | flops 1677721600 | bytes 13107200 | tf_op jit(solution)/shard_map/back/pallas_call | solution.py:292
  264.0 8.5 %collective-permute-done.55.refs_1_ = bf16[32,1280]{1,0:T(8,128)(2,1)S(1)} collective-permute-done((bf16[32,1280]{1,0:T(8,128)(2,1)S(1)}, bf16[32,1280]{1,0:T(8,128)(2,1)S(1)}, u32[]{:S(2)}, u32[]{:S(2)}) %collective-permute-start.55) | collective-permute-done | bytes 81952 | tf_op jit(solution)/shard_map/ppermute | solution.py:79
  273.8 4.3 %project.11 = (bf16[1280,128]{1,0:T(8,128)(2,1)}, bf16[1280,128]{1,0:T(8,128)(2,1)}, bf16[128,1280]{1,0:T(8,128)(2,1)}) custom-call(s32[42]{0:T(128)} %concatenate.3.table_ref.place_ref, bf16[2,4,2,32,1280]{4,3,2,1,0:T(8,128)(2,1)} %bitcast.46, bf16[32,1280]{1,0:T(8,128)(2,1)} %copy-done.59, bf16[32,1280]{1,0:T(8,128)(2,1)} %copy-done.57, ...), custom_call_target="tpu_custom_call" | custom-call | flops 419430400 | bytes 3276800 | tf_op jit(solution)/shard_map/project/pallas_call | solution.py:158
  285.3 8.0 %rest.11 = (bf16[1280,128]{1,0:T(8,128)(2,1)}, f32[1280,128]{1,0:T(8,128)}, f32[1280,128]{1,0:T(8,128)}) custom-call(s32[42]{0:T(128)} %concatenate.3.table_ref.place_ref, bf16[1280,128]{1,0:T(8,128)(2,1)} %get-tuple-element.115.turned_ref, bf16[5120,1280]{1,0:T(8,128)(2,1)} %bitcast.33), custom_call_target="tpu_custom_call" | custom-call | flops 1258291200 | bytes 9830400 | tf_op jit(solution)/shard_map/rest/pallas_call | solution.py:204
  295.0 4.3 %project.10 = (bf16[1280,128]{1,0:T(8,128)(2,1)}, bf16[1280,128]{1,0:T(8,128)(2,1)}, bf16[128,1280]{1,0:T(8,128)(2,1)}) custom-call(s32[42]{0:T(128)} %concatenate.3.table_ref.place_ref, bf16[2,4,2,32,1280]{4,3,2,1,0:T(8,128)(2,1)} %bitcast.47, bf16[32,1280]{1,0:T(8,128)(2,1)} %copy-done.55, bf16[32,1280]{1,0:T(8,128)(2,1)} %copy-done.54, ...), custom_call_target="tpu_custom_call" | custom-call | flops 419430400 | bytes 3276800 | tf_op jit(solution)/shard_map/project/pallas_call | solution.py:158
  301.0 8.0 %rest.10 = (bf16[1280,128]{1,0:T(8,128)(2,1)}, f32[1280,128]{1,0:T(8,128)}, f32[1280,128]{1,0:T(8,128)}) custom-call(s32[42]{0:T(128)} %concatenate.3.table_ref.place_ref, bf16[1280,128]{1,0:T(8,128)(2,1)} %get-tuple-element.105.turned_ref, bf16[5120,1280]{1,0:T(8,128)(2,1)} %bitcast.35), custom_call_target="tpu_custom_call" | custom-call | flops 1258291200 | bytes 9830400 | tf_op jit(solution)/shard_map/rest/pallas_call | solution.py:204
  312.5 24.9 %collective-permute-done.60.refs_1_ = bf16[1280,128]{1,0:T(8,128)(2,1)S(1)} collective-permute-done((bf16[1280,128]{1,0:T(8,128)(2,1)S(1)}, bf16[1280,128]{1,0:T(8,128)(2,1)S(1)}, u32[]{:S(2)}, u32[]{:S(2)}) %collective-permute-start.60) | collective-permute-done | bytes 327712 | tf_op jit(solution)/shard_map/ppermute | solution.py:29
  338.2 2.9 join.11.refs_0_
  341.1 3.4 collective-permute-done.47.refs_1_
  345.2 3.0 join.10.refs_0_
  352.5 9.9 %collective-permute-done.62.refs_2_ = bf16[1280,128]{1,0:T(8,128)(2,1)} collective-permute-done((bf16[1280,128]{1,0:T(8,128)(2,1)}, bf16[1280,128]{1,0:T(8,128)(2,1)}, u32[]{:S(2)}, u32[]{:S(2)}) %collective-permute-start.62) | collective-permute-done | bytes 327712 | tf_op jit(solution)/shard_map/ppermute | solution.py:29
  362.4 3.4 collective-permute-done.49.refs_2_
  365.8 15.4 %second_gradient.1 = f32[5120,1280]{1,0:T(8,128)} custom-call(s32[42]{0:T(128)} %concatenate.3.table_ref.place_ref, bf16[5120,512]{1,0:T(8,128)(2,1)} %copy.21.refs_2_.hidden_ref, bf16[128,1280]{1,0:T(8,128)(2,1)} %get-tuple-element.121.refs_0_.refs_5_, bf16[128,1280]{1,0:T(8,128)(2,1)} %get-tuple-element.122.refs_1_, ...), custom_call_target="tpu_custom_call" | custom-call | flops 6710886400 | bytes 26214400 | tf_op jit(solution)/shard_map/second_gradient/pallas_call | solution.py:385
  382.6 8.8 %back.11 = (f32[32,1280]{1,0:T(8,128)}, f32[32,1280]{1,0:T(8,128)}, f32[32,1280]{1,0:T(8,128)}, f32[32,1280]{1,0:T(8,128)}, bf16[5120,128]{1,0:T(8,128)(2,1)}) custom-call(s32[42]{0:T(128)} %concatenate.3.table_ref.place_ref, bf16[1280,128]{1,0:T(8,128)(2,1)} %join.11.refs_0_, bf16[1280,128]{1,0:T(8,128)(2,1)} %copy-done.32, ...), custom_call_target="tpu_custom_call" | custom-call | flops 1677721600 | bytes 13107200 | tf_op jit(solution)/shard_map/back/pallas_call | solution.py:292
  395.3 8.8 %back.10 = (f32[32,1280]{1,0:T(8,128)}, f32[32,1280]{1,0:T(8,128)}, f32[32,1280]{1,0:T(8,128)}, f32[32,1280]{1,0:T(8,128)}, bf16[5120,128]{1,0:T(8,128)(2,1)}) custom-call(s32[42]{0:T(128)} %concatenate.3.table_ref.place_ref, bf16[1280,128]{1,0:T(8,128)(2,1)} %join.10.refs_0_, bf16[1280,128]{1,0:T(8,128)(2,1)} %copy-done.26, bf16[1280,128]{1,0:T(8,128)(2,1)} %copy-done.23, ...), custom_call_target="tpu_custom_call" | custom-call | flops 1677721600 | bytes 13107200 | tf_op jit(solution)/shard_map/back/pallas_call | solution.py:292
  405.3 17.3 %first_gradient.1 = f32[1280,5120]{1,0:T(8,128)} custom-call(s32[42]{0:T(128)} %concatenate.3.table_ref.place_ref, bf16[1280,512]{1,0:T(8,128)(2,1)} %copy.27.inputs_ref, bf16[5120,128]{1,0:T(8,128)(2,1)} %get-tuple-element.83.refs_0_.refs_5_, bf16[5120,128]{1,0:T(8,128)(2,1)} %get-tuple-element.84.refs_1_, ...), custom_call_target="tpu_custom_call" | custom-call | flops 6710886400 | bytes 26214400 | tf_op jit(solution)/shard_map/first_gradient/pallas_call | solution.py:347
  424.1 2.8 collective-permute-done.66
  (267 shorter events, 93.7 us)
Async XLA Ops:
  18.4 32.1 %collective-permute-start.19 = (bf16[1280,128]{1,0:T(8,128)(2,1)}, bf16[1280,128]{1,0:T(8,128)(2,1)S(1)}, u32[]{:S(2)}, u32[]{:S(2)}) collective-permute-start(bf16[1280,128]{1,0:T(8,128)(2,1)} %get-tuple-element.87), channel_id=1, source_target_pairs={{0,1},{1,0},{2,3},{3,2},{4,5},{5,4},{6,7},{7,6},{8,9},{9,8},{10,11... | collective-permute-start | bytes 983048 | tf_op jit(solution)/shard_map/ppermute | solution.py:29
  19.6 30.9 %collective-permute-start.21 = (bf16[1280,128]{1,0:T(8,128)(2,1)S(1)}, bf16[1280,128]{1,0:T(8,128)(2,1)S(1)}, u32[]{:S(2)}, u32[]{:S(2)}) collective-permute-start(bf16[1280,128]{1,0:T(8,128)(2,1)S(1)} %add_convert_fusion.3), channel_id=1, source_target_pairs={{0,2},{1,3},{2,0},{3,1},{4,6},{5,7},{6,4},{7,5},{8,10},{9,11},{10,... | collective-permute-start | bytes 983048 | tf_op jit(solution)/shard_map/ppermute | solution.py:29
  27.4 27.0 %collective-permute-start.1 = (bf16[1280,128]{1,0:T(8,128)(2,1)}, bf16[1280,128]{1,0:T(8,128)(2,1)S(1)}, u32[]{:S(2)}, u32[]{:S(2)}) collective-permute-start(bf16[1280,128]{1,0:T(8,128)(2,1)} %get-tuple-element.73), channel_id=1, source_target_pairs={{0,1},{1,0},{2,3},{3,2},{4,5},{5,4},{6,7},{7,6},{8,9},{9,8},{10,11... | collective-permute-start | bytes 983048 | tf_op jit(solution)/shard_map/ppermute | solution.py:29
  36.9 41.9 %collective-permute-start = (bf16[1280,128]{1,0:T(8,128)(2,1)}, bf16[1280,128]{1,0:T(8,128)(2,1)S(1)}, u32[]{:S(2)}, u32[]{:S(2)}) collective-permute-start(bf16[1280,128]{1,0:T(8,128)(2,1)} %get-tuple-element.71), channel_id=1, source_target_pairs={{0,1},{1,0},{2,3},{3,2},{4,5},{5,4},{6,7},{7,6},{8,9},{9,8},{10,11... | collective-permute-start | bytes 983048 | tf_op jit(solution)/shard_map/ppermute | solution.py:29
  54.4 24.4 %collective-permute-start.23 = (bf16[1280,128]{1,0:T(8,128)(2,1)}, bf16[1280,128]{1,0:T(8,128)(2,1)S(1)}, u32[]{:S(2)}, u32[]{:S(2)}) collective-permute-start(bf16[1280,128]{1,0:T(8,128)(2,1)} %join.8.refs_0_), channel_id=1, source_target_pairs={{0,2},{1,3},{2,0},{3,1},{4,6},{5,7},{6,4},{7,5},{8,10},{9,11},{10,... | collective-permute-start | bytes 983048 | tf_op jit(solution)/shard_map/ppermute | solution.py:29
  54.5 30.2 %collective-permute-start.2 = (bf16[1280,128]{1,0:T(8,128)(2,1)S(1)}, bf16[1280,128]{1,0:T(8,128)(2,1)S(1)}, u32[]{:S(2)}, u32[]{:S(2)}) collective-permute-start(bf16[1280,128]{1,0:T(8,128)(2,1)S(1)} %add_convert_fusion.5), channel_id=1, source_target_pairs={{0,2},{1,3},{2,0},{3,1},{4,6},{5,7},{6,4},{7,5},{8,10},{9,11},{10,... | collective-permute-start | bytes 983048 | tf_op jit(solution)/shard_map/ppermute | solution.py:29
  57.4 30.9 %collective-permute-start.22 = (bf16[1280,128]{1,0:T(8,128)(2,1)S(1)}, bf16[1280,128]{1,0:T(8,128)(2,1)S(1)}, u32[]{:S(2)}, u32[]{:S(2)}) collective-permute-start(bf16[1280,128]{1,0:T(8,128)(2,1)S(1)} %copy-done.5), channel_id=1, source_target_pairs={{0,1},{1,0},{2,3},{3,2},{4,5},{5,4},{6,7},{7,6},{8,9},{9,8},{10,11... | collective-permute-start | bytes 983048 | tf_op jit(solution)/shard_map/ppermute | solution.py:29
  88.3 16.3 %collective-permute-start.4 = (bf16[1280,128]{1,0:T(8,128)(2,1)}, bf16[1280,128]{1,0:T(8,128)(2,1)S(1)}, u32[]{:S(2)}, u32[]{:S(2)}) collective-permute-start(bf16[1280,128]{1,0:T(8,128)(2,1)} %join.6.refs_0_), channel_id=1, source_target_pairs={{0,2},{1,3},{2,0},{3,1},{4,6},{5,7},{6,4},{7,5},{8,10},{9,11},{10,... | collective-permute-start | bytes 983048 | tf_op jit(solution)/shard_map/ppermute | solution.py:29
  104.6 15.4 %collective-permute-start.5 = (bf16[1280,128]{1,0:T(8,128)(2,1)S(1)}, bf16[1280,128]{1,0:T(8,128)(2,1)S(1)}, u32[]{:S(2)}, u32[]{:S(2)}) collective-permute-start(bf16[1280,128]{1,0:T(8,128)(2,1)S(1)} %collective-permute-done.4.refs_2_), channel_id=1, source_target_pairs={{0,1},{1,0},{2,3},{3,2},{4,5},{5,4},{6,7},{7,6},{8,9},{9,8},{10,11... | collective-permute-start | bytes 983048 | tf_op jit(solution)/shard_map/ppermute | solution.py:29
  111.6 20.8 %collective-permute-start.31 = (bf16[32,1280]{1,0:T(8,128)(2,1)S(1)}, bf16[32,1280]{1,0:T(8,128)(2,1)S(1)}, u32[]{:S(2)}, u32[]{:S(2)}) collective-permute-start(bf16[32,1280]{1,0:T(8,128)(2,1)S(1)} %add_convert_fusion.10), channel_id=1, source_target_pairs={{16,12},{20,0},{24,4},{28,8},{17,13},{21,1},{25,5},{29,9},{18,14},... | collective-permute-start | bytes 245768 | tf_op jit(solution)/shard_map/ppermute | solution.py:79
  112.9 20.7 %collective-permute-start.30 = (bf16[32,1280]{1,0:T(8,128)(2,1)S(1)}, bf16[32,1280]{1,0:T(8,128)(2,1)S(1)}, u32[]{:S(2)}, u32[]{:S(2)}) collective-permute-start(bf16[32,1280]{1,0:T(8,128)(2,1)S(1)} %add_convert_fusion.10), channel_id=1, source_target_pairs={{16,8},{20,12},{24,0},{28,4},{17,9},{21,13},{25,1},{29,5},{18,10},... | collective-permute-start | bytes 245768 | tf_op jit(solution)/shard_map/ppermute | solution.py:79
  129.6 18.0 %collective-permute-start.6 = (f32[32,1280]{1,0:T(8,128)}, f32[32,1280]{1,0:T(8,128)S(1)}, u32[]{:S(2)}, u32[]{:S(2)}) collective-permute-start(f32[32,1280]{1,0:T(8,128)} %get-tuple-element.75), channel_id=1, source_target_pairs={{0,4},{4,8},{8,12},{12,0},{1,5},{5,9},{9,13},{13,1},{2,6},{6,10},{... | collective-permute-start | bytes 491528 | tf_op jit(solution)/shard_map/ppermute | solution.py:23
  129.6 17.9 %collective-permute-start.7 = (f32[32,1280]{1,0:T(8,128)}, f32[32,1280]{1,0:T(8,128)S(1)}, u32[]{:S(2)}, u32[]{:S(2)}) collective-permute-start(f32[32,1280]{1,0:T(8,128)} %get-tuple-element.76), channel_id=1, source_target_pairs={{0,8},{4,12},{8,0},{12,4},{1,9},{5,13},{9,1},{13,5},{2,10},{6,14},... | collective-permute-start | bytes 491528 | tf_op jit(solution)/shard_map/ppermute | solution.py:23
  131.0 16.6 %collective-permute-start.8 = (f32[32,1280]{1,0:T(8,128)}, f32[32,1280]{1,0:T(8,128)S(1)}, u32[]{:S(2)}, u32[]{:S(2)}) collective-permute-start(f32[32,1280]{1,0:T(8,128)} %get-tuple-element.77), channel_id=1, source_target_pairs={{0,12},{4,0},{8,4},{12,8},{1,13},{5,1},{9,5},{13,9},{2,14},{6,2},{... | collective-permute-start | bytes 491528 | tf_op jit(solution)/shard_map/ppermute | solution.py:23
  147.3 13.6 %collective-permute-start.33 = (bf16[1280,128]{1,0:T(8,128)(2,1)}, bf16[1280,128]{1,0:T(8,128)(2,1)S(1)}, u32[]{:S(2)}, u32[]{:S(2)}) collective-permute-start(bf16[1280,128]{1,0:T(8,128)(2,1)} %get-tuple-element.98), channel_id=1, source_target_pairs={{0,1},{1,0},{2,3},{3,2},{4,5},{5,4},{6,7},{7,6},{8,9},{9,8},{10,11... | collective-permute-start | bytes 983048 | tf_op jit(solution)/shard_map/ppermute | solution.py:29
  147.6 16.2 %collective-permute-start.12 = (bf16[32,1280]{1,0:T(8,128)(2,1)S(1)}, bf16[32,1280]{1,0:T(8,128)(2,1)S(1)}, u32[]{:S(2)}, u32[]{:S(2)}) collective-permute-start(bf16[32,1280]{1,0:T(8,128)(2,1)S(1)} %add_convert_fusion.11), channel_id=1, source_target_pairs={{16,12},{20,0},{24,4},{28,8},{17,13},{21,1},{25,5},{29,9},{18,14},... | collective-permute-start | bytes 245768 | tf_op jit(solution)/shard_map/ppermute | solution.py:79
  148.9 15.0 %collective-permute-start.11 = (bf16[32,1280]{1,0:T(8,128)(2,1)S(1)}, bf16[32,1280]{1,0:T(8,128)(2,1)S(1)}, u32[]{:S(2)}, u32[]{:S(2)}) collective-permute-start(bf16[32,1280]{1,0:T(8,128)(2,1)S(1)} %add_convert_fusion.11), channel_id=1, source_target_pairs={{16,8},{20,12},{24,0},{28,4},{17,9},{21,13},{25,1},{29,5},{18,10},... | collective-permute-start | bytes 245768 | tf_op jit(solution)/shard_map/ppermute | solution.py:79
  150.2 13.7 %collective-permute-start.10 = (bf16[32,1280]{1,0:T(8,128)(2,1)S(1)}, bf16[32,1280]{1,0:T(8,128)(2,1)S(1)}, u32[]{:S(2)}, u32[]{:S(2)}) collective-permute-start(bf16[32,1280]{1,0:T(8,128)(2,1)S(1)} %add_convert_fusion.11), channel_id=1, source_target_pairs={{16,4},{20,8},{24,12},{28,0},{17,5},{21,9},{25,13},{29,1},{18,6},{... | collective-permute-start | bytes 245768 | tf_op jit(solution)/shard_map/ppermute | solution.py:79
  160.9 18.5 %collective-permute-start.32 = (bf16[1280,128]{1,0:T(8,128)(2,1)}, bf16[1280,128]{1,0:T(8,128)(2,1)S(1)}, u32[]{:S(2)}, u32[]{:S(2)}) collective-permute-start(bf16[1280,128]{1,0:T(8,128)(2,1)} %get-tuple-element.96), channel_id=1, source_target_pairs={{0,1},{1,0},{2,3},{3,2},{4,5},{5,4},{6,7},{7,6},{8,9},{9,8},{10,11... | collective-permute-start | bytes 983048 | tf_op jit(solution)/shard_map/ppermute | solution.py:29
  163.8 15.6 %collective-permute-start.34 = (bf16[1280,128]{1,0:T(8,128)(2,1)S(1)}, bf16[1280,128]{1,0:T(8,128)(2,1)S(1)}, u32[]{:S(2)}, u32[]{:S(2)}) collective-permute-start(bf16[1280,128]{1,0:T(8,128)(2,1)S(1)} %add_convert_fusion.2), channel_id=1, source_target_pairs={{0,2},{1,3},{2,0},{3,1},{4,6},{5,7},{6,4},{7,5},{8,10},{9,11},{10,... | collective-permute-start | bytes 983048 | tf_op jit(solution)/shard_map/ppermute | solution.py:29
  169.6 18.0 %collective-permute-start.14 = (bf16[1280,128]{1,0:T(8,128)(2,1)}, bf16[1280,128]{1,0:T(8,128)(2,1)S(1)}, u32[]{:S(2)}, u32[]{:S(2)}) collective-permute-start(bf16[1280,128]{1,0:T(8,128)(2,1)} %get-tuple-element.82), channel_id=1, source_target_pairs={{0,1},{1,0},{2,3},{3,2},{4,5},{5,4},{6,7},{7,6},{8,9},{9,8},{10,11... | collective-permute-start | bytes 983048 | tf_op jit(solution)/shard_map/ppermute | solution.py:29
  179.1 29.5 %collective-permute-start.13 = (bf16[1280,128]{1,0:T(8,128)(2,1)}, bf16[1280,128]{1,0:T(8,128)(2,1)S(1)}, u32[]{:S(2)}, u32[]{:S(2)}) collective-permute-start(bf16[1280,128]{1,0:T(8,128)(2,1)} %get-tuple-element.80), channel_id=1, source_target_pairs={{0,1},{1,0},{2,3},{3,2},{4,5},{5,4},{6,7},{7,6},{8,9},{9,8},{10,11... | collective-permute-start | bytes 983048 | tf_op jit(solution)/shard_map/ppermute | solution.py:29
  183.3 25.3 %collective-permute-start.36 = (bf16[1280,128]{1,0:T(8,128)(2,1)}, bf16[1280,128]{1,0:T(8,128)(2,1)S(1)}, u32[]{:S(2)}, u32[]{:S(2)}) collective-permute-start(bf16[1280,128]{1,0:T(8,128)(2,1)} %join.9.refs_0_), channel_id=1, source_target_pairs={{0,2},{1,3},{2,0},{3,1},{4,6},{5,7},{6,4},{7,5},{8,10},{9,11},{10,... | collective-permute-start | bytes 983048 | tf_op jit(solution)/shard_map/ppermute | solution.py:29
  187.6 24.5 %collective-permute-start.15 = (bf16[1280,128]{1,0:T(8,128)(2,1)S(1)}, bf16[1280,128]{1,0:T(8,128)(2,1)S(1)}, u32[]{:S(2)}, u32[]{:S(2)}) collective-permute-start(bf16[1280,128]{1,0:T(8,128)(2,1)S(1)} %add_convert_fusion.4), channel_id=1, source_target_pairs={{0,2},{1,3},{2,0},{3,1},{4,6},{5,7},{6,4},{7,5},{8,10},{9,11},{10,... | collective-permute-start | bytes 983048 | tf_op jit(solution)/shard_map/ppermute | solution.py:29
  187.7 28.0 %collective-permute-start.35 = (bf16[1280,128]{1,0:T(8,128)(2,1)S(1)}, bf16[1280,128]{1,0:T(8,128)(2,1)S(1)}, u32[]{:S(2)}, u32[]{:S(2)}) collective-permute-start(bf16[1280,128]{1,0:T(8,128)(2,1)S(1)} %copy-done.6), channel_id=1, source_target_pairs={{0,1},{1,0},{2,3},{3,2},{4,5},{5,4},{6,7},{7,6},{8,9},{9,8},{10,11... | collective-permute-start | bytes 983048 | tf_op jit(solution)/shard_map/ppermute | solution.py:29
  215.7 19.3 %collective-permute-start.17 = (bf16[1280,128]{1,0:T(8,128)(2,1)}, bf16[1280,128]{1,0:T(8,128)(2,1)S(1)}, u32[]{:S(2)}, u32[]{:S(2)}) collective-permute-start(bf16[1280,128]{1,0:T(8,128)(2,1)} %join.7.refs_0_), channel_id=1, source_target_pairs={{0,2},{1,3},{2,0},{3,1},{4,6},{5,7},{6,4},{7,5},{8,10},{9,11},{10,... | collective-permute-start | bytes 983048 | tf_op jit(solution)/shard_map/ppermute | solution.py:29
  235.0 14.0 %collective-permute-start.18 = (bf16[1280,128]{1,0:T(8,128)(2,1)S(1)}, bf16[1280,128]{1,0:T(8,128)(2,1)S(1)}, u32[]{:S(2)}, u32[]{:S(2)}) collective-permute-start(bf16[1280,128]{1,0:T(8,128)(2,1)S(1)} %collective-permute-done.17.refs_2_), channel_id=1, source_target_pairs={{0,1},{1,0},{2,3},{3,2},{4,5},{5,4},{6,7},{7,6},{8,9},{9,8},{10,11... | collective-permute-start | bytes 983048 | tf_op jit(solution)/shard_map/ppermute | solution.py:29
  239.8 21.5 %collective-permute-start.57 = (bf16[32,1280]{1,0:T(8,128)(2,1)S(1)}, bf16[32,1280]{1,0:T(8,128)(2,1)S(1)}, u32[]{:S(2)}, u32[]{:S(2)}) collective-permute-start(bf16[32,1280]{1,0:T(8,128)(2,1)S(1)} %add_convert_fusion.8), channel_id=1, source_target_pairs={{16,12},{20,0},{24,4},{28,8},{17,13},{21,1},{25,5},{29,9},{18,14},... | collective-permute-start | bytes 245768 | tf_op jit(solution)/shard_map/ppermute | solution.py:79
  241.1 21.5 %collective-permute-start.56 = (bf16[32,1280]{1,0:T(8,128)(2,1)S(1)}, bf16[32,1280]{1,0:T(8,128)(2,1)S(1)}, u32[]{:S(2)}, u32[]{:S(2)}) collective-permute-start(bf16[32,1280]{1,0:T(8,128)(2,1)S(1)} %add_convert_fusion.8), channel_id=1, source_target_pairs={{16,8},{20,12},{24,0},{28,4},{17,9},{21,13},{25,1},{29,5},{18,10},... | collective-permute-start | bytes 245768 | tf_op jit(solution)/shard_map/ppermute | solution.py:79
  258.6 21.2 %collective-permute-start.38 = (f32[32,1280]{1,0:T(8,128)}, f32[32,1280]{1,0:T(8,128)S(1)}, u32[]{:S(2)}, u32[]{:S(2)}) collective-permute-start(f32[32,1280]{1,0:T(8,128)} %get-tuple-element.102), channel_id=1, source_target_pairs={{0,4},{4,8},{8,12},{12,0},{1,5},{5,9},{9,13},{13,1},{2,6},{6,10},{... | collective-permute-start | bytes 491528 | tf_op jit(solution)/shard_map/ppermute | solution.py:23
  258.6 21.2 %collective-permute-start.39 = (f32[32,1280]{1,0:T(8,128)}, f32[32,1280]{1,0:T(8,128)S(1)}, u32[]{:S(2)}, u32[]{:S(2)}) collective-permute-start(f32[32,1280]{1,0:T(8,128)} %get-tuple-element.103), channel_id=1, source_target_pairs={{0,8},{4,12},{8,0},{12,4},{1,9},{5,13},{9,1},{13,5},{2,10},{6,14},... | collective-permute-start | bytes 491528 | tf_op jit(solution)/shard_map/ppermute | solution.py:23
  260.0 19.9 %collective-permute-start.40 = (f32[32,1280]{1,0:T(8,128)}, f32[32,1280]{1,0:T(8,128)S(1)}, u32[]{:S(2)}, u32[]{:S(2)}) collective-permute-start(f32[32,1280]{1,0:T(8,128)} %get-tuple-element.104), channel_id=1, source_target_pairs={{0,12},{4,0},{8,4},{12,8},{1,13},{5,1},{9,5},{13,9},{2,14},{6,2},{... | collective-permute-start | bytes 491528 | tf_op jit(solution)/shard_map/ppermute | solution.py:23
  278.1 31.2 %collective-permute-start.59 = (bf16[1280,128]{1,0:T(8,128)(2,1)}, bf16[1280,128]{1,0:T(8,128)(2,1)S(1)}, u32[]{:S(2)}, u32[]{:S(2)}) collective-permute-start(bf16[1280,128]{1,0:T(8,128)(2,1)} %get-tuple-element.119), channel_id=1, source_target_pairs={{0,1},{1,0},{2,3},{3,2},{4,5},{5,4},{6,7},{7,6},{8,9},{9,8},{10,11... | collective-permute-start | bytes 983048 | tf_op jit(solution)/shard_map/ppermute | solution.py:29
  293.3 19.2 %collective-permute-start.58 = (bf16[1280,128]{1,0:T(8,128)(2,1)}, bf16[1280,128]{1,0:T(8,128)(2,1)S(1)}, u32[]{:S(2)}, u32[]{:S(2)}) collective-permute-start(bf16[1280,128]{1,0:T(8,128)(2,1)} %get-tuple-element.117), channel_id=1, source_target_pairs={{0,1},{1,0},{2,3},{3,2},{4,5},{5,4},{6,7},{7,6},{8,9},{9,8},{10,11... | collective-permute-start | bytes 983048 | tf_op jit(solution)/shard_map/ppermute | solution.py:29
  309.0 32.0 %collective-permute-start.45 = (bf16[1280,128]{1,0:T(8,128)(2,1)}, bf16[1280,128]{1,0:T(8,128)(2,1)S(1)}, u32[]{:S(2)}, u32[]{:S(2)}) collective-permute-start(bf16[1280,128]{1,0:T(8,128)(2,1)} %get-tuple-element.107), channel_id=1, source_target_pairs={{0,1},{1,0},{2,3},{3,2},{4,5},{5,4},{6,7},{7,6},{8,9},{9,8},{10,11... | collective-permute-start | bytes 983048 | tf_op jit(solution)/shard_map/ppermute | solution.py:29
  309.4 28.1 %collective-permute-start.60 = (bf16[1280,128]{1,0:T(8,128)(2,1)S(1)}, bf16[1280,128]{1,0:T(8,128)(2,1)S(1)}, u32[]{:S(2)}, u32[]{:S(2)}) collective-permute-start(bf16[1280,128]{1,0:T(8,128)(2,1)S(1)} %add_convert_fusion), channel_id=1, source_target_pairs={{0,2},{1,3},{2,0},{3,1},{4,6},{5,7},{6,4},{7,5},{8,10},{9,11},{10,... | collective-permute-start | bytes 983048 | tf_op jit(solution)/shard_map/ppermute | solution.py:29
  311.9 32.6 %collective-permute-start.47 = (bf16[1280,128]{1,0:T(8,128)(2,1)S(1)}, bf16[1280,128]{1,0:T(8,128)(2,1)S(1)}, u32[]{:S(2)}, u32[]{:S(2)}) collective-permute-start(bf16[1280,128]{1,0:T(8,128)(2,1)S(1)} %add_convert_fusion.1), channel_id=1, source_target_pairs={{0,2},{1,3},{2,0},{3,1},{4,6},{5,7},{6,4},{7,5},{8,10},{9,11},{10,... | collective-permute-start | bytes 983048 | tf_op jit(solution)/shard_map/ppermute | solution.py:29
  341.1 21.3 %collective-permute-start.62 = (bf16[1280,128]{1,0:T(8,128)(2,1)}, bf16[1280,128]{1,0:T(8,128)(2,1)}, u32[]{:S(2)}, u32[]{:S(2)}) collective-permute-start(bf16[1280,128]{1,0:T(8,128)(2,1)} %join.11.refs_0_), channel_id=1, source_target_pairs={{0,2},{1,3},{2,0},{3,1},{4,6},{5,7},{6,4},{7,5},{8,10},{9,11},{10,... | collective-permute-start | bytes 983048 | tf_op jit(solution)/shard_map/ppermute | solution.py:29
  348.2 17.6 %collective-permute-start.49 = (bf16[1280,128]{1,0:T(8,128)(2,1)}, bf16[1280,128]{1,0:T(8,128)(2,1)S(1)}, u32[]{:S(2)}, u32[]{:S(2)}) collective-permute-start(bf16[1280,128]{1,0:T(8,128)(2,1)} %join.10.refs_0_), channel_id=1, source_target_pairs={{0,2},{1,3},{2,0},{3,1},{4,6},{5,7},{6,4},{7,5},{8,10},{9,11},{10,... | collective-permute-start | bytes 983048 | tf_op jit(solution)/shard_map/ppermute | solution.py:29
  349.9 31.3 %collective-permute-start.61 = (bf16[1280,128]{1,0:T(8,128)(2,1)S(1)}, bf16[1280,128]{1,0:T(8,128)(2,1)S(1)}, u32[]{:S(2)}, u32[]{:S(2)}) collective-permute-start(bf16[1280,128]{1,0:T(8,128)(2,1)S(1)} %copy-done.4), channel_id=1, source_target_pairs={{0,1},{1,0},{2,3},{3,2},{4,5},{5,4},{6,7},{7,6},{8,9},{9,8},{10,11... | collective-permute-start | bytes 983048 | tf_op jit(solution)/shard_map/ppermute | solution.py:29
  352.4 41.4 %collective-permute-start.48 = (bf16[1280,128]{1,0:T(8,128)(2,1)S(1)}, bf16[1280,128]{1,0:T(8,128)(2,1)S(1)}, u32[]{:S(2)}, u32[]{:S(2)}) collective-permute-start(bf16[1280,128]{1,0:T(8,128)(2,1)S(1)} %copy-done.1), channel_id=1, source_target_pairs={{0,1},{1,0},{2,3},{3,2},{4,5},{5,4},{6,7},{7,6},{8,9},{9,8},{10,11... | collective-permute-start | bytes 983048 | tf_op jit(solution)/shard_map/ppermute | solution.py:29
  362.4 19.3 %collective-permute-start.63 = (bf16[1280,128]{1,0:T(8,128)(2,1)}, bf16[1280,128]{1,0:T(8,128)(2,1)S(1)}, u32[]{:S(2)}, u32[]{:S(2)}) collective-permute-start(bf16[1280,128]{1,0:T(8,128)(2,1)} %collective-permute-done.62.refs_2_), channel_id=1, source_target_pairs={{0,1},{1,0},{2,3},{3,2},{4,5},{5,4},{6,7},{7,6},{8,9},{9,8},{10,11... | collective-permute-start | bytes 983048 | tf_op jit(solution)/shard_map/ppermute | solution.py:29
  365.8 28.0 %collective-permute-start.50 = (bf16[1280,128]{1,0:T(8,128)(2,1)S(1)}, bf16[1280,128]{1,0:T(8,128)(2,1)S(1)}, u32[]{:S(2)}, u32[]{:S(2)}) collective-permute-start(bf16[1280,128]{1,0:T(8,128)(2,1)S(1)} %collective-permute-done.49.refs_2_), channel_id=1, source_target_pairs={{0,1},{1,0},{2,3},{3,2},{4,5},{5,4},{6,7},{7,6},{8,9},{9,8},{10,11... | collective-permute-start | bytes 983048 | tf_op jit(solution)/shard_map/ppermute | solution.py:29
  391.5 31.1 %collective-permute-start.67 = (f32[32,1280]{1,0:T(8,128)}, f32[32,1280]{1,0:T(8,128)S(1)}, u32[]{:S(2)}, u32[]{:S(2)}) collective-permute-start(f32[32,1280]{1,0:T(8,128)} %get-tuple-element.132), channel_id=1, source_target_pairs={{0,4},{4,8},{8,12},{12,0},{1,5},{5,9},{9,13},{13,1},{2,6},{6,10},{... | collective-permute-start | bytes 491528 | tf_op jit(solution)/shard_map/ppermute | solution.py:23
  391.5 32.6 %collective-permute-start.68 = (f32[32,1280]{1,0:T(8,128)}, f32[32,1280]{1,0:T(8,128)S(1)}, u32[]{:S(2)}, u32[]{:S(2)}) collective-permute-start(f32[32,1280]{1,0:T(8,128)} %get-tuple-element.133), channel_id=1, source_target_pairs={{0,8},{4,12},{8,0},{12,4},{1,9},{5,13},{9,1},{13,5},{2,10},{6,14},... | collective-permute-start | bytes 491528 | tf_op jit(solution)/shard_map/ppermute | solution.py:23
  392.4 31.6 %collective-permute-start.69 = (f32[32,1280]{1,0:T(8,128)}, f32[32,1280]{1,0:T(8,128)S(1)}, u32[]{:S(2)}, u32[]{:S(2)}) collective-permute-start(f32[32,1280]{1,0:T(8,128)} %get-tuple-element.134), channel_id=1, source_target_pairs={{0,12},{4,0},{8,4},{12,8},{1,13},{5,1},{9,5},{13,9},{2,14},{6,2},{... | collective-permute-start | bytes 491528 | tf_op jit(solution)/shard_map/ppermute | solution.py:23
  404.0 20.1 %collective-permute-start.64 = (f32[32,1280]{1,0:T(8,128)}, f32[32,1280]{1,0:T(8,128)S(1)}, u32[]{:S(2)}, u32[]{:S(2)}) collective-permute-start(f32[32,1280]{1,0:T(8,128)} %get-tuple-element.128), channel_id=1, source_target_pairs={{0,4},{4,8},{8,12},{12,0},{1,5},{5,9},{9,13},{13,1},{2,6},{6,10},{... | collective-permute-start | bytes 491528 | tf_op jit(solution)/shard_map/ppermute | solution.py:23
  404.1 20.1 %collective-permute-start.65 = (f32[32,1280]{1,0:T(8,128)}, f32[32,1280]{1,0:T(8,128)S(1)}, u32[]{:S(2)}, u32[]{:S(2)}) collective-permute-start(f32[32,1280]{1,0:T(8,128)} %get-tuple-element.129), channel_id=1, source_target_pairs={{0,8},{4,12},{8,0},{12,4},{1,9},{5,13},{9,1},{13,5},{2,10},{6,14},... | collective-permute-start | bytes 491528 | tf_op jit(solution)/shard_map/ppermute | solution.py:23
  (83 other events, 557.8 us)

commit v3 on v2

--- a/solution.py
+++ b/solution.py
@@ -13,6 +13,7 @@
 REST_PIECE = 1280
 BACK_PIECE = 640
 HID_SENT_AS = jnp.float32
+LANES = 128
 
 
 def exchange(blocks, axis):
@@ -316,41 +317,96 @@
     return [refs[i : i + sections] for i in range(0, len(refs), sections)]
 
 
-def first_kernel(sections, place_ref, inputs_ref, *refs):
-    candidates, (out_ref, grads_ref) = grouped(refs[:-2], sections), refs[-2:]
-
-    def write(c, ref):
-        rows = ref.shape[1]
-        grads_ref[:, c * rows : (c + 1) * rows] = ref[...]
-
-    pick(place_ref, candidates, write)
+def first_kernel(sections, masks, table_ref, inputs_ref, *refs):
+    out_ref, grads_ref = refs[-2:]
+    late = refs[: len(masks)]
+    candidates = grouped(refs[len(masks) : -2], sections)
+    rows = late[0].shape[1]
+
+    for c, by_section in enumerate(candidates):
+        for s, ref in enumerate(by_section):
+            if (c, s) == (len(candidates) - 1, 0):
+                for k, last_ref in enumerate(late):
+
+                    @pl.when((table_ref[0] == s) & (pl.program_id(0) == k))
+                    def _(c=c, last_ref=last_ref):
+                        grads_ref[:, c * rows : (c + 1) * rows] = last_ref[...]
+
+            else:
+
+                @pl.when(table_ref[0] == s)
+                def _(c=c, ref=ref):
+                    grads_ref[:, c * rows : (c + 1) * rows] = ref[...]
+
     out_ref[...] = dot(inputs_ref[...], grads_ref[...], 1, 1)
 
 
-def first_gradient(place, inputs_t, candidates):
+def more_first_kernel(sections, masks, table_ref, so_far_ref, *refs):
+    first_kernel(sections, masks, table_ref, *refs)
+
+
+def first_gradient(table, places, masks, inputs_t, last, candidates, so_far=None):
     width, rows = inputs_t.shape
     sections = len(candidates[0])
     hidden, chunk_rows = candidates[0][0].shape
-    piece = piece_of(hidden, 640)
-
-    def only_on(section):
-        return pl.BlockSpec((piece, chunk_rows), lambda n, s: (jnp.where(s[0] == section, n, 0), 0))
-
+    columns = last[0].shape[0]
+    piece = piece_of(columns, 640)
+    if piece % 128:
+        piece = columns
+    pieces = columns // piece
+
+    def block_of(k, s):
+        block = s[places.by_mask + masks[0]]
+        for i, m in enumerate(masks[1:], 1):
+            block = jnp.where(k == i, s[places.by_mask + m], block)
+        return block
+
+    def only_on(section, unused):
+        def index(k, c, s):
+            here = block_of(k, s) * pieces + c
+            return (0 if unused else jnp.where(s[0] == section, here, 0), 0)
+
+        return pl.BlockSpec((piece, chunk_rows), index)
+
+    def late_at(own_step):
+        return pl.BlockSpec((piece, chunk_rows), lambda k, c, s: (jnp.where(k == own_step, c, 0), 0))
+
+    earlier = [] if so_far is None else [so_far]
+    kernel = first_kernel if so_far is None else more_first_kernel
     grid_spec = pltpu.PrefetchScalarGridSpec(
         num_scalar_prefetch=1,
-        grid=(hidden // piece,),
-        in_specs=[pl.BlockSpec((width, rows), lambda n, s: (0, 0))]
-        + [only_on(s) for _ in candidates for s in range(sections)],
-        out_specs=pl.BlockSpec((width, piece), lambda n, s: (0, n)),
+        grid=(len(masks), pieces),
+        in_specs=[pl.BlockSpec(memory_space=pl.ANY) for _ in earlier]
+        + [pl.BlockSpec((width, rows), lambda k, c, s: (0, 0))]
+        + [late_at(k) for k in range(len(masks))]
+        + [
+            only_on(s, (c, s) == (len(candidates) - 1, 0))
+            for c in range(len(candidates))
+            for s in range(sections)
+        ],
+        out_specs=pl.BlockSpec((width, piece), lambda k, c, s: (0, block_of(k, s) * pieces + c)),
         scratch_shapes=[pltpu.VMEM((piece, rows), jnp.bfloat16)],
     )
+    share = len(masks) * columns
     return pl.pallas_call(
-        functools.partial(first_kernel, sections),
+        functools.partial(kernel, sections, masks),
         grid_spec=grid_spec,
         out_shape=jax.ShapeDtypeStruct((width, hidden), jnp.float32),
-        cost_estimate=estimate(2 * rows * width * hidden, 4 * width * hidden),
+        input_output_aliases={} if so_far is None else {1: 0},
+        cost_estimate=estimate(2 * rows * width * share, 4 * width * share),
         name="first_gradient",
-    )(place, inputs_t, *[a for by_section in candidates for a in by_section])
+    )(
+        table,
+        *earlier,
+        inputs_t,
+        *[last[m] for m in masks],
+        *[a for by_section in candidates for a in by_section],
+    )
+
+
+def whole_first_gradient(inputs_t, section, candidates):
+    grads = jnp.concatenate([lax.select_n(section, *by_section) for by_section in candidates], axis=1)
+    return dot(inputs_t, grads, 1, 1)
 
 
 def second_kernel(sections, place_ref, hidden_ref, *refs):
@@ -408,6 +464,7 @@
     weight_second = w_second[0]
     micro, rows, width = cotangent.shape
     hidden = saved_hidden.shape[-1]
+    columns = hidden // wids
     sub = rows // hids // SUB_CHUNKS
     chunks = micro * SUB_CHUNKS
     periods = chunks + LAG * (sections - 1)
@@ -460,7 +517,17 @@
         ]
 
     grad_second = second_gradient(table, hidden_t, by_chunk(incoming))
-    grad_first = first_gradient(table, inputs_t, by_chunk(grads))
+    if columns % LANES:
+        grad_first = whole_first_gradient(inputs_t, section, by_chunk(grads))
+    else:
+        earlier = by_chunk(grads)
+        earlier[-1][0] = grads[0]
+        early = first_gradient(
+            table, places, list(range(0, wids, 2)), inputs_t, gathered, earlier
+        )
+        grad_first = first_gradient(
+            table, places, list(range(1, wids, 2)), inputs_t, gathered, earlier, early
+        )
     input_grads = jnp.stack(
         [lax.select_n(section, *by_section) if sections > 1 else by_section[0]
          for by_section in by_chunk(results)]

time: 436 us -> 469 us (1.076)
  waiting for transfers between devices: 140 us -> 188 us
  starting transfers between devices: 71.6 us -> 55.9 us
  Pallas kernels: 177 us -> 182 us
    ppermute x36, waiting for transfers between devices: 114 us -> 170 us  [swap(): return lax.ppermute(block, axis, pairs)]
    ppermute x16, waiting for transfers between devices: 15.3 us -> 3.9 us  [hand_down(): arrived.append(lax.ppermute(share, ('section', 'hid'), pairs))]
    ppermute x36, starting transfers between devices: 34.2 us -> 23.6 us  [swap(): return lax.ppermute(block, axis, pairs)]
    ppermute x18, starting transfers between devices: 16.3 us -> 11.3 us  [exchange(): arrived.append(lax.ppermute(blocks[shift - 1], axis, pairs))]
    pallas_call x1 -> x2, Pallas kernels: 17.3 us -> 21.6 us  [first_gradient(): pl.pallas_call(functools.partial(kernel, sections, masks), grid_spec=grid...]
  transfers between devices with their start and end apart: 70 -> 70, of which waited for: 27 -> 30; matrix products, arithmetic and copies ran while one was open for 5% -> 4% of each run, Pallas kernels for 40% -> 38%
where the time goes in v3:
time: 469 us; the launch traced here: 464 us
  waiting for transfers between devices  188 us (40%)
  Pallas kernels  182 us (39%)
  starting transfers between devices  55.9 us (12%)
  local copies, waits for them, and re-layouts  29.2 us (6%)
  other arithmetic  7.34 us (2%)
    ppermute x36, waiting for transfers between devices, swap(): return lax.ppermute(block, axis, pairs)  170 us
    pallas_call x6, Pallas kernels, back(): pl.pallas_call(functools.partial(back_kernel, count, hids, places), grid_...  52.9 us
    pallas_call x6, Pallas kernels, rest(): pl.pallas_call(rest_kernel, grid_spec=grid_spec, out_shape=[jax.ShapeDtyp...  47.6 us
    pallas_call x6, Pallas kernels, project(): pl.pallas_call(functools.partial(project_kernel, hids, at, places.senders...  26.9 us
    ppermute x36, starting transfers between devices, swap(): return lax.ppermute(block, axis, pairs)  23.6 us
    pallas_call x2, Pallas kernels, first_gradient(): pl.pallas_call(functools.partial(kernel, sections, masks), grid_spec=grid...  21.6 us
    ppermute x16, starting transfers between devices, hand_down(): arrived.append(lax.ppermute(share, ('section', 'hid'), pairs))  21 us
    pallas_call x6, Pallas kernels, join(): pl.pallas_call(join_kernel, grid_spec=grid_spec, out_shape=jax.ShapeDtype...  17.7 us
  transfers between devices with their start and end apart: 70, of which 30 were waited for; matrix products, arithmetic and copies ran while one was open for 4% of the time, Pallas kernels for 38%

profile of v3, /device:TPU:0, one launch (start us, length us, event | category | flops | bytes accessed | tf_op | source)
XLA Modules:
  0.0 463.7 jit_solution(14834068378050356609)
XLA Ops:
  2.8 4.8 %project.9 = (bf16[1280,128]{1,0:T(8,128)(2,1)}, bf16[1280,128]{1,0:T(8,128)(2,1)}, bf16[128,1280]{1,0:T(8,128)(2,1)}) custom-call(s32[42]{0:T(128)} %concatenate.3.table_ref.place_ref, bf16[2,4,2,32,1280]{4,3,2,1,0:T(8,128)(2,1)} %bitcast.43, bf16[32,1280]{1,0:T(8,128)(2,1)} %broadcast_in_dim.19.refs_0_.refs_1_.refs_2_.refs_3_, ...), custom_call_target="tpu_custom_call" | custom-call | flops 419430400 | bytes 3276800 | tf_op jit(solution)/shard_map/project/pallas_call | solution.py:159
  7.6 3.1 collective-permute-start.31
  10.7 4.8 %project.6 = (bf16[1280,128]{1,0:T(8,128)(2,1)}, bf16[1280,128]{1,0:T(8,128)(2,1)}, bf16[128,1280]{1,0:T(8,128)(2,1)}) custom-call(s32[42]{0:T(128)} %concatenate.3.table_ref.place_ref, bf16[2,4,2,32,1280]{4,3,2,1,0:T(8,128)(2,1)} %bitcast.44, bf16[32,1280]{1,0:T(8,128)(2,1)} %broadcast_in_dim.19.refs_0_.refs_1_.refs_2_.refs_3_, ...), custom_call_target="tpu_custom_call" | custom-call | flops 419430400 | bytes 3276800 | tf_op jit(solution)/shard_map/project/pallas_call | solution.py:159
  15.5 8.0 %rest.6 = (bf16[1280,128]{1,0:T(8,128)(2,1)}, f32[1280,128]{1,0:T(8,128)}, f32[1280,128]{1,0:T(8,128)}) custom-call(s32[42]{0:T(128)} %concatenate.3.table_ref.place_ref, bf16[1280,128]{1,0:T(8,128)(2,1)} %get-tuple-element.68.turned_ref, bf16[5120,1280]{1,0:T(8,128)(2,1)} %bitcast.26), custom_call_target="tpu_custom_call" | custom-call | flops 1258291200 | bytes 9830400 | tf_op jit(solution)/shard_map/rest/pallas_call | solution.py:205
  25.5 7.9 %rest.9 = (bf16[1280,128]{1,0:T(8,128)(2,1)}, f32[1280,128]{1,0:T(8,128)}, f32[1280,128]{1,0:T(8,128)}) custom-call(s32[42]{0:T(128)} %concatenate.3.table_ref.place_ref, bf16[1280,128]{1,0:T(8,128)(2,1)} %get-tuple-element.91.turned_ref, bf16[5120,1280]{1,0:T(8,128)(2,1)} %bitcast.27), custom_call_target="tpu_custom_call" | custom-call | flops 1258291200 | bytes 9830400 | tf_op jit(solution)/shard_map/rest/pallas_call | solution.py:205
  37.5 10.8 %collective-permute-done.1 = bf16[1280,128]{1,0:T(8,128)(2,1)S(1)} collective-permute-done((bf16[1280,128]{1,0:T(8,128)(2,1)S(1)}, bf16[1280,128]{1,0:T(8,128)(2,1)S(1)}, u32[]{:S(2)}, u32[]{:S(2)}) %collective-permute-start.1) | collective-permute-done | bytes 327712 | tf_op jit(solution)/shard_map/ppermute | solution.py:30
  49.8 5.3 %copy.22 = bf16[5120,2,2,4,32]{0,4,3,2,1:T(8,128)(2,1)} copy(bf16[5120,2,2,4,32]{0,4,2,3,1:T(8,128)(2,1)} %bitcast.51) | data formatting | bytes 10485760 | tf_op jit(solution)/shard_map/transpose | solution.py:451
  55.1 7.9 %copy.23.refs_2_.hidden_ref = bf16[5120,512]{1,0:T(8,128)(2,1)} copy(bf16[5120,512]{0,1:T(8,128)(2,1)} %bitcast.50) | data formatting | bytes 10485760 | tf_op jit(solution)/shard_map/reshape | solution.py:451
  68.3 12.8 %collective-permute-done.2.refs_1_ = bf16[1280,128]{1,0:T(8,128)(2,1)S(1)} collective-permute-done((bf16[1280,128]{1,0:T(8,128)(2,1)S(1)}, bf16[1280,128]{1,0:T(8,128)(2,1)S(1)}, u32[]{:S(2)}, u32[]{:S(2)}) %collective-permute-start.2) | collective-permute-done | bytes 327712 | tf_op jit(solution)/shard_map/ppermute | solution.py:30
  85.0 6.1 %collective-permute-done.34.refs_2_ = bf16[1280,128]{1,0:T(8,128)(2,1)S(1)} collective-permute-done((bf16[1280,128]{1,0:T(8,128)(2,1)}, bf16[1280,128]{1,0:T(8,128)(2,1)S(1)}, u32[]{:S(2)}, u32[]{:S(2)}) %collective-permute-start.34) | collective-permute-done | bytes 327712 | tf_op jit(solution)/shard_map/ppermute | solution.py:30
  93.1 4.4 collective-permute-done.4.refs_2_
  97.6 6.8 %collective-permute-done.33.refs_1_ = bf16[1280,128]{1,0:T(8,128)(2,1)S(1)} collective-permute-done((bf16[1280,128]{1,0:T(8,128)(2,1)S(1)}, bf16[1280,128]{1,0:T(8,128)(2,1)S(1)}, u32[]{:S(2)}, u32[]{:S(2)}) %collective-permute-start.33) | collective-permute-done | bytes 327712 | tf_op jit(solution)/shard_map/ppermute | solution.py:30
  104.4 7.0 %collective-permute-done.35.refs_3_ = bf16[1280,128]{1,0:T(8,128)(2,1)S(1)} collective-permute-done((bf16[1280,128]{1,0:T(8,128)(2,1)S(1)}, bf16[1280,128]{1,0:T(8,128)(2,1)S(1)}, u32[]{:S(2)}, u32[]{:S(2)}) %collective-permute-start.35) | collective-permute-done | bytes 327712 | tf_op jit(solution)/shard_map/ppermute | solution.py:30
  112.1 8.8 %back.8 = (f32[32,1280]{1,0:T(8,128)}, f32[32,1280]{1,0:T(8,128)}, f32[32,1280]{1,0:T(8,128)}, f32[32,1280]{1,0:T(8,128)}, bf16[5120,128]{1,0:T(8,128)(2,1)}) custom-call(s32[42]{0:T(128)} %concatenate.3.table_ref.place_ref, bf16[1280,128]{1,0:T(8,128)(2,1)} %join.9.refs_0_, bf16[1280,128]{1,0:T(8,128)(2,1)} %copy-done.33, bf16[1280,128]{1,0:T(8,128)(2,1)} %copy-done.27, ...), custom_call_target="tpu_custom_call" | custom-call | flops 1677721600 | bytes 13107200 | tf_op jit(solution)/shard_map/back/pallas_call | solution.py:293
  124.2 8.8 %back.6 = (f32[32,1280]{1,0:T(8,128)}, f32[32,1280]{1,0:T(8,128)}, f32[32,1280]{1,0:T(8,128)}, f32[32,1280]{1,0:T(8,128)}, bf16[5120,128]{1,0:T(8,128)(2,1)}) custom-call(s32[42]{0:T(128)} %concatenate.3.table_ref.place_ref, bf16[1280,128]{1,0:T(8,128)(2,1)} %join.6.refs_0_, bf16[1280,128]{1,0:T(8,128)(2,1)} %copy-done.29, bf16[1280,128]{1,0:T(8,128)(2,1)} %copy-done.24, ...), custom_call_target="tpu_custom_call" | custom-call | flops 1677721600 | bytes 13107200 | tf_op jit(solution)/shard_map/back/pallas_call | solution.py:293
  151.8 4.3 project.10
  158.4 4.3 project.7
  162.7 8.0 %rest.7 = (bf16[1280,128]{1,0:T(8,128)(2,1)}, f32[1280,128]{1,0:T(8,128)}, f32[1280,128]{1,0:T(8,128)}) custom-call(s32[42]{0:T(128)} %concatenate.3.table_ref.place_ref, bf16[1280,128]{1,0:T(8,128)(2,1)} %get-tuple-element.77.turned_ref, bf16[5120,1280]{1,0:T(8,128)(2,1)} %bitcast.30), custom_call_target="tpu_custom_call" | custom-call | flops 1258291200 | bytes 9830400 | tf_op jit(solution)/shard_map/rest/pallas_call | solution.py:205
  172.7 7.8 %rest.10 = (bf16[1280,128]{1,0:T(8,128)(2,1)}, f32[1280,128]{1,0:T(8,128)}, f32[1280,128]{1,0:T(8,128)}) custom-call(s32[42]{0:T(128)} %concatenate.3.table_ref.place_ref, bf16[1280,128]{1,0:T(8,128)(2,1)} %get-tuple-element.100.turned_ref, bf16[5120,1280]{1,0:T(8,128)(2,1)} %bitcast.31), custom_call_target="tpu_custom_call" | custom-call | flops 1258291200 | bytes 9830400 | tf_op jit(solution)/shard_map/rest/pallas_call | solution.py:205
  182.9 9.0 %collective-permute-done.14 = bf16[1280,128]{1,0:T(8,128)(2,1)S(1)} collective-permute-done((bf16[1280,128]{1,0:T(8,128)(2,1)S(1)}, bf16[1280,128]{1,0:T(8,128)(2,1)S(1)}, u32[]{:S(2)}, u32[]{:S(2)}) %collective-permute-start.14) | collective-permute-done | bytes 327712 | tf_op jit(solution)/shard_map/ppermute | solution.py:30
  192.1 5.9 %collective-permute-done.43.refs_0_ = bf16[1280,128]{1,0:T(8,128)(2,1)S(1)} collective-permute-done((bf16[1280,128]{1,0:T(8,128)(2,1)}, bf16[1280,128]{1,0:T(8,128)(2,1)S(1)}, u32[]{:S(2)}, u32[]{:S(2)}) %collective-permute-start.43) | collective-permute-done | bytes 327712 | tf_op jit(solution)/shard_map/ppermute | solution.py:30
  198.0 16.8 %collective-permute-done.45.refs_1_ = bf16[1280,128]{1,0:T(8,128)(2,1)S(1)} collective-permute-done((bf16[1280,128]{1,0:T(8,128)(2,1)S(1)}, bf16[1280,128]{1,0:T(8,128)(2,1)S(1)}, u32[]{:S(2)}, u32[]{:S(2)}) %collective-permute-start.45) | collective-permute-done | bytes 327712 | tf_op jit(solution)/shard_map/ppermute | solution.py:30
  218.4 10.5 %collective-permute-done.15.refs_1_ = bf16[1280,128]{1,0:T(8,128)(2,1)S(1)} collective-permute-done((bf16[1280,128]{1,0:T(8,128)(2,1)S(1)}, bf16[1280,128]{1,0:T(8,128)(2,1)S(1)}, u32[]{:S(2)}, u32[]{:S(2)}) %collective-permute-start.15) | collective-permute-done | bytes 327712 | tf_op jit(solution)/shard_map/ppermute | solution.py:30
  229.6 3.0 join.7.refs_0_
  232.7 3.2 collective-permute-done.47.refs_2_
  237.9 3.2 collective-permute-done.17.refs_2_
  241.2 7.0 %collective-permute-done.46.refs_1_ = bf16[1280,128]{1,0:T(8,128)(2,1)S(1)} collective-permute-done((bf16[1280,128]{1,0:T(8,128)(2,1)S(1)}, bf16[1280,128]{1,0:T(8,128)(2,1)S(1)}, u32[]{:S(2)}, u32[]{:S(2)}) %collective-permute-start.46) | collective-permute-done | bytes 327712 | tf_op jit(solution)/shard_map/ppermute | solution.py:30
  248.2 7.0 %collective-permute-done.48.refs_3_ = bf16[1280,128]{1,0:T(8,128)(2,1)S(1)} collective-permute-done((bf16[1280,128]{1,0:T(8,128)(2,1)S(1)}, bf16[1280,128]{1,0:T(8,128)(2,1)S(1)}, u32[]{:S(2)}, u32[]{:S(2)}) %collective-permute-start.48) | collective-permute-done | bytes 327712 | tf_op jit(solution)/shard_map/ppermute | solution.py:30
  256.0 8.8 %back.9 = (f32[32,1280]{1,0:T(8,128)}, f32[32,1280]{1,0:T(8,128)}, f32[32,1280]{1,0:T(8,128)}, f32[32,1280]{1,0:T(8,128)}, bf16[5120,128]{1,0:T(8,128)(2,1)}) custom-call(s32[42]{0:T(128)} %concatenate.3.table_ref.place_ref, bf16[1280,128]{1,0:T(8,128)(2,1)} %join.10.refs_0_, bf16[1280,128]{1,0:T(8,128)(2,1)} %copy-done.34, bf16[1280,128]{1,0:T(8,128)(2,1)} %copy-done.28, ...), custom_call_target="tpu_custom_call" | custom-call | flops 1677721600 | bytes 13107200 | tf_op jit(solution)/shard_map/back/pallas_call | solution.py:293
  269.9 8.8 %back.7 = (f32[32,1280]{1,0:T(8,128)}, f32[32,1280]{1,0:T(8,128)}, f32[32,1280]{1,0:T(8,128)}, f32[32,1280]{1,0:T(8,128)}, bf16[5120,128]{1,0:T(8,128)(2,1)}) custom-call(s32[42]{0:T(128)} %concatenate.3.table_ref.place_ref, bf16[1280,128]{1,0:T(8,128)(2,1)} %join.7.refs_0_, bf16[1280,128]{1,0:T(8,128)(2,1)} %copy-done.30, bf16[1280,128]{1,0:T(8,128)(2,1)} %copy-done.25, ...), custom_call_target="tpu_custom_call" | custom-call | flops 1677721600 | bytes 13107200 | tf_op jit(solution)/shard_map/back/pallas_call | solution.py:293
  284.9 4.1 collective-permute-done.20
  297.9 4.3 project.11
  304.8 4.3 project.8
  309.1 8.0 %rest.8 = (bf16[1280,128]{1,0:T(8,128)(2,1)}, f32[1280,128]{1,0:T(8,128)}, f32[1280,128]{1,0:T(8,128)}) custom-call(s32[42]{0:T(128)} %concatenate.3.table_ref.place_ref, bf16[1280,128]{1,0:T(8,128)(2,1)} %get-tuple-element.86.turned_ref, bf16[5120,1280]{1,0:T(8,128)(2,1)} %bitcast.34), custom_call_target="tpu_custom_call" | custom-call | flops 1258291200 | bytes 9830400 | tf_op jit(solution)/shard_map/rest/pallas_call | solution.py:205
  319.1 7.9 %rest.11 = (bf16[1280,128]{1,0:T(8,128)(2,1)}, f32[1280,128]{1,0:T(8,128)}, f32[1280,128]{1,0:T(8,128)}) custom-call(s32[42]{0:T(128)} %concatenate.3.table_ref.place_ref, bf16[1280,128]{1,0:T(8,128)(2,1)} %get-tuple-element.113.turned_ref, bf16[5120,1280]{1,0:T(8,128)(2,1)} %bitcast.35), custom_call_target="tpu_custom_call" | custom-call | flops 1258291200 | bytes 9830400 | tf_op jit(solution)/shard_map/rest/pallas_call | solution.py:205
  329.0 10.4 %collective-permute-done.27 = bf16[1280,128]{1,0:T(8,128)(2,1)S(1)} collective-permute-done((bf16[1280,128]{1,0:T(8,128)(2,1)S(1)}, bf16[1280,128]{1,0:T(8,128)(2,1)S(1)}, u32[]{:S(2)}, u32[]{:S(2)}) %collective-permute-start.27) | collective-permute-done | bytes 327712 | tf_op jit(solution)/shard_map/ppermute | solution.py:30
  339.5 6.7 %collective-permute-done.56.refs_0_ = bf16[1280,128]{1,0:T(8,128)(2,1)S(1)} collective-permute-done((bf16[1280,128]{1,0:T(8,128)(2,1)}, bf16[1280,128]{1,0:T(8,128)(2,1)S(1)}, u32[]{:S(2)}, u32[]{:S(2)}) %collective-permute-start.56) | collective-permute-done | bytes 327712 | tf_op jit(solution)/shard_map/ppermute | solution.py:30
  346.3 15.3 %collective-permute-done.58.refs_1_ = bf16[1280,128]{1,0:T(8,128)(2,1)S(1)} collective-permute-done((bf16[1280,128]{1,0:T(8,128)(2,1)S(1)}, bf16[1280,128]{1,0:T(8,128)(2,1)S(1)}, u32[]{:S(2)}, u32[]{:S(2)}) %collective-permute-start.58) | collective-permute-done | bytes 327712 | tf_op jit(solution)/shard_map/ppermute | solution.py:30
  365.2 3.4 collective-permute-done.28.refs_1_
  376.0 8.0 %collective-permute-done.60.refs_2_ = bf16[1280,128]{1,0:T(8,128)(2,1)} collective-permute-done((bf16[1280,128]{1,0:T(8,128)(2,1)}, bf16[1280,128]{1,0:T(8,128)(2,1)}, u32[]{:S(2)}, u32[]{:S(2)}) %collective-permute-start.60) | collective-permute-done | bytes 327712 | tf_op jit(solution)/shard_map/ppermute | solution.py:30
  384.1 4.4 collective-permute-done.29.refs_1_.refs_2_
  388.6 15.3 %second_gradient.1 = f32[5120,1280]{1,0:T(8,128)} custom-call(s32[42]{0:T(128)} %concatenate.3.table_ref.place_ref, bf16[5120,512]{1,0:T(8,128)(2,1)} %copy.23.refs_2_.hidden_ref, bf16[128,1280]{1,0:T(8,128)(2,1)} %get-tuple-element.119.refs_0_.refs_5_, bf16[128,1280]{1,0:T(8,128)(2,1)} %get-tuple-element.120.refs_1_, ...), custom_call_target="tpu_custom_call" | custom-call | flops 6710886400 | bytes 26214400 | tf_op jit(solution)/shard_map/second_gradient/pallas_call | solution.py:441
  404.0 8.8 %collective-permute-done.63.refs_2_.refs_3_ = bf16[1280,128]{1,0:T(8,128)(2,1)S(1)} collective-permute-done((bf16[1280,128]{1,0:T(8,128)(2,1)S(1)}, bf16[1280,128]{1,0:T(8,128)(2,1)S(1)}, u32[]{:S(2)}, u32[]{:S(2)}) %collective-permute-start.63) | collective-permute-done | bytes 327712 | tf_op jit(solution)/shard_map/ppermute | solution.py:30
  413.5 8.8 %back.11 = (f32[32,1280]{1,0:T(8,128)}, f32[32,1280]{1,0:T(8,128)}, f32[32,1280]{1,0:T(8,128)}, f32[32,1280]{1,0:T(8,128)}, bf16[5120,128]{1,0:T(8,128)(2,1)}) custom-call(s32[42]{0:T(128)} %concatenate.3.table_ref.place_ref, bf16[1280,128]{1,0:T(8,128)(2,1)} %join.8.refs_0_, bf16[1280,128]{1,0:T(8,128)(2,1)} %copy-done.2, bf16[1280,128]{1,0:T(8,128)(2,1)} %copy-done.1, ...), custom_call_target="tpu_custom_call" | custom-call | flops 1677721600 | bytes 13107200 | tf_op jit(solution)/shard_map/back/pallas_call | solution.py:293
  425.2 8.8 %back.10 = (f32[32,1280]{1,0:T(8,128)}, f32[32,1280]{1,0:T(8,128)}, f32[32,1280]{1,0:T(8,128)}, f32[32,1280]{1,0:T(8,128)}, bf16[5120,128]{1,0:T(8,128)(2,1)}) custom-call(s32[42]{0:T(128)} %concatenate.3.table_ref.place_ref, bf16[1280,128]{1,0:T(8,128)(2,1)} %join.11.refs_0_, bf16[1280,128]{1,0:T(8,128)(2,1)} %copy-done.23, ...), custom_call_target="tpu_custom_call" | custom-call | flops 1677721600 | bytes 13107200 | tf_op jit(solution)/shard_map/back/pallas_call | solution.py:293
  436.5 10.7 %first_gradient.2.so_far_ref = f32[1280,5120]{1,0:T(8,128)} custom-call(s32[42]{0:T(128)} %concatenate.3.table_ref.place_ref, bf16[1280,512]{1,0:T(8,128)(2,1)} %copy.29.inputs_ref.refs_0_, bf16[1280,128]{1,0:T(8,128)(2,1)} %join.8.refs_0_, bf16[1280,128]{1,0:T(8,128)(2,1)} %copy-done.1, ...), custom_call_target="tpu_custom_call" | custom-call | flops 3355443200 | bytes 13107200 | tf_op jit(solution)/shard_map/first_gradient/pallas_call | solution.py:391
  447.2 10.9 %first_gradient.3 = f32[1280,5120]{1,0:T(8,128)} custom-call(s32[42]{0:T(128)} %concatenate.3.table_ref.place_ref, f32[1280,5120]{1,0:T(8,128)} %first_gradient.2.so_far_ref, bf16[1280,512]{1,0:T(8,128)(2,1)} %copy.29.inputs_ref.refs_0_, bf16[1280,128]{1,0:T(8,128)(2,1)} %copy-done.2, bf16[1280,128]{1,0:T(8,128)(2,1)} %copy-done.3, ...), custom_call_target="tpu_custom_call", output_to_operand_aliasing={{}: (1, {})} | custom-call | flops 3355443200 | bytes 13107200 | tf_op jit(solution)/shard_map/first_gradient/pallas_call | solution.py:391
  458.2 4.6 collective-permute-done.64
  (268 shorter events, 102.3 us)
Async XLA Ops:
  7.6 25.8 %collective-permute-start.31 = (bf16[1280,128]{1,0:T(8,128)(2,1)}, bf16[1280,128]{1,0:T(8,128)(2,1)S(1)}, u32[]{:S(2)}, u32[]{:S(2)}) collective-permute-start(bf16[1280,128]{1,0:T(8,128)(2,1)} %get-tuple-element.95), channel_id=1, source_target_pairs={{0,1},{1,0},{2,3},{3,2},{4,5},{5,4},{6,7},{7,6},{8,9},{9,8},{10,11... | collective-permute-start | bytes 983048 | tf_op jit(solution)/shard_map/ppermute | solution.py:30
  23.5 44.9 %collective-permute-start = (bf16[1280,128]{1,0:T(8,128)(2,1)}, bf16[1280,128]{1,0:T(8,128)(2,1)S(1)}, u32[]{:S(2)}, u32[]{:S(2)}) collective-permute-start(bf16[1280,128]{1,0:T(8,128)(2,1)} %get-tuple-element.70), channel_id=1, source_target_pairs={{0,1},{1,0},{2,3},{3,2},{4,5},{5,4},{6,7},{7,6},{8,9},{9,8},{10,11... | collective-permute-start | bytes 983048 | tf_op jit(solution)/shard_map/ppermute | solution.py:30
  23.5 24.8 %collective-permute-start.1 = (bf16[1280,128]{1,0:T(8,128)(2,1)S(1)}, bf16[1280,128]{1,0:T(8,128)(2,1)S(1)}, u32[]{:S(2)}, u32[]{:S(2)}) collective-permute-start(bf16[1280,128]{1,0:T(8,128)(2,1)S(1)} %copy-done.59), channel_id=1, source_target_pairs={{0,1},{1,0},{2,3},{3,2},{4,5},{5,4},{6,7},{7,6},{8,9},{9,8},{10,11... | collective-permute-start | bytes 983048 | tf_op jit(solution)/shard_map/ppermute | solution.py:30
  33.3 29.7 %collective-permute-start.30 = (bf16[1280,128]{1,0:T(8,128)(2,1)}, bf16[1280,128]{1,0:T(8,128)(2,1)S(1)}, u32[]{:S(2)}, u32[]{:S(2)}) collective-permute-start(bf16[1280,128]{1,0:T(8,128)(2,1)} %get-tuple-element.93), channel_id=1, source_target_pairs={{0,1},{1,0},{2,3},{3,2},{4,5},{5,4},{6,7},{7,6},{8,9},{9,8},{10,11... | collective-permute-start | bytes 983048 | tf_op jit(solution)/shard_map/ppermute | solution.py:30
  34.6 28.4 %collective-permute-start.32 = (bf16[1280,128]{1,0:T(8,128)(2,1)S(1)}, bf16[1280,128]{1,0:T(8,128)(2,1)S(1)}, u32[]{:S(2)}, u32[]{:S(2)}) collective-permute-start(bf16[1280,128]{1,0:T(8,128)(2,1)S(1)} %add_convert_fusion.2), channel_id=1, source_target_pairs={{0,2},{1,3},{2,0},{3,1},{4,6},{5,7},{6,4},{7,5},{8,10},{9,11},{10,... | collective-permute-start | bytes 983048 | tf_op jit(solution)/shard_map/ppermute | solution.py:30
  48.4 32.8 %collective-permute-start.2 = (bf16[1280,128]{1,0:T(8,128)(2,1)S(1)}, bf16[1280,128]{1,0:T(8,128)(2,1)S(1)}, u32[]{:S(2)}, u32[]{:S(2)}) collective-permute-start(bf16[1280,128]{1,0:T(8,128)(2,1)S(1)} %add_convert_fusion.5), channel_id=1, source_target_pairs={{0,2},{1,3},{2,0},{3,1},{4,6},{5,7},{6,4},{7,5},{8,10},{9,11},{10,... | collective-permute-start | bytes 983048 | tf_op jit(solution)/shard_map/ppermute | solution.py:30
  66.8 24.3 %collective-permute-start.34 = (bf16[1280,128]{1,0:T(8,128)(2,1)}, bf16[1280,128]{1,0:T(8,128)(2,1)S(1)}, u32[]{:S(2)}, u32[]{:S(2)}) collective-permute-start(bf16[1280,128]{1,0:T(8,128)(2,1)} %join.9.refs_0_), channel_id=1, source_target_pairs={{0,2},{1,3},{2,0},{3,1},{4,6},{5,7},{6,4},{7,5},{8,10},{9,11},{10,... | collective-permute-start | bytes 983048 | tf_op jit(solution)/shard_map/ppermute | solution.py:30
  84.9 12.6 %collective-permute-start.4 = (bf16[1280,128]{1,0:T(8,128)(2,1)}, bf16[1280,128]{1,0:T(8,128)(2,1)S(1)}, u32[]{:S(2)}, u32[]{:S(2)}) collective-permute-start(bf16[1280,128]{1,0:T(8,128)(2,1)} %join.6.refs_0_), channel_id=1, source_target_pairs={{0,2},{1,3},{2,0},{3,1},{4,6},{5,7},{6,4},{7,5},{8,10},{9,11},{10,... | collective-permute-start | bytes 983048 | tf_op jit(solution)/shard_map/ppermute | solution.py:30
  84.9 19.5 %collective-permute-start.33 = (bf16[1280,128]{1,0:T(8,128)(2,1)S(1)}, bf16[1280,128]{1,0:T(8,128)(2,1)S(1)}, u32[]{:S(2)}, u32[]{:S(2)}) collective-permute-start(bf16[1280,128]{1,0:T(8,128)(2,1)S(1)} %copy-done.6), channel_id=1, source_target_pairs={{0,1},{1,0},{2,3},{3,2},{4,5},{5,4},{6,7},{7,6},{8,9},{9,8},{10,11... | collective-permute-start | bytes 983048 | tf_op jit(solution)/shard_map/ppermute | solution.py:30
  91.1 20.3 %collective-permute-start.35 = (bf16[1280,128]{1,0:T(8,128)(2,1)S(1)}, bf16[1280,128]{1,0:T(8,128)(2,1)S(1)}, u32[]{:S(2)}, u32[]{:S(2)}) collective-permute-start(bf16[1280,128]{1,0:T(8,128)(2,1)S(1)} %collective-permute-done.34.refs_2_), channel_id=1, source_target_pairs={{0,1},{1,0},{2,3},{3,2},{4,5},{5,4},{6,7},{7,6},{8,9},{9,8},{10,11... | collective-permute-start | bytes 983048 | tf_op jit(solution)/shard_map/ppermute | solution.py:30
  91.1 31.6 %collective-permute-start.3 = (bf16[1280,128]{1,0:T(8,128)(2,1)}, bf16[1280,128]{1,0:T(8,128)(2,1)S(1)}, u32[]{:S(2)}, u32[]{:S(2)}) collective-permute-start(bf16[1280,128]{1,0:T(8,128)(2,1)} %join.6.refs_0_), channel_id=1, source_target_pairs={{0,1},{1,0},{2,3},{3,2},{4,5},{5,4},{6,7},{7,6},{8,9},{9,8},{10,11... | collective-permute-start | bytes 983048 | tf_op jit(solution)/shard_map/ppermute | solution.py:30
  97.6 25.2 %collective-permute-start.5 = (bf16[1280,128]{1,0:T(8,128)(2,1)S(1)}, bf16[1280,128]{1,0:T(8,128)(2,1)S(1)}, u32[]{:S(2)}, u32[]{:S(2)}) collective-permute-start(bf16[1280,128]{1,0:T(8,128)(2,1)S(1)} %collective-permute-done.4.refs_2_), channel_id=1, source_target_pairs={{0,1},{1,0},{2,3},{3,2},{4,5},{5,4},{6,7},{7,6},{8,9},{9,8},{10,11... | collective-permute-start | bytes 983048 | tf_op jit(solution)/shard_map/ppermute | solution.py:30
  121.0 14.2 %collective-permute-start.38 = (f32[32,1280]{1,0:T(8,128)}, f32[32,1280]{1,0:T(8,128)S(1)}, u32[]{:S(2)}, u32[]{:S(2)}) collective-permute-start(f32[32,1280]{1,0:T(8,128)} %get-tuple-element.99), channel_id=1, source_target_pairs={{0,12},{4,0},{8,4},{12,8},{1,13},{5,1},{9,5},{13,9},{2,14},{6,2},{... | collective-permute-start | bytes 491528 | tf_op jit(solution)/shard_map/ppermute | solution.py:24
  121.0 14.2 %collective-permute-start.37 = (f32[32,1280]{1,0:T(8,128)}, f32[32,1280]{1,0:T(8,128)S(1)}, u32[]{:S(2)}, u32[]{:S(2)}) collective-permute-start(f32[32,1280]{1,0:T(8,128)} %get-tuple-element.98), channel_id=1, source_target_pairs={{0,8},{4,12},{8,0},{12,4},{1,9},{5,13},{9,1},{13,5},{2,10},{6,14},... | collective-permute-start | bytes 491528 | tf_op jit(solution)/shard_map/ppermute | solution.py:24
  122.6 12.6 %collective-permute-start.36 = (f32[32,1280]{1,0:T(8,128)}, f32[32,1280]{1,0:T(8,128)S(1)}, u32[]{:S(2)}, u32[]{:S(2)}) collective-permute-start(f32[32,1280]{1,0:T(8,128)} %get-tuple-element.97), channel_id=1, source_target_pairs={{0,4},{4,8},{8,12},{12,0},{1,5},{5,9},{9,13},{13,1},{2,6},{6,10},{... | collective-permute-start | bytes 491528 | tf_op jit(solution)/shard_map/ppermute | solution.py:24
  156.1 25.6 %collective-permute-start.44 = (bf16[1280,128]{1,0:T(8,128)(2,1)}, bf16[1280,128]{1,0:T(8,128)(2,1)S(1)}, u32[]{:S(2)}, u32[]{:S(2)}) collective-permute-start(bf16[1280,128]{1,0:T(8,128)(2,1)} %get-tuple-element.104), channel_id=1, source_target_pairs={{0,1},{1,0},{2,3},{3,2},{4,5},{5,4},{6,7},{7,6},{8,9},{9,8},{10,11... | collective-permute-start | bytes 983048 | tf_op jit(solution)/shard_map/ppermute | solution.py:30
  170.7 47.6 %collective-permute-start.13 = (bf16[1280,128]{1,0:T(8,128)(2,1)}, bf16[1280,128]{1,0:T(8,128)(2,1)S(1)}, u32[]{:S(2)}, u32[]{:S(2)}) collective-permute-start(bf16[1280,128]{1,0:T(8,128)(2,1)} %get-tuple-element.79), channel_id=1, source_target_pairs={{0,1},{1,0},{2,3},{3,2},{4,5},{5,4},{6,7},{7,6},{8,9},{9,8},{10,11... | collective-permute-start | bytes 983048 | tf_op jit(solution)/shard_map/ppermute | solution.py:30
  171.8 20.1 %collective-permute-start.14 = (bf16[1280,128]{1,0:T(8,128)(2,1)S(1)}, bf16[1280,128]{1,0:T(8,128)(2,1)S(1)}, u32[]{:S(2)}, u32[]{:S(2)}) collective-permute-start(bf16[1280,128]{1,0:T(8,128)(2,1)S(1)} %copy-done.57), channel_id=1, source_target_pairs={{0,1},{1,0},{2,3},{3,2},{4,5},{5,4},{6,7},{7,6},{8,9},{9,8},{10,11... | collective-permute-start | bytes 983048 | tf_op jit(solution)/shard_map/ppermute | solution.py:30
  180.6 17.4 %collective-permute-start.43 = (bf16[1280,128]{1,0:T(8,128)(2,1)}, bf16[1280,128]{1,0:T(8,128)(2,1)S(1)}, u32[]{:S(2)}, u32[]{:S(2)}) collective-permute-start(bf16[1280,128]{1,0:T(8,128)(2,1)} %get-tuple-element.102), channel_id=1, source_target_pairs={{0,1},{1,0},{2,3},{3,2},{4,5},{5,4},{6,7},{7,6},{8,9},{9,8},{10,11... | collective-permute-start | bytes 983048 | tf_op jit(solution)/shard_map/ppermute | solution.py:30
  182.9 31.9 %collective-permute-start.45 = (bf16[1280,128]{1,0:T(8,128)(2,1)S(1)}, bf16[1280,128]{1,0:T(8,128)(2,1)S(1)}, u32[]{:S(2)}, u32[]{:S(2)}) collective-permute-start(bf16[1280,128]{1,0:T(8,128)(2,1)S(1)} %add_convert_fusion.1), channel_id=1, source_target_pairs={{0,2},{1,3},{2,0},{3,1},{4,6},{5,7},{6,4},{7,5},{8,10},{9,11},{10,... | collective-permute-start | bytes 983048 | tf_op jit(solution)/shard_map/ppermute | solution.py:30
  192.0 36.8 %collective-permute-start.15 = (bf16[1280,128]{1,0:T(8,128)(2,1)S(1)}, bf16[1280,128]{1,0:T(8,128)(2,1)S(1)}, u32[]{:S(2)}, u32[]{:S(2)}) collective-permute-start(bf16[1280,128]{1,0:T(8,128)(2,1)S(1)} %add_convert_fusion.4), channel_id=1, source_target_pairs={{0,2},{1,3},{2,0},{3,1},{4,6},{5,7},{6,4},{7,5},{8,10},{9,11},{10,... | collective-permute-start | bytes 983048 | tf_op jit(solution)/shard_map/ppermute | solution.py:30
  218.4 17.6 %collective-permute-start.47 = (bf16[1280,128]{1,0:T(8,128)(2,1)}, bf16[1280,128]{1,0:T(8,128)(2,1)S(1)}, u32[]{:S(2)}, u32[]{:S(2)}) collective-permute-start(bf16[1280,128]{1,0:T(8,128)(2,1)} %join.10.refs_0_), channel_id=1, source_target_pairs={{0,2},{1,3},{2,0},{3,1},{4,6},{5,7},{6,4},{7,5},{8,10},{9,11},{10,... | collective-permute-start | bytes 983048 | tf_op jit(solution)/shard_map/ppermute | solution.py:30
  232.6 15.6 %collective-permute-start.46 = (bf16[1280,128]{1,0:T(8,128)(2,1)S(1)}, bf16[1280,128]{1,0:T(8,128)(2,1)S(1)}, u32[]{:S(2)}, u32[]{:S(2)}) collective-permute-start(bf16[1280,128]{1,0:T(8,128)(2,1)S(1)} %copy-done.7), channel_id=1, source_target_pairs={{0,1},{1,0},{2,3},{3,2},{4,5},{5,4},{6,7},{7,6},{8,9},{9,8},{10,11... | collective-permute-start | bytes 983048 | tf_op jit(solution)/shard_map/ppermute | solution.py:30
  235.9 19.3 %collective-permute-start.48 = (bf16[1280,128]{1,0:T(8,128)(2,1)S(1)}, bf16[1280,128]{1,0:T(8,128)(2,1)S(1)}, u32[]{:S(2)}, u32[]{:S(2)}) collective-permute-start(bf16[1280,128]{1,0:T(8,128)(2,1)S(1)} %collective-permute-done.47.refs_2_), channel_id=1, source_target_pairs={{0,1},{1,0},{2,3},{3,2},{4,5},{5,4},{6,7},{7,6},{8,9},{9,8},{10,11... | collective-permute-start | bytes 983048 | tf_op jit(solution)/shard_map/ppermute | solution.py:30
  235.9 30.7 %collective-permute-start.16 = (bf16[1280,128]{1,0:T(8,128)(2,1)}, bf16[1280,128]{1,0:T(8,128)(2,1)S(1)}, u32[]{:S(2)}, u32[]{:S(2)}) collective-permute-start(bf16[1280,128]{1,0:T(8,128)(2,1)} %join.7.refs_0_), channel_id=1, source_target_pairs={{0,1},{1,0},{2,3},{3,2},{4,5},{5,4},{6,7},{7,6},{8,9},{9,8},{10,11... | collective-permute-start | bytes 983048 | tf_op jit(solution)/shard_map/ppermute | solution.py:30
  241.2 28.0 %collective-permute-start.18 = (bf16[1280,128]{1,0:T(8,128)(2,1)S(1)}, bf16[1280,128]{1,0:T(8,128)(2,1)S(1)}, u32[]{:S(2)}, u32[]{:S(2)}) collective-permute-start(bf16[1280,128]{1,0:T(8,128)(2,1)S(1)} %collective-permute-done.17.refs_2_), channel_id=1, source_target_pairs={{0,1},{1,0},{2,3},{3,2},{4,5},{5,4},{6,7},{7,6},{8,9},{9,8},{10,11... | collective-permute-start | bytes 983048 | tf_op jit(solution)/shard_map/ppermute | solution.py:30
  264.8 15.6 %collective-permute-start.51 = (f32[32,1280]{1,0:T(8,128)}, f32[32,1280]{1,0:T(8,128)S(1)}, u32[]{:S(2)}, u32[]{:S(2)}) collective-permute-start(f32[32,1280]{1,0:T(8,128)} %get-tuple-element.112), channel_id=1, source_target_pairs={{0,12},{4,0},{8,4},{12,8},{1,13},{5,1},{9,5},{13,9},{2,14},{6,2},{... | collective-permute-start | bytes 491528 | tf_op jit(solution)/shard_map/ppermute | solution.py:24
  264.9 15.5 %collective-permute-start.50 = (f32[32,1280]{1,0:T(8,128)}, f32[32,1280]{1,0:T(8,128)S(1)}, u32[]{:S(2)}, u32[]{:S(2)}) collective-permute-start(f32[32,1280]{1,0:T(8,128)} %get-tuple-element.111), channel_id=1, source_target_pairs={{0,8},{4,12},{8,0},{12,4},{1,9},{5,13},{9,1},{13,5},{2,10},{6,14},... | collective-permute-start | bytes 491528 | tf_op jit(solution)/shard_map/ppermute | solution.py:24
  266.4 14.0 %collective-permute-start.49 = (f32[32,1280]{1,0:T(8,128)}, f32[32,1280]{1,0:T(8,128)S(1)}, u32[]{:S(2)}, u32[]{:S(2)}) collective-permute-start(f32[32,1280]{1,0:T(8,128)} %get-tuple-element.110), channel_id=1, source_target_pairs={{0,4},{4,8},{8,12},{12,0},{1,5},{5,9},{9,13},{13,1},{2,6},{6,10},{... | collective-permute-start | bytes 491528 | tf_op jit(solution)/shard_map/ppermute | solution.py:24
  280.5 12.2 %collective-permute-start.52 = (bf16[32,1280]{1,0:T(8,128)(2,1)S(1)}, bf16[32,1280]{1,0:T(8,128)(2,1)S(1)}, u32[]{:S(2)}, u32[]{:S(2)}) collective-permute-start(bf16[32,1280]{1,0:T(8,128)(2,1)S(1)} %add_convert_fusion.8), channel_id=1, source_target_pairs={{16,0},{20,4},{24,8},{28,12},{17,1},{21,5},{25,9},{29,13},{18,2},{... | collective-permute-start | bytes 245768 | tf_op jit(solution)/shard_map/ppermute | solution.py:80
  281.8 12.6 %collective-permute-start.53 = (bf16[32,1280]{1,0:T(8,128)(2,1)S(1)}, bf16[32,1280]{1,0:T(8,128)(2,1)S(1)}, u32[]{:S(2)}, u32[]{:S(2)}) collective-permute-start(bf16[32,1280]{1,0:T(8,128)(2,1)S(1)} %add_convert_fusion.8), channel_id=1, source_target_pairs={{16,4},{20,8},{24,12},{28,0},{17,5},{21,9},{25,13},{29,1},{18,6},{... | collective-permute-start | bytes 245768 | tf_op jit(solution)/shard_map/ppermute | solution.py:80
  302.2 25.6 %collective-permute-start.57 = (bf16[1280,128]{1,0:T(8,128)(2,1)}, bf16[1280,128]{1,0:T(8,128)(2,1)S(1)}, u32[]{:S(2)}, u32[]{:S(2)}) collective-permute-start(bf16[1280,128]{1,0:T(8,128)(2,1)} %get-tuple-element.117), channel_id=1, source_target_pairs={{0,1},{1,0},{2,3},{3,2},{4,5},{5,4},{6,7},{7,6},{8,9},{9,8},{10,11... | collective-permute-start | bytes 983048 | tf_op jit(solution)/shard_map/ppermute | solution.py:30
  317.1 48.1 %collective-permute-start.26 = (bf16[1280,128]{1,0:T(8,128)(2,1)}, bf16[1280,128]{1,0:T(8,128)(2,1)S(1)}, u32[]{:S(2)}, u32[]{:S(2)}) collective-permute-start(bf16[1280,128]{1,0:T(8,128)(2,1)} %get-tuple-element.88), channel_id=1, source_target_pairs={{0,1},{1,0},{2,3},{3,2},{4,5},{5,4},{6,7},{7,6},{8,9},{9,8},{10,11... | collective-permute-start | bytes 983048 | tf_op jit(solution)/shard_map/ppermute | solution.py:30
  317.8 21.5 %collective-permute-start.27 = (bf16[1280,128]{1,0:T(8,128)(2,1)S(1)}, bf16[1280,128]{1,0:T(8,128)(2,1)S(1)}, u32[]{:S(2)}, u32[]{:S(2)}) collective-permute-start(bf16[1280,128]{1,0:T(8,128)(2,1)S(1)} %copy-done.58), channel_id=1, source_target_pairs={{0,1},{1,0},{2,3},{3,2},{4,5},{5,4},{6,7},{7,6},{8,9},{9,8},{10,11... | collective-permute-start | bytes 983048 | tf_op jit(solution)/shard_map/ppermute | solution.py:30
  327.1 19.2 %collective-permute-start.56 = (bf16[1280,128]{1,0:T(8,128)(2,1)}, bf16[1280,128]{1,0:T(8,128)(2,1)S(1)}, u32[]{:S(2)}, u32[]{:S(2)}) collective-permute-start(bf16[1280,128]{1,0:T(8,128)(2,1)} %get-tuple-element.115), channel_id=1, source_target_pairs={{0,1},{1,0},{2,3},{3,2},{4,5},{5,4},{6,7},{7,6},{8,9},{9,8},{10,11... | collective-permute-start | bytes 983048 | tf_op jit(solution)/shard_map/ppermute | solution.py:30
  328.9 32.6 %collective-permute-start.58 = (bf16[1280,128]{1,0:T(8,128)(2,1)S(1)}, bf16[1280,128]{1,0:T(8,128)(2,1)S(1)}, u32[]{:S(2)}, u32[]{:S(2)}) collective-permute-start(bf16[1280,128]{1,0:T(8,128)(2,1)S(1)} %add_convert_fusion), channel_id=1, source_target_pairs={{0,2},{1,3},{2,0},{3,1},{4,6},{5,7},{6,4},{7,5},{8,10},{9,11},{10,... | collective-permute-start | bytes 983048 | tf_op jit(solution)/shard_map/ppermute | solution.py:30
  339.5 29.1 %collective-permute-start.28 = (bf16[1280,128]{1,0:T(8,128)(2,1)S(1)}, bf16[1280,128]{1,0:T(8,128)(2,1)S(1)}, u32[]{:S(2)}, u32[]{:S(2)}) collective-permute-start(bf16[1280,128]{1,0:T(8,128)(2,1)S(1)} %add_convert_fusion.3), channel_id=1, source_target_pairs={{0,2},{1,3},{2,0},{3,1},{4,6},{5,7},{6,4},{7,5},{8,10},{9,11},{10,... | collective-permute-start | bytes 983048 | tf_op jit(solution)/shard_map/ppermute | solution.py:30
  365.2 18.9 %collective-permute-start.60 = (bf16[1280,128]{1,0:T(8,128)(2,1)}, bf16[1280,128]{1,0:T(8,128)(2,1)}, u32[]{:S(2)}, u32[]{:S(2)}) collective-permute-start(bf16[1280,128]{1,0:T(8,128)(2,1)} %join.11.refs_0_), channel_id=1, source_target_pairs={{0,2},{1,3},{2,0},{3,1},{4,6},{5,7},{6,4},{7,5},{8,10},{9,11},{10,... | collective-permute-start | bytes 983048 | tf_op jit(solution)/shard_map/ppermute | solution.py:30
  372.3 16.2 %collective-permute-start.29 = (bf16[1280,128]{1,0:T(8,128)(2,1)}, bf16[1280,128]{1,0:T(8,128)(2,1)S(1)}, u32[]{:S(2)}, u32[]{:S(2)}) collective-permute-start(bf16[1280,128]{1,0:T(8,128)(2,1)} %join.8.refs_0_), channel_id=1, source_target_pairs={{0,2},{1,3},{2,0},{3,1},{4,6},{5,7},{6,4},{7,5},{8,10},{9,11},{10,... | collective-permute-start | bytes 983048 | tf_op jit(solution)/shard_map/ppermute | solution.py:30
  374.0 49.8 %collective-permute-start.59 = (bf16[1280,128]{1,0:T(8,128)(2,1)S(1)}, bf16[1280,128]{1,0:T(8,128)(2,1)S(1)}, u32[]{:S(2)}, u32[]{:S(2)}) collective-permute-start(bf16[1280,128]{1,0:T(8,128)(2,1)S(1)} %copy-done.5), channel_id=1, source_target_pairs={{0,1},{1,0},{2,3},{3,2},{4,5},{5,4},{6,7},{7,6},{8,9},{9,8},{10,11... | collective-permute-start | bytes 983048 | tf_op jit(solution)/shard_map/ppermute | solution.py:30
  374.0 29.9 %collective-permute-start.62 = (bf16[1280,128]{1,0:T(8,128)(2,1)S(1)}, bf16[1280,128]{1,0:T(8,128)(2,1)S(1)}, u32[]{:S(2)}, u32[]{:S(2)}) collective-permute-start(bf16[1280,128]{1,0:T(8,128)(2,1)S(1)} %copy-done), channel_id=1, source_target_pairs={{0,1},{1,0},{2,3},{3,2},{4,5},{5,4},{6,7},{7,6},{8,9},{9,8},{10,11... | collective-permute-start | bytes 983048 | tf_op jit(solution)/shard_map/ppermute | solution.py:30
  384.1 39.7 %collective-permute-start.61 = (bf16[1280,128]{1,0:T(8,128)(2,1)}, bf16[1280,128]{1,0:T(8,128)(2,1)S(1)}, u32[]{:S(2)}, u32[]{:S(2)}) collective-permute-start(bf16[1280,128]{1,0:T(8,128)(2,1)} %collective-permute-done.60.refs_2_), channel_id=1, source_target_pairs={{0,1},{1,0},{2,3},{3,2},{4,5},{5,4},{6,7},{7,6},{8,9},{9,8},{10,11... | collective-permute-start | bytes 983048 | tf_op jit(solution)/shard_map/ppermute | solution.py:30
  388.5 24.3 %collective-permute-start.63 = (bf16[1280,128]{1,0:T(8,128)(2,1)S(1)}, bf16[1280,128]{1,0:T(8,128)(2,1)S(1)}, u32[]{:S(2)}, u32[]{:S(2)}) collective-permute-start(bf16[1280,128]{1,0:T(8,128)(2,1)S(1)} %collective-permute-done.29.refs_1_.refs_2_), channel_id=1, source_target_pairs={{0,1},{1,0},{2,3},{3,2},{4,5},{5,4},{6,7},{7,6},{8,9},{9,8},{10,11... | collective-permute-start | bytes 983048 | tf_op jit(solution)/shard_map/ppermute | solution.py:30
  422.3 35.8 %collective-permute-start.69 = (f32[32,1280]{1,0:T(8,128)}, f32[32,1280]{1,0:T(8,128)S(1)}, u32[]{:S(2)}, u32[]{:S(2)}) collective-permute-start(f32[32,1280]{1,0:T(8,128)} %get-tuple-element.132), channel_id=1, source_target_pairs={{0,12},{4,0},{8,4},{12,8},{1,13},{5,1},{9,5},{13,9},{2,14},{6,2},{... | collective-permute-start | bytes 491528 | tf_op jit(solution)/shard_map/ppermute | solution.py:24
  422.3 35.8 %collective-permute-start.68 = (f32[32,1280]{1,0:T(8,128)}, f32[32,1280]{1,0:T(8,128)S(1)}, u32[]{:S(2)}, u32[]{:S(2)}) collective-permute-start(f32[32,1280]{1,0:T(8,128)} %get-tuple-element.131), channel_id=1, source_target_pairs={{0,8},{4,12},{8,0},{12,4},{1,9},{5,13},{9,1},{13,5},{2,10},{6,14},... | collective-permute-start | bytes 491528 | tf_op jit(solution)/shard_map/ppermute | solution.py:24
  423.6 34.5 %collective-permute-start.67 = (f32[32,1280]{1,0:T(8,128)}, f32[32,1280]{1,0:T(8,128)S(1)}, u32[]{:S(2)}, u32[]{:S(2)}) collective-permute-start(f32[32,1280]{1,0:T(8,128)} %get-tuple-element.130), channel_id=1, source_target_pairs={{0,4},{4,8},{8,12},{12,0},{1,5},{5,9},{9,13},{13,1},{2,6},{6,10},{... | collective-permute-start | bytes 491528 | tf_op jit(solution)/shard_map/ppermute | solution.py:24
  434.1 24.1 %collective-permute-start.66 = (f32[32,1280]{1,0:T(8,128)}, f32[32,1280]{1,0:T(8,128)S(1)}, u32[]{:S(2)}, u32[]{:S(2)}) collective-permute-start(f32[32,1280]{1,0:T(8,128)} %get-tuple-element.128), channel_id=1, source_target_pairs={{0,12},{4,0},{8,4},{12,8},{1,13},{5,1},{9,5},{13,9},{2,14},{6,2},{... | collective-permute-start | bytes 491528 | tf_op jit(solution)/shard_map/ppermute | solution.py:24
  435.7 22.6 %collective-permute-start.65 = (f32[32,1280]{1,0:T(8,128)}, f32[32,1280]{1,0:T(8,128)S(1)}, u32[]{:S(2)}, u32[]{:S(2)}) collective-permute-start(f32[32,1280]{1,0:T(8,128)} %get-tuple-element.127), channel_id=1, source_target_pairs={{0,8},{4,12},{8,0},{12,4},{1,9},{5,13},{9,1},{13,5},{2,10},{6,14},... | collective-permute-start | bytes 491528 | tf_op jit(solution)/shard_map/ppermute | solution.py:24
  (83 other events, 566.0 us)
